TPU v7x, 32 devices: a whole 2x2x4 slice. The times are simulated.
32 devices in a mesh: dp: 8 (over y, x, core), tensor: 4 (over z).
Axes of the slice: x: 2, y: 2, z: 4, core: 2. Of those that a mesh axis runs over, the one named last changes fastest.
Arguments:
- inputs: bfloat16 [32, 1024, 1024], P(None, 'dp', 'tensor'), may hold values from -6 to 6
- cotangent: bfloat16 [32, 1024, 1024], P(None, 'dp', 'tensor'), may hold values from -6 to 6
- lengths: int32 [32], replicated, may hold values from 513 to 1024, as said below
- dealing: int32 [32], replicated, may hold values from 0 to 31, each once
- buckets: int32 [2047], replicated, may hold values from 1 to 511, as said below
- rel_embed: bfloat16 [512, 1024], P('dp'), may hold values from -6 to 6
- query_weight: bfloat16 [1024, 1024], P('dp', 'tensor'), may hold values from -0.25 to 0.25
- key_weight: bfloat16 [1024, 1024], P('dp', 'tensor'), may hold values from -0.25 to 0.25
- value_weight: bfloat16 [1024, 1024], P('dp', 'tensor'), may hold values from -0.1875 to 0.1875
- proj_shifts: bfloat16 [3, 1024], P(None, 'tensor'), may hold values from -3 to 3
- merge_weight: bfloat16 [1024, 1024], P('dp', 'tensor'), may hold values from -1.5 to 1.5
- inner_weight: bfloat16 [1024, 4096], P('dp', 'tensor'), may hold values from -0.1875 to 0.1875
- hidden_shift: bfloat16 [4096], P('tensor'), may hold values from -3 to 3
- outer_weight: bfloat16 [1024, 4096], P('dp', 'tensor'), may hold values from -0.09375 to 0.09375
- layer_vectors: bfloat16 [6, 1024], replicated, may hold values from -2 to 2, as said below
Outputs:
- output: bfloat16 [32, 1024, 1024], P(None, 'dp', 'tensor')
- input_grad: bfloat16 [32, 1024, 1024], P(None, 'dp', 'tensor')
- rel_grad: float32 [512, 1024], replicated
- query_grad: float32 [1024, 1024], P('dp', 'tensor')
- key_grad: float32 [1024, 1024], P('dp', 'tensor')
- value_grad: float32 [1024, 1024], P('dp', 'tensor')
- shifts_grad: float32 [3, 1024], replicated
- merge_grad: float32 [1024, 1024], P('dp', 'tensor')
- inner_grad: float32 [1024, 4096], P('dp', 'tensor')
- hidden_grad: float32 [4096], replicated
- outer_grad: float32 [1024, 4096], P('dp', 'tensor')
- vectors_grad: float32 [6, 1024], replicated
Inputs may be any that keep to these rules, and one draw needn't show every extreme that they name: lengths[k] is the length of the sequence in slot k; in each aligned block of 4 slots one has length 1024. Slot k holds the given sequence dealing[k]; each sequence once. buckets[r + 1023] is the bucket of distance r; it equals 256 at r = 0, never falls as r rises, rises by one per step while |r| <= 128, beyond that by one at each even |r| and by zero or one at each odd |r| until it is capped, and the buckets of r and -r sum to 512. `layer_vectors`: rows 1 and 4 (from 0) are gains near one, the others biases.
All inputs are finite; a program needn't handle non-finite values.
Results may differ from a plain program's by a relative error of at most 0.02.
Values may be sent and summed in bfloat16 or wider, within the bound.
A program may use at most 512 MiB of HBM per device.

v0:
```python
import math

import jax
import jax.numpy as jnp
from jax import lax
from jax.sharding import PartitionSpec as P

D = 1024
HEAD = 64
FF = 4096
MICRO = 2


EPSILON = 1e-07
NEGATIVE = -1e30


def layer_norm(values, gain, shift):
    center = values - jnp.mean(values, axis=-1, keepdims=True)
    spread = jnp.mean(center * center, axis=-1, keepdims=True)
    return center * lax.rsqrt(spread + EPSILON) * gain + shift


def gelu_exact(values):
    return jax.nn.gelu(values, approximate=False)


def spread_rows(values):
    return lax.all_gather(values, "tensor", axis=1, tiled=True)


def spread_grads(values):
    return lax.all_gather(values, "tensor", axis=1, tiled=True)


def reduce_rows(values):
    return lax.psum_scatter(
        values.astype(jnp.bfloat16), "tensor", scatter_dimension=1, tiled=True
    ).astype(jnp.float32)


def reduce_grads(values):
    return lax.psum_scatter(
        values.astype(jnp.bfloat16), "tensor", scatter_dimension=1, tiled=True
    ).astype(jnp.float32)


def skew_heads(table):
    heads_count = table.shape[0]
    count = table.shape[1]
    width = table.shape[2]
    padded = jnp.pad(table, ((0, 0), (0, 0), (0, 1)))
    flat = padded.reshape(heads_count, count * (width + 1))
    cut = lax.slice_in_dim(flat, count - 1, count - 1 + count * width, axis=1)
    return cut.reshape(heads_count, count, width)[:, :, :count]


def position_term(query_matrix, keys, query_far, key_far):
    into_position = jnp.einsum(
        "ihd,rhd->hir", query_matrix, key_far, preferred_element_type=jnp.float32
    )
    from_pos = jnp.einsum("jhd,rhd->hjr", keys, query_far, preferred_element_type=jnp.float32)
    return skew_heads(into_position) + jnp.swapaxes(skew_heads(from_pos), 1, 2)


def masked_score(query_matrix, keys, positional, length, scale):
    content = jnp.einsum("ihd,jhd->hij", query_matrix, keys, preferred_element_type=jnp.float32)
    total = (content + positional) * scale
    column = jnp.arange(keys.shape[0], dtype=jnp.int32)
    return jnp.where((column < length)[None, None, :], total, NEGATIVE)


def attend_forward(query_matrix, keys, values, lengths_here, query_far, key_far, scale):

    def single(item):
        sequence_query, seq_k, seq_v, length = item
        positional = position_term(sequence_query, seq_k, query_far, key_far)
        score = masked_score(sequence_query, seq_k, positional, length, scale)
        top = jnp.max(score, axis=-1, keepdims=True)
        weights = jnp.exp(score - top)
        total = jnp.sum(weights, axis=-1, keepdims=True)
        probs = weights / total
        context = jnp.einsum(
            "hij,jhd->ihd", probs.astype(jnp.bfloat16), seq_v, preferred_element_type=jnp.float32
        )
        return (context.astype(jnp.bfloat16), (top + jnp.log(total))[..., 0], positional)

    return lax.map(single, (query_matrix, keys, values, lengths_here))


def attend_backward(
    query_matrix,
    keys,
    values,
    lengths_here,
    log_totals,
    positionals,
    grad_context,
    query_far,
    key_far,
    scale,
):
    table_zero = jnp.zeros(
        (key_far.shape[1], query_matrix.shape[1], key_far.shape[0]), jnp.bfloat16
    )
    _, skew_back = jax.vjp(skew_heads, table_zero)

    def single(carry, item):
        key_far_grad, query_far_grad = carry
        sequence_query, seq_k, seq_v, length, log_total, positional, dcontext = item
        score = masked_score(sequence_query, seq_k, positional, length, scale)
        probs = jnp.exp(score - log_total[..., None])
        dprobs = jnp.einsum("ihd,jhd->hij", dcontext, seq_v, preferred_element_type=jnp.float32)
        inner = jnp.sum(probs * dprobs, axis=-1, keepdims=True)
        dscore = probs * (dprobs - inner) * scale
        dscore_low = dscore.astype(jnp.bfloat16)
        (into_narrow,) = skew_back(dscore_low)
        (from_low,) = skew_back(jnp.swapaxes(dscore_low, 1, 2))
        grad_q = jnp.einsum(
            "hij,jhd->ihd", dscore_low, seq_k, preferred_element_type=jnp.float32
        ) + jnp.einsum("hir,rhd->ihd", into_narrow, key_far, preferred_element_type=jnp.float32)
        grad_k = jnp.einsum(
            "hij,ihd->jhd", dscore_low, sequence_query, preferred_element_type=jnp.float32
        ) + jnp.einsum("hjr,rhd->jhd", from_low, query_far, preferred_element_type=jnp.float32)
        grad_v = jnp.einsum(
            "hij,ihd->jhd", probs.astype(jnp.bfloat16), dcontext, preferred_element_type=jnp.float32
        )
        key_far_grad = key_far_grad + jnp.einsum(
            "hir,ihd->rhd", into_narrow, sequence_query, preferred_element_type=jnp.float32
        )
        query_far_grad = query_far_grad + jnp.einsum(
            "hjr,jhd->rhd", from_low, seq_k, preferred_element_type=jnp.float32
        )
        return ((key_far_grad, query_far_grad), (grad_q, grad_k, grad_v))

    zero = jnp.zeros(key_far.shape, jnp.float32)
    return lax.scan(
        single,
        (zero, zero),
        (query_matrix, keys, values, lengths_here, log_totals, positionals, grad_context),
    )


def shards(
    inputs,
    cotangent,
    lengths,
    dealing,
    buckets,
    rel_embed,
    query_weight,
    key_weight,
    value_weight,
    proj_shifts,
    merge_weight,
    inner_weight,
    hidden_shift,
    outer_weight,
    layer_vectors,
):
    tensor_count = lax.axis_size("tensor")
    tensor_place = lax.axis_index("tensor")
    group_place = lax.axis_index("dp")
    slots = jnp.arange(dealing.shape[0], dtype=jnp.int32)
    inverse = jnp.zeros_like(dealing).at[dealing].set(slots)
    rows_in, rows_cot = (
        lax.all_to_all(
            lax.all_to_all(inputs[dealing], "dp", split_axis=0, concat_axis=1, tiled=True),
            "tensor",
            split_axis=1,
            concat_axis=2,
            tiled=True,
        ),
        lax.all_to_all(
            lax.all_to_all(cotangent[dealing], "dp", split_axis=0, concat_axis=1, tiled=True),
            "tensor",
            split_axis=1,
            concat_axis=2,
            tiled=True,
        ),
    )
    local_seqs = rows_in.shape[0]
    per_micro = local_seqs // MICRO
    seq_length = rows_in.shape[1] * tensor_count
    my_lengths = lax.dynamic_slice_in_dim(lengths, group_place * local_seqs, local_seqs)
    reversed_buckets = buckets[::-1]
    scale = 1.0 / math.sqrt(3.0 * HEAD)
    vectors = layer_vectors.astype(jnp.float32)
    shifts = proj_shifts.astype(jnp.float32)
    hidden_bias = hidden_shift.astype(jnp.float32)
    columns = query_weight.shape[1]
    heads_here = columns // HEAD
    hidden_cols = inner_weight.shape[1]
    spans = rel_embed.shape[0] * lax.axis_size("dp")
    distances = reversed_buckets.shape[0]
    bucket_table = (
        reversed_buckets[None, :] == jnp.arange(spans, dtype=jnp.int32)[:, None]
    ).astype(jnp.float32)
    highest = lax.Precision.HIGHEST
    grad_totals = [
        jnp.zeros(query_weight.shape, jnp.float32),
        jnp.zeros(key_weight.shape, jnp.float32),
        jnp.zeros(value_weight.shape, jnp.float32),
        jnp.zeros(merge_weight.shape, jnp.float32),
        jnp.zeros(inner_weight.shape, jnp.float32),
        jnp.zeros(outer_weight.shape, jnp.float32),
    ]
    rel_total = jnp.zeros((spans, D), jnp.float32)
    shift_total = jnp.zeros((3, columns), jnp.float32)
    hidden_total = jnp.zeros((hidden_cols,), jnp.float32)
    vector_total = jnp.zeros((6, D), jnp.float32)
    outputs = []
    input_grads = []

    def split_heads(tensor):
        return tensor.reshape(tensor.shape[0], tensor.shape[1], heads_here, HEAD)

    for micro in range(MICRO):
        gathered = (
            lax.all_gather(query_weight, "dp", axis=0, tiled=True),
            lax.all_gather(key_weight, "dp", axis=0, tiled=True),
            lax.all_gather(value_weight, "dp", axis=0, tiled=True),
            lax.all_gather(merge_weight, "dp", axis=0, tiled=True),
            lax.all_gather(inner_weight, "dp", axis=0, tiled=True),
            lax.all_gather(outer_weight, "dp", axis=0, tiled=True),
            lax.all_gather(rel_embed, "dp", axis=0, tiled=True),
        )
        (
            complete_query_rows,
            complete_key_rows,
            complete_value_rows,
            full_merge,
            complete_inner_matrix,
            full_outer,
            full_rel,
        ) = gathered
        start = micro * per_micro
        block_in = rows_in[start : start + per_micro]
        block_cot = rows_cot[start : start + per_micro]
        block_len = my_lengths[start : start + per_micro]
        complete_input = spread_rows(block_in)
        query_matrix = (
            jnp.einsum(
                "yqk,km->yqm",
                complete_input,
                complete_query_rows,
                preferred_element_type=jnp.float32,
            )
            + shifts[0]
        ).astype(jnp.bfloat16)
        keys = (
            jnp.einsum(
                "yqk,km->yqm", complete_input, complete_key_rows, preferred_element_type=jnp.float32
            )
            + shifts[1]
        ).astype(jnp.bfloat16)
        values = (
            jnp.einsum(
                "yqk,km->yqm",
                complete_input,
                complete_value_rows,
                preferred_element_type=jnp.float32,
            )
            + shifts[2]
        ).astype(jnp.bfloat16)
        query_pos = (
            (jnp.dot(full_rel, complete_query_rows, preferred_element_type=jnp.float32) + shifts[0])
            .astype(jnp.bfloat16)
            .reshape(spans, heads_here, HEAD)
        )
        key_position_rows = (
            (jnp.dot(full_rel, complete_key_rows, preferred_element_type=jnp.float32) + shifts[1])
            .astype(jnp.bfloat16)
            .reshape(spans, heads_here, HEAD)
        )
        query_far = query_pos[reversed_buckets]
        key_far = key_position_rows[reversed_buckets]
        context, log_totals, positionals = attend_forward(
            split_heads(query_matrix),
            split_heads(keys),
            split_heads(values),
            block_len,
            query_far,
            key_far,
            scale,
        )
        context = context.reshape(per_micro, seq_length, columns)
        attn = reduce_rows(
            jnp.einsum("slc,oc->slo", context, full_merge, preferred_element_type=jnp.float32)
        )
        first_sum = attn + vectors[0] + block_in.astype(jnp.float32)
        first_out, first_back = jax.vjp(layer_norm, first_sum, vectors[1], vectors[2])
        complete_hidden = spread_rows(first_out.astype(jnp.bfloat16))
        pre_act = (
            jnp.einsum(
                "nta,ah->nth",
                complete_hidden,
                complete_inner_matrix,
                preferred_element_type=jnp.float32,
            )
            + hidden_bias
        )
        act_value, act_back = jax.vjp(gelu_exact, pre_act)
        act_low = act_value.astype(jnp.bfloat16)
        ffn = reduce_rows(
            jnp.einsum("slf,of->slo", act_low, full_outer, preferred_element_type=jnp.float32)
        )
        second_sum = ffn + vectors[3] + first_out
        second_out, second_back = jax.vjp(layer_norm, second_sum, vectors[4], vectors[5])
        outputs.append(second_out.astype(jnp.bfloat16))
        dsecond, dgain_two, dshift_two = second_back(block_cot.astype(jnp.float32))
        whole_dffn = spread_grads(dsecond.astype(jnp.bfloat16))
        outer_part = jnp.einsum(
            "slo,slf->of", whole_dffn, act_low, preferred_element_type=jnp.float32
        )
        dact = jnp.einsum("slo,of->slf", whole_dffn, full_outer, preferred_element_type=jnp.float32)
        (dpre,) = act_back(dact)
        narrow_preact_grad = dpre.astype(jnp.bfloat16)
        inner_part = jnp.einsum(
            "ynz,ynq->zq", complete_hidden, narrow_preact_grad, preferred_element_type=jnp.float32
        )
        dmid = dsecond + reduce_grads(
            jnp.einsum(
                "qhx,rx->qhr",
                narrow_preact_grad,
                complete_inner_matrix,
                preferred_element_type=jnp.float32,
            )
        )
        dfirst, dgain_one, dshift_one = first_back(dmid)
        dattn_low = dfirst.astype(jnp.bfloat16)
        whole_dattn = spread_grads(dattn_low)
        dcontext = jnp.einsum(
            "slo,oc->slc", whole_dattn, full_merge, preferred_element_type=jnp.float32
        ).astype(jnp.bfloat16)
        merge_part = jnp.einsum(
            "slo,slc->oc", whole_dattn, context, preferred_element_type=jnp.float32
        )
        (dkey_far, dquery_far), (grad_q, grad_k, grad_v) = attend_backward(
            split_heads(query_matrix),
            split_heads(keys),
            split_heads(values),
            block_len,
            log_totals,
            positionals,
            split_heads(dcontext),
            query_far,
            key_far,
            scale,
        )
        grad_q = grad_q.reshape(per_micro, seq_length, columns)
        grad_k = grad_k.reshape(per_micro, seq_length, columns)
        grad_v = grad_v.reshape(per_micro, seq_length, columns)
        dkey_pos = jnp.dot(bucket_table, dkey_far.reshape(distances, columns), precision=highest)
        dquery_pos = jnp.dot(
            bucket_table, dquery_far.reshape(distances, columns), precision=highest
        )
        shift_total = shift_total + jnp.stack(
            [
                jnp.sum(grad_q, axis=(0, 1)) + jnp.sum(dquery_pos, axis=0),
                jnp.sum(grad_k, axis=(0, 1)) + jnp.sum(dkey_pos, axis=0),
                jnp.sum(grad_v, axis=(0, 1)),
            ]
        )
        hidden_total = hidden_total + jnp.sum(dpre, axis=(0, 1))
        vector_total = vector_total + jnp.stack(
            [
                jnp.sum(dfirst, axis=(0, 1)),
                dgain_one,
                dshift_one,
                jnp.sum(dsecond, axis=(0, 1)),
                dgain_two,
                dshift_two,
            ]
        )
        narrow_query_rows = grad_q.astype(jnp.bfloat16)
        narrow_key_rows = grad_k.astype(jnp.bfloat16)
        narrow_value_rows = grad_v.astype(jnp.bfloat16)
        rel_float = full_rel.astype(jnp.float32)
        query_part = jnp.einsum(
            "tue,tuj->ej", complete_input, narrow_query_rows, preferred_element_type=jnp.float32
        ) + jnp.dot(rel_float.T, dquery_pos, precision=highest)
        key_part = jnp.einsum(
            "tue,tuj->ej", complete_input, narrow_key_rows, preferred_element_type=jnp.float32
        ) + jnp.dot(rel_float.T, dkey_pos, precision=highest)
        value_portion = jnp.einsum(
            "tue,tuj->ej", complete_input, narrow_value_rows, preferred_element_type=jnp.float32
        )
        rel_total = (
            rel_total
            + jnp.dot(dquery_pos, complete_query_rows.astype(jnp.float32).T, precision=highest)
            + jnp.dot(dkey_pos, complete_key_rows.astype(jnp.float32).T, precision=highest)
        )
        dinput_part = jnp.einsum(
            "eiy,xy->eix",
            narrow_query_rows,
            complete_query_rows,
            preferred_element_type=jnp.float32,
        )
        dinput_part = dinput_part + jnp.einsum(
            "eiy,xy->eix", narrow_key_rows, complete_key_rows, preferred_element_type=jnp.float32
        )
        dinput_part = dinput_part + jnp.einsum(
            "eiy,xy->eix",
            narrow_value_rows,
            complete_value_rows,
            preferred_element_type=jnp.float32,
        )
        dinput = dfirst + reduce_grads(dinput_part)
        input_grads.append(dinput.astype(jnp.bfloat16))
        reduced = (
            lax.psum_scatter(
                query_part.astype(jnp.bfloat16), "dp", scatter_dimension=0, tiled=True
            ).astype(jnp.float32),
            lax.psum_scatter(
                key_part.astype(jnp.bfloat16), "dp", scatter_dimension=0, tiled=True
            ).astype(jnp.float32),
            lax.psum_scatter(
                value_portion.astype(jnp.bfloat16), "dp", scatter_dimension=0, tiled=True
            ).astype(jnp.float32),
            lax.psum_scatter(
                merge_part.astype(jnp.bfloat16), "dp", scatter_dimension=0, tiled=True
            ).astype(jnp.float32),
            lax.psum_scatter(
                inner_part.astype(jnp.bfloat16), "dp", scatter_dimension=0, tiled=True
            ).astype(jnp.float32),
            lax.psum_scatter(
                outer_part.astype(jnp.bfloat16), "dp", scatter_dimension=0, tiled=True
            ).astype(jnp.float32),
        )
        grad_totals = [total + piece for total, piece in zip(grad_totals, reduced)]
    shift_pad = lax.dynamic_update_slice_in_dim(
        jnp.zeros((3, D), jnp.float32), shift_total, tensor_place * columns, 1
    )
    hidden_pad = lax.dynamic_update_slice_in_dim(
        jnp.zeros((FF,), jnp.float32), hidden_total, tensor_place * hidden_cols, 0
    )
    rel_sum, shift_sum, hidden_sum, vector_sum = lax.psum(
        (rel_total, shift_pad, hidden_pad, vector_total), ("dp", "tensor")
    )
    back_out, back_grad = (
        lax.all_to_all(
            lax.all_to_all(
                jnp.concatenate(outputs, axis=0), "tensor", split_axis=2, concat_axis=1, tiled=True
            ),
            "dp",
            split_axis=1,
            concat_axis=0,
            tiled=True,
        ),
        lax.all_to_all(
            lax.all_to_all(
                jnp.concatenate(input_grads, axis=0),
                "tensor",
                split_axis=2,
                concat_axis=1,
                tiled=True,
            ),
            "dp",
            split_axis=1,
            concat_axis=0,
            tiled=True,
        ),
    )
    return (
        back_out[inverse],
        back_grad[inverse],
        rel_sum,
        grad_totals[0],
        grad_totals[1],
        grad_totals[2],
        shift_sum,
        grad_totals[3],
        grad_totals[4],
        hidden_sum,
        grad_totals[5],
        vector_sum,
    )


def solution(mesh):
    in_specs = (
        P(None, "dp", "tensor"),
        P(None, "dp", "tensor"),
        P(),
        P(),
        P(),
        P("dp", None),
        P("dp", "tensor"),
        P("dp", "tensor"),
        P("dp", "tensor"),
        P(None, "tensor"),
        P("dp", "tensor"),
        P("dp", "tensor"),
        P("tensor"),
        P("dp", "tensor"),
        P(),
    )
    out_specs = (
        P(None, "dp", "tensor"),
        P(None, "dp", "tensor"),
        P(),
        P("dp", "tensor"),
        P("dp", "tensor"),
        P("dp", "tensor"),
        P(),
        P("dp", "tensor"),
        P("dp", "tensor"),
        P(),
        P("dp", "tensor"),
        P(),
    )
    return jax.shard_map(shards, mesh=mesh, in_specs=in_specs, out_specs=out_specs, check_vma=False)
```

profile of v0, /device:TPU:0, one launch (start us, length us, event | category | flops | bytes accessed | tf_op | source)
XLA Modules:
  0.0 5373.8 jit_solution(2627263343682885572)
XLA Ops:
  10.8 31.8 all_to_all.138
  51.3 46.8 all-to-all-done.1
  203.4 1138.4 %while.70 = (s32[]{:T(128)}, bf16[2,1024,4,64]{1,3,2,0:T(8,128)(2,1)}, f32[2,4,1024]{2,1,0:T(4,128)}, f32[2,4,1024,1024]{2,3,1,0:T(8,128)}, bf16[2,1024,4,64]{1,...) while((s32[]{:T(128)}, ...), condition=%wide.region_3.4_spmd, body=%wide.region_0.3_spmd.sunk | while | flops 3266573312 | bytes 1003621952 | solution.py:88
  241.8 37.9 copy.486
  279.7 23.8 slice.210
  303.5 94.3 %reshape.612 = f32[8384512]{0:T(1024)} reshape(f32[4,2096128]{1,0:T(4,128)} %slice.210) | data formatting | bytes 67076096 | tf_op jit(solution)/shard_map/while
  397.8 49.9 reshape.613
  513.4 37.9 copy.488
  574.8 94.6 %reshape.614 = f32[8384512]{0:T(1024)} reshape(f32[4,2096128]{1,0:T(4,128)} %slice.212) | data formatting | bytes 67076096 | tf_op jit(solution)/shard_map/while
  669.4 49.8 reshape.615
  808.7 37.9 copy.486
  846.6 23.7 slice.210
  870.3 94.3 %reshape.612 = f32[8384512]{0:T(1024)} reshape(f32[4,2096128]{1,0:T(4,128)} %slice.210) | data formatting | bytes 67076096 | tf_op jit(solution)/shard_map/while
  964.7 49.9 reshape.613
  1080.2 37.9 copy.488
  1141.6 94.6 %reshape.614 = f32[8384512]{0:T(1024)} reshape(f32[4,2096128]{1,0:T(4,128)} %slice.212) | data formatting | bytes 67076096 | tf_op jit(solution)/shard_map/while
  1236.2 49.8 reshape.615
  1367.9 1140.6 %while.71 = (s32[]{:T(128)}, bf16[2,1024,4,64]{1,3,2,0:T(8,128)(2,1)}, f32[2,4,1024]{2,1,0:T(4,128)}, f32[2,4,1024,1024]{2,3,1,0:T(8,128)}, bf16[2,1024,4,64]{1,...) while((s32[]{:T(128)}, ...), condition=%wide.region_13.14_spmd, body=%wide.region_10.13_spmd.sunk | while | flops 3266573312 | bytes 1003621952 | solution.py:88
  1406.4 37.9 copy.489
  1467.8 94.4 %reshape.616 = f32[8384512]{0:T(1024)} reshape(f32[4,2096128]{1,0:T(4,128)} %slice.214) | data formatting | bytes 67076096 | tf_op jit(solution)/shard_map/while
  1562.2 49.7 reshape.617
  1677.6 37.9 copy.491
  1715.5 23.5 slice.216
  1739.0 94.3 %reshape.618 = f32[8384512]{0:T(1024)} reshape(f32[4,2096128]{1,0:T(4,128)} %slice.216) | data formatting | bytes 67076096 | tf_op jit(solution)/shard_map/while
  1833.3 49.8 reshape.619
  1973.0 37.9 copy.489
  2034.4 94.4 %reshape.616 = f32[8384512]{0:T(1024)} reshape(f32[4,2096128]{1,0:T(4,128)} %slice.214) | data formatting | bytes 67076096 | tf_op jit(solution)/shard_map/while
  2128.8 49.7 reshape.617
  2244.1 37.9 copy.491
  2282.1 23.5 slice.216
  2305.6 94.3 %reshape.618 = f32[8384512]{0:T(1024)} reshape(f32[4,2096128]{1,0:T(4,128)} %slice.216) | data formatting | bytes 67076096 | tf_op jit(solution)/shard_map/while
  2399.9 49.8 reshape.619
  2516.4 72.7 %reduce-scatter.25.cloned.1.call-done = bf16[2,256,1024]{2,1,0:T(8,128)(2,1)} async-done(((bf16[2,1024,1024]{2,1,0:T(8,128)(2,1)}), bf16[2,256,1024]{2,1,0:T(8,128)(2,1)}) %reduce-scatter.25.cloned.1.call-update) | async-done | bytes 1048592 | tf_op jit(solution)/shard_map/reduce_scatter | solution.py:37
  2619.3 82.9 %all-gather.24.cloned.1.call-done = bf16[2,1024,1024]{2,1,0:T(8,128)(2,1)} async-done(((bf16[2,256,1024]{2,1,0:T(8,128)(2,1)}), bf16[2,1024,1024]{2,1,0:T(8,128)(2,1)}) %all-gather.24.cloned.1.call-update) | async-done | bytes 4194320 | tf_op jit(solution)/shard_map/all_gather | solution.py:29
  2713.2 70.5 %all-gather.16.cloned.1.call-done = bf16[2,1024,1024]{2,1,0:T(8,128)(2,1)} async-done(((bf16[2,256,1024]{2,1,0:T(8,128)(2,1)}), bf16[2,1024,1024]{2,1,0:T(8,128)(2,1)}) %all-gather.16.cloned.1.call-update) | async-done | bytes 4194320 | tf_op jit(solution)/shard_map/all_gather | solution.py:29
  2802.6 42.8 multiply_convert_fusion.3
  2868.2 30.3 all_to_all.139
  2900.2 74.7 %all_to_all.140 = bf16[4,1024,256]{2,0,1:T(4,128)(2,1)S(1)} all-to-all(bf16[4,1024,256]{2,0,1:T(4,128)(2,1)S(1)} %copy.340), channel_id=1, replica_groups=mesh['dp'=8,'tensor'=4] {'tensor'}, dimensions={1} | all-to-all | bytes 4194304 | tf_op jit(solution)/shard_map/all_to_all | solution.py:174
  2978.9 65.0 %reduce-scatter.27.cloned.1.call-done = bf16[2,256,1024]{2,1,0:T(8,128)(2,1)} async-done(((bf16[2,1024,1024]{2,1,0:T(8,128)(2,1)}), bf16[2,256,1024]{2,1,0:T(8,128)(2,1)}) %reduce-scatter.27.cloned.1.call-update) | async-done | bytes 1048592 | tf_op jit(solution)/shard_map/reduce_scatter | solution.py:37
  3060.2 78.5 %all-gather.30.cloned.1.call-done = bf16[2,1024,1024]{2,1,0:T(8,128)(2,1)} async-done(((bf16[2,256,1024]{2,1,0:T(8,128)(2,1)}), bf16[2,1024,1024]{2,1,0:T(8,128)(2,1)}) %all-gather.30.cloned.1.call-update) | async-done | bytes 4194320 | tf_op jit(solution)/shard_map/all_gather | solution.py:33
  3159.9 60.3 %all-gather.26.cloned.1.call-done = bf16[2,1024,1024]{2,1,0:T(8,128)(2,1)} async-done(((bf16[2,256,1024]{2,1,0:T(8,128)(2,1)}), bf16[2,1024,1024]{2,1,0:T(8,128)(2,1)}) %all-gather.26.cloned.1.call-update) | async-done | bytes 4194320 | tf_op jit(solution)/shard_map/all_gather | solution.py:33
  3241.4 56.2 %reduce-scatter.33.cloned.1.call-done = bf16[2,256,1024]{2,1,0:T(8,128)(2,1)} async-done(((bf16[2,1024,1024]{2,1,0:T(8,128)(2,1)}), bf16[2,256,1024]{2,1,0:T(8,128)(2,1)}) %reduce-scatter.33.cloned.1.call-update) | async-done | bytes 1048592 | tf_op jit(solution)/shard_map/reduce_scatter | solution.py:43
  3297.6 79.6 %reduce-scatter.29.cloned.1.call-done = bf16[2,256,1024]{2,1,0:T(8,128)(2,1)} async-done(((bf16[2,1024,1024]{2,1,0:T(8,128)(2,1)}), bf16[2,256,1024]{2,1,0:T(8,128)(2,1)}) %reduce-scatter.29.cloned.1.call-update) | async-done | bytes 1048592 | tf_op jit(solution)/shard_map/reduce_scatter | solution.py:43
  3410.6 60.1 %all-gather.32.cloned.1.call-done = bf16[2,1024,1024]{2,1,0:T(8,128)(2,1)} async-done(((bf16[2,256,1024]{2,1,0:T(8,128)(2,1)}), bf16[2,1024,1024]{2,1,0:T(8,128)(2,1)}) %all-gather.32.cloned.1.call-update) | async-done | bytes 4194320 | tf_op jit(solution)/shard_map/all_gather | solution.py:33
  3479.0 560.6 %while.73 = (s32[]{:T(128)}, f32[2047,4,64]{0,2,1:T(8,128)}, f32[2047,4,64]{0,2,1:T(8,128)}, f32[2,1024,4,64]{1,3,2,0:T(8,128)}, f32[2,1024,4,64]{1,3,2,0:T(8,12...) while((s32[]{:T(128)}, f32[2047,4,64]{0,2,1:T(8,128)}, ...), condition=%wide.region_37.38_spmd.clone, body=%wide.region_35.37_spmd.clone.sunk | while | flops 7558665216 | bytes 602361728 | solution.py:137
  3531.9 28.4 reshape.624
  3635.1 28.0 reshape.626
  3811.1 28.1 reshape.624
  3912.9 28.0 reshape.626
  4048.0 563.6 %while.72 = (s32[]{:T(128)}, f32[2047,4,64]{0,2,1:T(8,128)}, f32[2047,4,64]{0,2,1:T(8,128)}, f32[2,1024,4,64]{1,3,2,0:T(8,128)}, f32[2,1024,4,64]{1,3,2,0:T(8,12...) while((s32[]{:T(128)}, f32[2047,4,64]{0,2,1:T(8,128)}, ...), condition=%wide.region_28.29_spmd.clone, body=%wide.region_26.28_spmd.clone.sunk | while | flops 7558665216 | bytes 602361728 | solution.py:137
  4100.5 28.5 reshape.620
  4202.5 28.0 reshape.622
  4378.6 28.1 reshape.620
  4480.3 28.0 reshape.622
  4663.7 82.7 %all-to-all-done.2 = bf16[4,256,1024]{1,0,2:T(4,128)(2,1)S(1)} async-done(((bf16[4,256,1024]{1,0,2:T(4,128)(2,1)}), bf16[4,256,1024]{1,0,2:T(4,128)(2,1)S(1)}, u32[]{:S(2)}, u32[]{:S(2)}) %all-to-all-start.2) | async-done | bytes 2097184 | tf_op jit(solution)/shard_map/all_to_all | solution.py:443
  4926.3 42.3 all-reduce.12
  4968.7 32.2 reduce-scatter.51.cloned.1.call-done
  5002.4 35.5 reduce-scatter.45.cloned.1.call-done
  5037.9 37.4 reduce-scatter.47.cloned.1.call-done
  5076.8 35.7 reduce-scatter.41.cloned.1.call-done
  5112.5 37.6 reduce-scatter.43.cloned.1.call-done
  5151.6 35.5 reduce-scatter.37.cloned.1.call-done
  5187.1 37.6 reduce-scatter.39.cloned.1.call-done
  5233.4 130.5 %all-reduce.15.cloned.1.call-done = f32[512,1024]{1,0:T(8,128)} async-done(((f32[512,1024]{1,0:T(8,128)}), f32[512,1024]{1,0:T(8,128)}) %all-reduce.15.cloned.1.call-update) | async-done | bytes 2097168 | tf_op jit(solution)/shard_map/psum | solution.py:438
  (769 shorter events, 2197.7 us)
Async XLA Ops:
  45.6 52.4 all-to-all-start.1
  50.5 90.9 %all-gather.14.cloned.1.call-start = ((), (), s32[]{:S(2)}) async-start(), calls=%async_computation.29 | async-start | bytes 1179648 | tf_op jit(solution)/shard_map/all_gather | solution.py:226
  51.2 131.6 %all-gather.12.cloned.1.call-start = ((), (), s32[]{:S(2)}) async-start(), calls=%async_computation.28 | async-start | bytes 5242880 | tf_op jit(solution)/shard_map/all_gather | solution.py:29
  98.4 42.9 copy-start.100
  100.7 1246.9 %all-gather.22.cloned.1.call-start = ((), (), s32[]{:S(2)}) async-start(), calls=%async_computation.35 | async-start | bytes 5242880 | tf_op jit(solution)/shard_map/all_gather | solution.py:29
  111.7 71.1 %copy-start.37 = (bf16[1024,256]{0,1:T(8,128)(2,1)}, bf16[1024,256]{0,1:T(8,128)(2,1)S(1)}, u32[]{:S(2)}) copy-start(bf16[1024,256]{0,1:T(8,128)(2,1)S(1)} %all_gather.54) | copy-start | bytes 1572868
  120.9 65.6 %copy-start.33 = (bf16[1024,256]{0,1:T(8,128)(2,1)}, bf16[1024,256]{0,1:T(8,128)(2,1)S(1)}, u32[]{:S(2)}) copy-start(bf16[1024,256]{0,1:T(8,128)(2,1)S(1)} %all_gather.55) | copy-start | bytes 1572868
  130.7 57.2 %copy-start.47 = (bf16[1024,256]{0,1:T(8,128)(2,1)}, bf16[1024,256]{0,1:T(8,128)(2,1)S(1)}, u32[]{:S(2)}) copy-start(bf16[1024,256]{0,1:T(8,128)(2,1)S(1)} %all_gather.53) | copy-start | bytes 1572868
  141.3 41.5 copy-start.108
  141.3 45.2 copy-start.106
  141.3 46.5 copy-start.104
  182.7 2331.9 %reduce-scatter.21.cloned.1.call-start = ((), (), s32[]{:S(2)}) async-start(), calls=%async_computation.30 | async-start | bytes 5242880 | tf_op jit(solution)/shard_map/reduce_scatter | solution.py:37
  669.4 49.8 copy-start.111
  669.4 51.0 copy-start.3
  1236.2 49.8 copy-start.111
  1236.2 51.0 copy-start.3
  1347.5 1241.6 %reduce-scatter.25.cloned.1.call-start = ((), (), s32[]{:S(2)}) async-start(), calls=%async_computation.36 | async-start | bytes 5242880 | tf_op jit(solution)/shard_map/reduce_scatter | solution.py:37
  1833.3 49.8 copy-start.114
  1833.3 51.1 copy-start.9
  2399.9 49.8 copy-start.114
  2399.9 51.1 copy-start.9
  2514.0 105.3 %all-gather.18.cloned.1.call-start = ((), (), s32[]{:S(2)}) async-start(), calls=%async_computation.32 | async-start | bytes 2359296 | tf_op jit(solution)/shard_map/all_gather | solution.py:224
  2514.0 78.0 %copy-start.15 = (bf16[2,4,32,8,256]{4,3,1,2,0:T(8,128)(2,1)S(1)}, bf16[2,4,32,8,256]{4,3,1,2,0:T(8,128)(2,1)}, u32[]{:S(2)}) copy-start(bf16[2,4,32,8,256]{4,3,1,2,0:T(8,128)(2,1)} %copy.461) | copy-start | bytes 3145732
  2514.5 187.7 %all-gather.24.cloned.1.call-start = ((), (), s32[]{:S(2)}) async-start(), calls=%async_computation.37 | async-start | bytes 5242880 | tf_op jit(solution)/shard_map/all_gather | solution.py:29
  2514.7 77.9 %copy-start.18 = (bf16[2,256,1024]{2,1,0:T(8,128)(2,1)S(1)}, bf16[2,256,1024]{2,1,0:T(8,128)(2,1)}, u32[]{:S(2)}) copy-start(bf16[2,256,1024]{2,1,0:T(8,128)(2,1)} %reduce-scatter.21.cloned.1.call-done) | copy-start | bytes 3145732
  2594.8 188.9 %all-gather.16.cloned.1.call-start = ((), (), s32[]{:S(2)}) async-start(), calls=%async_computation.31 | async-start | bytes 5242880 | tf_op jit(solution)/shard_map/all_gather | solution.py:29
  2595.6 249.9 %all-gather.20.cloned.1.call-start = ((), (), s32[]{:S(2)}) async-start(), calls=%async_computation.33 | async-start | bytes 2359296 | tf_op jit(solution)/shard_map/all_gather | solution.py:225
  2596.3 382.6 %reduce-scatter.23.cloned.1.call-start = ((), (), s32[]{:S(2)}) async-start(), calls=%async_computation.34 | async-start | bytes 5242880 | tf_op jit(solution)/shard_map/reduce_scatter | solution.py:37
  2855.0 189.0 %reduce-scatter.27.cloned.1.call-start = ((), (), s32[]{:S(2)}) async-start(), calls=%async_computation.38 | async-start | bytes 5242880 | tf_op jit(solution)/shard_map/reduce_scatter | solution.py:37
  2864.4 274.3 %all-gather.30.cloned.1.call-start = ((), (), s32[]{:S(2)}) async-start(), calls=%async_computation.43 | async-start | bytes 5242880 | tf_op jit(solution)/shard_map/all_gather | solution.py:33
  3057.3 162.9 %all-gather.26.cloned.1.call-start = ((), (), s32[]{:S(2)}) async-start(), calls=%async_computation.39 | async-start | bytes 5242880 | tf_op jit(solution)/shard_map/all_gather | solution.py:33
  3060.1 237.5 %reduce-scatter.33.cloned.1.call-start = ((), (), s32[]{:S(2)}) async-start(), calls=%async_computation.44 | async-start | bytes 5242880 | tf_op jit(solution)/shard_map/reduce_scatter | solution.py:43
  3159.8 217.3 %reduce-scatter.29.cloned.1.call-start = ((), (), s32[]{:S(2)}) async-start(), calls=%async_computation.40 | async-start | bytes 5242880 | tf_op jit(solution)/shard_map/reduce_scatter | solution.py:43
  3241.4 229.3 %all-gather.32.cloned.1.call-start = ((), (), s32[]{:S(2)}) async-start(), calls=%async_computation.45 | async-start | bytes 5242880 | tf_op jit(solution)/shard_map/all_gather | solution.py:33
  3389.3 650.3 %all-gather.28.cloned.1.call-start = ((), (), s32[]{:S(2)}) async-start(), calls=%async_computation.41 | async-start | bytes 5242880 | tf_op jit(solution)/shard_map/all_gather | solution.py:33
  3391.2 1408.5 %reduce-scatter.57.cloned.1.call-start = ((), (), s32[]{:S(2)}) async-start(), calls=%async_computation.58 | async-start | bytes 2359296 | tf_op jit(solution)/shard_map/reduce_scatter | solution.py:427
  3401.1 1398.7 %reduce-scatter.59.cloned.1.call-start = ((), (), s32[]{:S(2)}) async-start(), calls=%async_computation.59 | async-start | bytes 2359296 | tf_op jit(solution)/shard_map/reduce_scatter | solution.py:427
  3401.2 69.6 %copy-start.50 = (bf16[1024,256]{1,0:T(8,128)(2,1)S(1)}, bf16[1024,256]{1,0:T(8,128)(2,1)}, u32[]{:S(2)}) copy-start(bf16[1024,256]{1,0:T(8,128)(2,1)} %all_gather.57) | copy-start | bytes 1572868
  3410.6 1409.3 %reduce-scatter.31.cloned.1.call-start = ((), (), s32[]{:S(2)}) async-start(), calls=%async_computation.42 | async-start | bytes 5242880 | tf_op jit(solution)/shard_map/reduce_scatter | solution.py:43
  3583.1 42.8 slice-start
  3685.2 42.3 slice-start.2
  3861.4 42.3 slice-start
  3962.9 42.5 slice-start.2
  4151.1 42.3 slice-start.4
  4252.6 42.3 slice-start.6
  4428.9 42.3 slice-start.4
  4530.5 42.5 slice-start.6
  4626.5 197.7 %reduce-scatter.35.cloned.1.call-start = ((), (), s32[]{:S(2)}) async-start(), calls=%async_computation.46 | async-start | bytes 5242880 | tf_op jit(solution)/shard_map/reduce_scatter | solution.py:43
  4636.6 271.3 %reduce-scatter.53.cloned.1.call-start = ((), (), s32[]{:S(2)}) async-start(), calls=%async_computation.56 | async-start | bytes 2359296 | tf_op jit(solution)/shard_map/reduce_scatter | solution.py:424
  4650.5 95.8 %all-to-all-start.2 = ((bf16[4,256,1024]{1,0,2:T(4,128)(2,1)}), bf16[4,256,1024]{1,0,2:T(4,128)(2,1)S(1)}, u32[]{:S(2)}, u32[]{:S(2)}) async-start(bf16[4,256,1024]{1,0,2:T(4,128)(2,1)} %copy.333), calls=%async_computation.6 | async-start | bytes 4194304 | tf_op jit(solution)/shard_map/all_to_all | solution.py:443
  4654.1 269.6 %reduce-scatter.55.cloned.1.call-start = ((), (), s32[]{:S(2)}) async-start(), calls=%async_computation.57 | async-start | bytes 2359296 | tf_op jit(solution)/shard_map/reduce_scatter | solution.py:424
  4757.1 31.0 all-to-all-start.3
  4761.4 207.2 %reduce-scatter.49.cloned.1.call-start = ((), (), s32[]{:S(2)}) async-start(), calls=%async_computation.54 | async-start | bytes 589824 | tf_op jit(solution)/shard_map/reduce_scatter | solution.py:421
  4766.2 234.6 %reduce-scatter.51.cloned.1.call-start = ((), (), s32[]{:S(2)}) async-start(), calls=%async_computation.55 | async-start | bytes 589824 | tf_op jit(solution)/shard_map/reduce_scatter | solution.py:421
  4771.6 266.2 %reduce-scatter.45.cloned.1.call-start = ((), (), s32[]{:S(2)}) async-start(), calls=%async_computation.52 | async-start | bytes 589824 | tf_op jit(solution)/shard_map/reduce_scatter | solution.py:418
  4799.6 275.6 %reduce-scatter.47.cloned.1.call-start = ((), (), s32[]{:S(2)}) async-start(), calls=%async_computation.53 | async-start | bytes 589824 | tf_op jit(solution)/shard_map/reduce_scatter | solution.py:418
  4806.2 306.3 %reduce-scatter.41.cloned.1.call-start = ((), (), s32[]{:S(2)}) async-start(), calls=%async_computation.50 | async-start | bytes 589824 | tf_op jit(solution)/shard_map/reduce_scatter | solution.py:415
  4831.7 53.4 all-to-all-start.6
  4836.2 313.9 %reduce-scatter.43.cloned.1.call-start = ((), (), s32[]{:S(2)}) async-start(), calls=%async_computation.51 | async-start | bytes 589824 | tf_op jit(solution)/shard_map/reduce_scatter | solution.py:415
  4841.5 345.6 %reduce-scatter.37.cloned.1.call-start = ((), (), s32[]{:S(2)}) async-start(), calls=%async_computation.48 | async-start | bytes 589824 | tf_op jit(solution)/shard_map/reduce_scatter | solution.py:412
  4851.8 372.9 %reduce-scatter.39.cloned.1.call-start = ((), (), s32[]{:S(2)}) async-start(), calls=%async_computation.49 | async-start | bytes 589824 | tf_op jit(solution)/shard_map/reduce_scatter | solution.py:412
  4897.0 329.2 %all-to-all-start.7 = ((bf16[4,1024,256]{2,0,1:T(4,128)(2,1)}), bf16[4,1024,256]{2,0,1:T(4,128)(2,1)}, u32[]{:S(2)}, u32[]{:S(2)}) async-start(bf16[4,1024,256]{2,0,1:T(4,128)(2,1)} %copy.365), calls=%async_computation.15 | async-start | bytes 4194304 | tf_op jit(solution)/shard_map/all_to_all | solution.py:451
  4901.5 462.3 %all-reduce.15.cloned.1.call-start = ((), (), s32[]{:S(2)}) async-start(), calls=%async_computation.47 | async-start | bytes 4194304 | tf_op jit(solution)/shard_map/psum | solution.py:438
  5229.6 137.4 %copy-start.1 = (bf16[32,128,256]{2,1,0:T(8,128)(2,1)S(1)}, bf16[32,128,256]{2,1,0:T(8,128)(2,1)}, u32[]{:S(2)}) copy-start(bf16[32,128,256]{2,1,0:T(8,128)(2,1)} %param.23) | copy-start | bytes 6291460
  (145 other events, 1346.7 us)
Sparse Core Ops, SparseCore 0:
  53.2 23.0 all-gather.13
  100.8 78.7 all-gather.11
  182.9 78.9 all-gather.21
  1347.5 75.1 reduce-scatter.20
  2514.1 75.0 reduce-scatter.24
  2590.9 28.3 all-gather.17
  2621.4 80.7 all-gather.23
  2704.4 79.2 all-gather.15
  2785.6 26.4 all-gather.19
  2855.1 99.0 reduce-scatter.22
  2956.5 87.3 reduce-scatter.26
  3057.4 81.2 all-gather.29
  3140.8 79.2 all-gather.25
  3222.3 75.2 reduce-scatter.32
  3299.9 77.2 reduce-scatter.28
  3389.4 81.2 all-gather.31
  3472.1 79.2 all-gather.27
  3554.6 39.7 reduce-scatter.56
  3598.0 41.2 reduce-scatter.58
  4626.6 108.4 reduce-scatter.30
  4737.5 86.6 reduce-scatter.34
  4827.5 41.6 reduce-scatter.52
  4872.8 50.8 reduce-scatter.54
  4926.6 36.5 reduce-scatter.48
  4966.7 34.1 reduce-scatter.50
  5003.8 34.0 reduce-scatter.44
  5041.1 34.1 reduce-scatter.46
  5078.4 34.0 reduce-scatter.40
  5115.9 34.1 reduce-scatter.42
  5153.0 34.0 reduce-scatter.36
  5190.5 34.1 reduce-scatter.38
  5230.0 133.8 all-reduce.14
where the time goes:
time: 5390 us; the launch traced here: 5370 us
  local copies, waits for them, and re-layouts  2880 us (53%)
  waiting for transfers between devices  1210 us (22%)
  matrix products  797 us (15%)
  blocking collectives  218 us (4%)
  other arithmetic  197 us (4%)
    while x176, local copies, waits for them, and re-layouts  1740 us
    reshape x16, local copies, waits for them, and re-layouts, skew_heads(): return cut.reshape(heads_count, count, width)[:, :, :count]  576 us
    all_gather x4, waiting for transfers between devices, spread_grads(): return lax.all_gather(values, 'tensor', axis=1, tiled=True)  199 us
    slice x8, local copies, waits for them, and re-layouts, skew_heads(): cut = lax.slice_in_dim(flat, count - 1, count - 1 + count * width, axis=1)  188 us
    all_gather x4, waiting for transfers between devices, spread_rows(): return lax.all_gather(values, 'tensor', axis=1, tiled=True)  154 us
    reduce_scatter x4, waiting for transfers between devices, reduce_rows(): lax.psum_scatter(values.astype(jnp.bfloat16), 'tensor', scatter_dimension...  138 us
    reduce_scatter x4, waiting for transfers between devices, reduce_grads(): lax.psum_scatter(values.astype(jnp.bfloat16), 'tensor', scatter_dimension...  137 us
    psum x1, waiting for transfers between devices, shards(): lax.psum((rel_total, shift_pad, hidden_pad, vector_total), ('dp', 'tensor'))  131 us
  transfers between devices with their start and end apart: 37, of which 24 were waited for; matrix products, arithmetic and copies ran while one was open for 71% of the time, Pallas kernels for 0%

commit v1 on v0

v1 whole, which is shorter than its diff:
```python
import functools
import math

import jax
import jax.numpy as jnp
from jax import lax
from jax.experimental import pallas as pl
from jax.experimental.pallas import tpu as pltpu
from jax.sharding import PartitionSpec as P

EPSILON = 1e-07
HEAD = 64
B = 128
SR = 16
UN = 8
NT = (((1,), (1,)), ((), ()))


def dotnt(a, b):
    return lax.dot_general(a, b, NT, preferred_element_type=jnp.float32)


def dotnn(a, b):
    return lax.dot_general(a, b, (((1,), (0,)), ((), ())), preferred_element_type=jnp.float32)


def skew(g_ref, a, n, L):
    parts=[]
    nb=L//B
    for a8 in range(a,a+n,8):
        rot=[pltpu.roll(g_ref[a8:a8+8,t*128:t*128+128], 1+a8, 1, stride=1, stride_axis=0) for t in range(nb+1)]
        msk=lax.broadcasted_iota(jnp.int32,(8,128),1) < (1+a8+lax.broadcasted_iota(jnp.int32,(8,128),0))
        parts.append(jnp.concatenate([jnp.where(msk,rot[t],rot[t+1]) for t in range(nb)],axis=1))
    return jnp.concatenate(parts,axis=0)

def fwd_kernel(len_ref, q_ref, k_ref, v_ref, kf_ref, qf_ref, ctx_ref, p_ref, l_ref, t_ref, kx_ref, vx_ref, g0, g1, s0, s1, *, L, scale):
    W = L + B
    nb = L // B
    gs=(g0,g1); ss=(s0,s1)
    lane = lax.broadcasted_iota(jnp.int32, (1, 128), 1)
    length = len_ref[0]
    row = lax.broadcasted_iota(jnp.int32, (L, 128), 0)
    c2 = scale * math.log2(math.e)
    eye = (lax.broadcasted_iota(jnp.int32,(B,B),0)==lax.broadcasted_iota(jnp.int32,(B,B),1)).astype(jnp.bfloat16)
    zero = jnp.zeros((), jnp.bfloat16)
    mine = [lane < 64, lane >= 64]
    first_other = [lane==64, lane==0]
    for h in range(2):
        bias = jnp.where((row >= length) & first_other[h], -1e30, 0.0).astype(jnp.bfloat16)
        kx_ref[h] = jnp.where(mine[h], k_ref[...], bias)
        vx_ref[h] = jnp.where(mine[h], v_ref[...], jnp.ones((), jnp.bfloat16))
    def tblock(b, _):
        r0 = pl.multiple_of(b*B, B)
        base = pl.multiple_of(L - B - b*B, B)
        for h in range(2):
            kb = jnp.where(mine[h], k_ref[pl.ds(r0,B),:], zero)
            gs[h][...] = dotnt(kb, qf_ref[pl.ds(base, W), :])
        for h in range(2):
            for a in range(0, B, SR):
                t_ref[h, pl.ds(r0+a,SR), :] = skew(gs[h], a, SR, L).astype(jnp.bfloat16)
        return 0
    lax.fori_loop(0, nb, tblock, 0, unroll=2)
    def scores(b, h):
        r0 = pl.multiple_of(b*B, B)
        base = pl.multiple_of(L - B - b*B, B)
        qb = q_ref[pl.ds(r0,B),:]
        qm = jnp.where(mine[h], qb, zero)
        qx = jnp.where(mine[h], qb, first_other[h].astype(jnp.bfloat16))
        gs[h][...] = dotnt(qm, kf_ref[pl.ds(base, W), :])
        lhs = jnp.concatenate([qx, eye], axis=1)
        rhs = jnp.concatenate([kx_ref[h], t_ref[h, :, pl.ds(r0,B)]], axis=1)
        ss[h][...] = dotnt(lhs, rhs)
    def soft(b, h):
        r0 = pl.multiple_of(b*B, B)
        tops=[]
        for a in range(0, B, 8):
            s = ss[h][a:a+8] + skew(gs[h], a, 8, L)
            ss[h][a:a+8] = s
            tops.append(functools.reduce(jnp.maximum,[s[:,t*128:t*128+128] for t in range(nb)]))
        m = jnp.max(jnp.concatenate(tops,axis=0), axis=1, keepdims=True) * c2
        for a in range(0, B, SR):
            p_ref[h, pl.ds(r0+a,SR), :] = jnp.exp2(ss[h][a:a+SR]*c2 - m[a:a+SR]).astype(jnp.bfloat16)
    def out(b, h):
        r0 = pl.multiple_of(b*B, B)
        return dotnn(p_ref[h, pl.ds(r0,B), :], vx_ref[h])
    def finish(b, o0, o1):
        r0 = pl.multiple_of(b*B, B)
        num = jnp.where(mine[0], o0, o1)
        den = jnp.where(mine[0], pltpu.roll(o0,64,1), pltpu.roll(o1,64,1))
        inv = 1.0/den
        ctx_ref[pl.ds(r0,B),:] = (num*inv).astype(jnp.bfloat16)
        l_ref[pl.ds(r0,B),:] = inv
    scores(0,0)
    def sblock(b, o0):
        scores(b,1)
        soft(b,0)
        o0 = out(b,0)
        scores(jnp.minimum(b+1,nb-1),0)
        soft(b,1)
        o1 = out(b,1)
        finish(b,o0,o1)
        return 0
    lax.fori_loop(0, nb, sblock, 0, unroll=8)

def attn_fwd(length, q, k, v, kf, qf, *, scale):
    L, C = q.shape
    col = lambda r: pl.BlockSpec((r,128), lambda h, *_: (0,h))
    return pl.pallas_call(
        functools.partial(fwd_kernel, L=L, scale=scale),
        grid_spec=pltpu.PrefetchScalarGridSpec(num_scalar_prefetch=1, grid=(C//128,),
            in_specs=[col(L),col(L),col(L),col(2*L),col(2*L)],
            out_specs=[col(L), pl.BlockSpec((2,L,L), lambda h,*_: (h,0,0)), col(L)],
            scratch_shapes=[pltpu.VMEM((2,L,L),jnp.bfloat16), pltpu.VMEM((2,L,128),jnp.bfloat16), pltpu.VMEM((2,L,128),jnp.bfloat16)]
              +[pltpu.VMEM((B,L+B),jnp.float32)]*2+[pltpu.VMEM((B,L),jnp.float32)]*2),
        out_shape=[jax.ShapeDtypeStruct((L,C),jnp.bfloat16), jax.ShapeDtypeStruct((C//64,L,L),jnp.bfloat16), jax.ShapeDtypeStruct((L,C),jnp.float32)],
        compiler_params=pltpu.CompilerParams(vmem_limit_bytes=50<<20),
    )(length, q, k, v, kf, qf)


def unskew(x, a8):
    nb = x.shape[1]//B
    sub = lax.broadcasted_iota(jnp.int32,(8,128),0)
    lane = lax.broadcasted_iota(jnp.int32,(8,128),1)
    keep = lane >= (127-a8) - sub
    idx=(lane-(127-a8)+sub)&127
    rot=[jnp.take_along_axis(x[:,t*128:t*128+128], idx, axis=1) for t in range(nb)]
    zero = jnp.zeros((8,128), x.dtype)
    return jnp.concatenate([jnp.where(keep, rot[t] if t<nb else zero, rot[t-1] if t>0 else zero) for t in range(nb+1)], axis=1)

def bwd_kernel(p_ref, q_ref, k_ref, v_ref, do_ref, ctx_ref, li_ref, kf_ref, qf_ref,
               dq_ref, dk_ref, dv_ref, dkf_ref, dqf_ref, sums_ref,
               dox_ref, dot_ref, qt_ref, kt_ref, vx_ref, ds_ref, d0, d1, akf, aqf, *, L, scale):
    W = L + B
    nb = L // B
    dd=(d0,d1)
    lane = lax.broadcasted_iota(jnp.int32, (1, 128), 1)
    mine = [lane < 64, lane >= 64]
    base_lane = [64, 0]
    dos = (do_ref[...].astype(jnp.float32) * li_ref[...]).astype(jnp.bfloat16)
    prod = dos.astype(jnp.float32) * ctx_ref[...].astype(jnp.float32)
    for h in range(2):
        delta = -jnp.sum(jnp.where(mine[h], prod, 0.0), axis=1, keepdims=True)
        hi = delta.astype(jnp.bfloat16).astype(jnp.float32)
        lo = delta - hi
        extra = jnp.where(lane == base_lane[h], hi, jnp.where(lane == base_lane[h]+1, lo, 0.0)).astype(jnp.bfloat16)
        dox_ref[h] = jnp.where(mine[h], dos, extra)
        vx_ref[h] = jnp.where(mine[h], v_ref[...], jnp.ones((), jnp.bfloat16))
    dot_ref[...] = dos.T
    qt_ref[...] = q_ref[...].T
    kt_ref[...] = k_ref[...].T
    akf[...] = jnp.zeros_like(akf)
    aqf[...] = jnp.zeros_like(aqf)
    def iblock(b, sq):
        r0 = pl.multiple_of(b*B, B)
        base = pl.multiple_of(L - B - b*B, B)
        outs=[]
        for h in range(2):
            dp = dotnt(dox_ref[h, pl.ds(r0,B), :], vx_ref[h])
            for a in range(0, B, SR):
                ds = p_ref[h, pl.ds(r0+a,SR), :].astype(jnp.float32) * dp[a:a+SR]
                ds_ref[h, pl.ds(r0+a,SR), :] = ds.astype(jnp.bfloat16)
                dd[h][a:a+SR, :] = jnp.concatenate([unskew(ds[s:s+8], a+s) for s in range(0,SR,8)],axis=0).astype(jnp.bfloat16)
            outs.append(dotnn(ds_ref[h, pl.ds(r0,B), :], k_ref[...]) + dotnn(dd[h][...], kf_ref[pl.ds(base, W), :]))
            akf[h*64:h*64+64, pl.ds(base, W)] += dotnn(qt_ref[h*64:h*64+64, pl.ds(r0,B)], dd[h][...])
        dq = jnp.where(mine[0], outs[0], outs[1]) * scale
        dq_ref[pl.ds(r0,B),:] = dq.astype(jnp.bfloat16)
        return sq + jnp.sum(dq.reshape(B//8,8,128), axis=0)
    sq = lax.fori_loop(0, nb, iblock, jnp.zeros((8,128),jnp.float32), unroll=UN)
    def jblock(b, sk):
        r0 = pl.multiple_of(b*B, B)
        base = pl.multiple_of(L - B - b*B, B)
        outs=[]
        for h in range(2):
            dst = ds_ref[h, :, pl.ds(r0,B)].T
            for a in range(0, B, SR):
                x = dst[a:a+SR].astype(jnp.float32)
                dd[h][a:a+SR, :] = jnp.concatenate([unskew(x[s:s+8], a+s) for s in range(0,SR,8)],axis=0).astype(jnp.bfloat16)
            outs.append(dotnn(dst, q_ref[...]) + dotnn(dd[h][...], qf_ref[pl.ds(base, W), :]))
            aqf[h*64:h*64+64, pl.ds(base, W)] += dotnn(kt_ref[h*64:h*64+64, pl.ds(r0,B)], dd[h][...])
        dk = jnp.where(mine[0], outs[0], outs[1]) * scale
        dk_ref[pl.ds(r0,B),:] = dk.astype(jnp.bfloat16)
        return sk + jnp.sum(dk.reshape(B//8,8,128), axis=0)
    sk = lax.fori_loop(0, nb, jblock, jnp.zeros((8,128),jnp.float32), unroll=UN)
    dvt = jnp.concatenate([dotnn(dot_ref[h*64:h*64+64,:], p_ref[h]) for h in range(2)], axis=0)
    dv = dvt.T
    dv_ref[...] = dv.astype(jnp.bfloat16)
    sv = jnp.sum(dv.reshape(L//8,8,128), axis=0)
    sums_ref[0:8] = sq
    sums_ref[8:16] = sk
    sums_ref[16:24] = sv
    dkf_ref[...] = (akf[...]*scale).astype(jnp.bfloat16)
    dqf_ref[...] = (aqf[...]*scale).astype(jnp.bfloat16)

def attn_bwd(p, q, k, v, do, ctx, linv, kf, qf, *, scale):
    L, C = q.shape
    col = lambda r: pl.BlockSpec((r,128), lambda h: (0,h))
    rowb = pl.BlockSpec((128,2*L), lambda h: (h,0))
    bf=jnp.bfloat16
    return pl.pallas_call(
        functools.partial(bwd_kernel, L=L, scale=scale),
        grid=(C//128,),
        in_specs=[pl.BlockSpec((2,L,L), lambda h:(h,0,0))]+[col(L)]*6+[col(2*L)]*2,
        out_specs=[col(L)]*3+[rowb]*2+[pl.BlockSpec((24,128), lambda h:(0,h))],
        scratch_shapes=[pltpu.VMEM((2,L,128),bf), pltpu.VMEM((128,L),bf), pltpu.VMEM((128,L),bf), pltpu.VMEM((128,L),bf), pltpu.VMEM((2,L,128),bf),
            pltpu.VMEM((2,L,L),bf), pltpu.VMEM((B,L+B),bf), pltpu.VMEM((B,L+B),bf), pltpu.VMEM((128,2*L),jnp.float32), pltpu.VMEM((128,2*L),jnp.float32)],
        out_shape=[jax.ShapeDtypeStruct((L,C),bf)]*3+[jax.ShapeDtypeStruct((C,2*L),bf)]*2+[jax.ShapeDtypeStruct((24,C),jnp.float32)],
        compiler_params=pltpu.CompilerParams(vmem_limit_bytes=56<<20),
    )(p, q, k, v, do, ctx, linv, kf, qf)


def normalize(z):
    center = z - jnp.mean(z, axis=-1, keepdims=True)
    r = lax.rsqrt(jnp.mean(center * center, axis=-1, keepdims=True) + EPSILON)
    return center * r, r


def norm_back(g, n, r):
    return r * (g - jnp.mean(g, axis=-1, keepdims=True) - n * jnp.mean(g * n, axis=-1, keepdims=True))


def mm(spec, a, b):
    return jnp.einsum(spec, a, b, preferred_element_type=jnp.float32)


def shards(
    inputs,
    cotangent,
    lengths,
    dealing,
    buckets,
    rel_embed,
    query_weight,
    key_weight,
    value_weight,
    proj_shifts,
    merge_weight,
    inner_weight,
    hidden_shift,
    outer_weight,
    layer_vectors,
):
    tn = lax.axis_size("tensor")
    gn = lax.axis_size("dp")
    me = lax.axis_index("dp") * tn + lax.axis_index("tensor")
    count, lg, dt = inputs.shape
    L, D = lg * gn, dt * tn
    assert count == tn * gn
    bf = jnp.bfloat16
    f32 = jnp.float32
    scale = 1.0 / math.sqrt(3.0 * HEAD)
    seq_axes = ("dp", "tensor")
    w_axes = ("tensor", "dp")

    def deal(a):
        a = lax.all_to_all(a, seq_axes, split_axis=0, concat_axis=0, tiled=True)
        return a.reshape(gn, tn, lg, dt).transpose(0, 2, 1, 3).reshape(L, D)

    def undeal(a):
        a = a.reshape(gn, lg, tn, dt).transpose(0, 2, 1, 3).reshape(count, lg, dt)
        return lax.all_to_all(a, seq_axes, split_axis=0, concat_axis=0, tiled=True)

    def gather(w):
        rows, cols = w.shape
        return lax.all_gather(w, w_axes, axis=0, tiled=False).reshape(tn, gn * rows, cols)

    def scatter(g):
        t, rows, cols = g.shape
        g = g.astype(bf).reshape(t, gn, rows // gn, cols)
        g = lax.psum_scatter(g, "dp", scatter_dimension=1, tiled=False)
        return lax.psum_scatter(g, "tensor", scatter_dimension=0, tiled=False)

    x = deal(inputs)
    rel_cols = lax.dynamic_slice_in_dim(rel_embed, lax.axis_index("tensor") * dt, dt, 1)
    first = gather(jnp.concatenate([query_weight, key_weight, value_weight], axis=1))
    rel4 = gather(rel_cols)
    wq, wk, wv = first[:, :, :dt], first[:, :, dt : 2 * dt], first[:, :, 2 * dt :]
    ff = inner_weight.shape[1]
    second = gather(jnp.concatenate([inner_weight, outer_weight, merge_weight], axis=1))
    wi, wo, wm = second[:, :, :ff], second[:, :, ff : 2 * ff], second[:, :, 2 * ff :]
    cot = deal(cotangent)
    biases = lax.all_gather(
        jnp.concatenate([proj_shifts.reshape(-1), hidden_shift]), "tensor", axis=0, tiled=False
    ).astype(f32)
    shifts = biases[:, : 3 * dt].reshape(tn, 3, dt)
    hidden_bias = biases[:, 3 * dt :]
    vectors = layer_vectors.astype(f32)
    length = jnp.sum(jnp.where(dealing == me, lengths, 0)).reshape(1)
    spans = rel4.shape[1]
    places = jnp.concatenate([buckets[::-1], jnp.full((1,), -1, jnp.int32)])
    onehot = (places[:, None] == jnp.arange(spans, dtype=jnp.int32)[None, :]).astype(bf)
    rel = rel4.transpose(1, 0, 2).reshape(spans, D)

    q = (mm("lk,tkc->ltc", x, wq) + shifts[:, 0]).astype(bf).reshape(L, D)
    k = (mm("lk,tkc->ltc", x, wk) + shifts[:, 1]).astype(bf).reshape(L, D)
    v = (mm("lk,tkc->ltc", x, wv) + shifts[:, 2]).astype(bf).reshape(L, D)
    qpos = (mm("lk,tkc->ltc", rel, wq) + shifts[:, 0]).astype(bf).reshape(spans, D)
    kpos = (mm("lk,tkc->ltc", rel, wk) + shifts[:, 1]).astype(bf).reshape(spans, D)
    qf = mm("ms,sd->md", onehot, qpos).astype(bf)
    kf = mm("ms,sd->md", onehot, kpos).astype(bf)
    ctx, probs, inv = attn_fwd(length, q, k, v, kf, qf, scale=scale)
    ctx4 = ctx.reshape(L, tn, dt)
    z1 = mm("ltc,toc->lo", ctx4, wm) + vectors[0] + x.astype(f32)
    n1, r1 = normalize(z1)
    h1 = n1 * vectors[1] + vectors[2]
    h1_low = h1.astype(bf)
    pre = mm("la,tah->lth", h1_low, wi) + hidden_bias
    phi = 0.5 + 0.5 * lax.erf(pre * math.sqrt(0.5))
    act = (pre * phi).astype(bf)
    slope = phi + pre * jnp.exp(-0.5 * pre * pre) * (1.0 / math.sqrt(2.0 * math.pi))
    slope = slope.astype(bf)
    z2 = mm("ltf,tof->lo", act, wo) + vectors[3] + h1
    n2, r2 = normalize(z2)
    y = n2 * vectors[4] + vectors[5]
    out = undeal(y.astype(bf))
    dy = cot.astype(f32)
    dz2 = norm_back(dy * vectors[4], n2, r2)
    dffn = dz2.astype(bf)
    outer_part = mm("lo,ltf->tof", dffn, act)
    dact = mm("lo,tof->ltf", dffn, wo)
    dpre = dact * slope.astype(f32)
    dpre_low = dpre.astype(bf)
    hidden_sum = jnp.sum(dpre, axis=0).reshape(-1)
    inner_part = mm("la,lth->tah", h1_low, dpre_low)
    dh1 = dz2 + mm("lth,tah->la", dpre_low, wi)
    dz1 = norm_back(dh1 * vectors[1], n1, r1)
    dattn = dz1.astype(bf)
    merge_part = mm("lo,ltc->toc", dattn, ctx4)
    dctx = mm("lo,toc->ltc", dattn, wm).astype(bf).reshape(L, D)
    outer_grad = scatter(outer_part)
    inner_grad = scatter(inner_part)
    merge_grad = scatter(merge_part)
    dq, dk, dv, dkf, dqf, sums = attn_bwd(probs, q, k, v, dctx, ctx, inv, kf, qf, scale=scale)
    dkpos = mm("dm,ms->sd", dkf, onehot)
    dqpos = mm("dm,ms->sd", dqf, onehot)
    sums = sums.reshape(3, 8, D).sum(axis=1)
    shift_sum = sums + jnp.stack(
        [jnp.sum(dqpos, axis=0), jnp.sum(dkpos, axis=0), jnp.zeros((D,), f32)]
    )
    dq4, dk4, dv4 = (a.reshape(L, tn, dt) for a in (dq, dk, dv))
    dqp4, dkp4 = (a.astype(bf).reshape(spans, tn, dt) for a in (dqpos, dkpos))
    dx = dz1 + mm("ltj,tej->le", dq4, wq) + mm("ltj,tej->le", dk4, wk) + mm("ltj,tej->le", dv4, wv)
    grad_in = undeal(dx.astype(bf))
    query_part = mm("le,ltj->tej", x, dq4) + mm("se,stj->tej", rel, dqp4)
    key_part = mm("le,ltj->tej", x, dk4) + mm("se,stj->tej", rel, dkp4)
    value_part = mm("le,ltj->tej", x, dv4)
    rel_part = mm("stj,tej->se", dqp4, wq) + mm("stj,tej->se", dkp4, wk)
    qkv = scatter(jnp.concatenate([query_part, key_part, value_part], axis=2)).astype(f32)
    rel_mine = lax.psum_scatter(
        rel_part.astype(bf).reshape(count, spans // count, D), seq_axes, scatter_dimension=0, tiled=False
    )
    rel_grad = lax.all_gather(rel_mine.astype(f32), seq_axes, axis=0, tiled=True)
    vector_sum = jnp.stack(
        [
            jnp.sum(dz1, axis=0),
            jnp.sum(dh1 * n1, axis=0),
            jnp.sum(dh1, axis=0),
            jnp.sum(dz2, axis=0),
            jnp.sum(dy * n2, axis=0),
            jnp.sum(dy, axis=0),
        ]
    )
    hidden_sum, vector_sum = lax.psum((hidden_sum, vector_sum), seq_axes)
    shift_sum = lax.psum(shift_sum, seq_axes)
    return (
        out,
        grad_in,
        rel_grad,
        qkv[:, :dt],
        qkv[:, dt : 2 * dt],
        qkv[:, 2 * dt :],
        shift_sum,
        merge_grad.astype(f32),
        inner_grad.astype(f32),
        hidden_sum,
        outer_grad.astype(f32),
        vector_sum,
    )


def solution(mesh):
    split = P("dp", "tensor")
    whole = P(None, "dp", "tensor")
    in_specs = (
        whole, whole, P(), P(), P(), P("dp", None), split, split, split, P(None, "tensor"),
        split, split, P("tensor"), split, P(),
    )
    out_specs = (whole, whole, P(), split, split, split, P(), split, split, P(), split, P())
    return jax.shard_map(shards, mesh=mesh, in_specs=in_specs, out_specs=out_specs, check_vma=False)
```

time: 5390 us -> 1110 us (0.21)
  local copies, waits for them, and re-layouts: 2880 us -> 108 us
  waiting for transfers between devices: 1210 us -> 350 us
  matrix products: 797 us -> 219 us
  Pallas kernels: 0 us -> 196 us
  other arithmetic: 197 us -> 35.6 us
    while x178 -> x0, local copies, waits for them, and re-layouts: 1740 us -> none
    dot_general x98 -> x28, matrix products: 726 us -> 219 us  [mm(): return jnp.einsum(spec, a, b, preferred_element_type=jnp.float32)]
    reshape x18 -> x20, local copies, waits for them, and re-layouts: 577 us -> 72.3 us  [the longest x3 19.1 us: scatter(): g = g.astype(bf).reshape(t, gn, rows // gn, cols)]
    all_gather x11 -> x4, waiting for transfers between devices: 375 us -> 37.9 us  [the longest x1 37.8 us: shards(): lax.all_gather(rel_mine.astype(f32), seq_axes, axis=0, tiled=True)]
    slice x17 -> x5, local copies, waits for them, and re-layouts: 238 us -> 0.79 us  [the longest x1 0.75 us: shards(): qkv[:, 2 * dt:]]
    reduce_scatter x20 -> x9, waiting for transfers between devices: 542 us -> 311 us  [the longest x4 192 us: scatter(): g = lax.psum_scatter(g, 'dp', scatter_dimension=1, tiled=False)]
    pallas_call x0 -> x2, Pallas kernels: none -> 196 us  [the longest x1 119 us: attn_bwd(): pl.pallas_call(functools.partial(bwd_kernel, L=L, scale=scale), grid=(C /...]
    pad x16 -> x0, local copies, waits for them, and re-layouts: 177 us -> none  [the longest x8 115 us: skew_heads(): cut = lax.slice_in_dim(flat, count - 1, count - 1 + count * width, axis=1)]
  transfers between devices with their start and end apart: 37 -> 16, of which waited for: 24 -> 8; matrix products, arithmetic and copies ran while one was open for 71% -> 23% of each run, Pallas kernels for 0% -> 18%
where the time goes in v1:
time: 1110 us; the launch traced here: 1100 us
  waiting for transfers between devices  350 us (32%)
  matrix products  219 us (20%)
  Pallas kernels  196 us (18%)
  blocking collectives  167 us (15%)
  local copies, waits for them, and re-layouts  108 us (10%)
  other arithmetic  35.6 us (3%)
  between operations  14.8 us (1%)
  starting transfers between devices  14 us (1%)
    dot_general x28, matrix products, mm(): return jnp.einsum(spec, a, b, preferred_element_type=jnp.float32)  219 us
    reduce_scatter x4, waiting for transfers between devices, scatter(): g = lax.psum_scatter(g, 'dp', scatter_dimension=1, tiled=False)  192 us
    pallas_call x1, Pallas kernels, attn_bwd(): pl.pallas_call(functools.partial(bwd_kernel, L=L, scale=scale), grid=(C /...  119 us
    reduce_scatter x4, waiting for transfers between devices, scatter(): return lax.psum_scatter(g, 'tensor', scatter_dimension=0, tiled=False)  77.8 us
    pallas_call x1, Pallas kernels, attn_fwd(): pl.pallas_call(functools.partial(fwd_kernel, L=L, scale=scale), grid_spec...  76.3 us
    all_gather x1, blocking collectives, shards(): lax.all_gather(jnp.concatenate([proj_shifts.reshape(-1), hidden_shift]),...  66.7 us
    all_to_all x1, blocking collectives, deal(): a = lax.all_to_all(a, seq_axes, split_axis=0, concat_axis=0, tiled=True)  59.9 us
    reduce_scatter x1, waiting for transfers between devices, shards(): lax.psum_scatter(rel_part.astype(bf).reshape(count, spans // count, D), s...  41 us
  transfers between devices with their start and end apart: 16, of which 8 were waited for; matrix products, arithmetic and copies ran while one was open for 23% of the time, Pallas kernels for 18%

profile of v1, /device:TPU:0, one launch (start us, length us, event | category | flops | bytes accessed | tf_op | source)
XLA Modules:
  0.0 1104.1 jit_solution(11045224591122373240)
XLA Ops:
  12.5 59.9 %all_to_all.20 = bf16[32,128,256]{2,1,0:T(8,128)(2,1)} all-to-all(bf16[32,128,256]{2,1,0:T(8,128)(2,1)} %param.15), channel_id=1, replica_groups=mesh['dp'=8,'tensor'=4] {'dp','tensor'}, dimensions={0} | all-to-all | bytes 4194304 | tf_op jit(solution)/shard_map/all_to_all | solution.py:255
  72.4 4.5 all-to-all-start.2
  77.0 66.7 %all-gather.5 = bf16[4,1,1792]{2,1,0:T(2,128)(2,1)S(1)} all-gather(bf16[1,1,1792]{2,1,0:T(2,128)(2,1)S(1)} %reshape.248), channel_id=3, replica_groups=mesh['dp'=8,'tensor'=4] {'tensor'}, dimensions={0}, use_global_device_ids=true | all-gather | bytes 17920 | tf_op jit(solution)/shard_map/all_gather | solution.py:281
  144.8 3.0 copy.224
  149.6 5.0 copy.227
  154.6 4.9 reshape.252
  159.5 3.4 copy.209
  164.6 2.9 copy.210
  168.0 6.4 bitcast_reduce_fusion
  174.5 5.4 add_convert_fusion.3
  179.9 4.1 copy.194.v_ref
  184.0 5.4 add_convert_fusion.4
  189.4 3.9 copy.193.k_ref
  193.3 5.4 add_convert_fusion.5
  198.7 3.9 copy.192.q_ref
  202.7 2.9 add_convert_fusion.6
  205.6 2.9 add_convert_fusion.7
  208.5 4.0 fusion.22.kf_ref
  212.5 3.9 fusion.23.qf_ref
  216.4 76.3 %shard_map.238 = (bf16[1024,1024]{1,0:T(8,128)(2,1)S(1)}, bf16[16,1024,1024]{2,1,0:T(8,128)(2,1)}, f32[1024,1024]{1,0:T(8,128)}) custom-call(s32[1]{0:T(128)} %bitcast.len_ref, bf16[1024,1024]{1,0:T(8,128)(2,1)} %copy.192.q_ref, bf16[1024,1024]{1,0:T(8,128)(2,1)} %copy.193.k_ref, bf16[1024,1024]{1,0:T(8,128)(2,1)} %copy.194.v_ref, ...), custom_call_target="tpu_custom_call" | custom-call | tf_op jit(solution)/shard_map/pallas_call | solution.py:108
  292.7 2.6 copy.203
  295.3 5.4 fusion.82
  301.3 17.8 %multiply_convert_fusion = (bf16[1024,4,1024]{2,0,1:T(8,128)(2,1)}, f32[1024,4,1024]{2,0,1:T(8,128)}) fusion(f32[4,1024]{1,0:T(4,128)S(1)} %slice.96, bf16[4,1024,2304]{2,1,0:T(8,128)(2,1)} %bitcast.290, f32[1024,1024]{1,0:T(8,128)S(1)} %get-tuple-element.67, f32[1024]{0:T(1024)S(1)} %bitcast.282, f32[1024]{0:T(1024)S(1)} %bitcast.270, ...), kind=kOutput, calls=%fused_computation.7 | convolution fusion | flops 8620343296 | bytes 37781504 | tf_op jit(solution)/shard_map/la,tah->lth/dot_general | solution.py:222
  319.2 14.6 %fusion.83 = (f32[1024]{0:T(1024)S(1)}, f32[1024,1024]{1,0:T(8,128)S(1)}) fusion(f32[1024]{0:T(1024)S(1)} %bitcast.283, f32[1024]{0:T(1024)S(1)} %bitcast.271, f32[1024]{0:T(1024)S(1)} %add_rsqrt_fusion.1, f32[1024,1024]{1,0:T(8,128)S(1)} %get-tuple-element.67, f32[1024]{0:T(1024)S(1)} %broadcast_multiply_fusion.4, f32[1024]{0:T(1024)S(1)} %bitcast.285, ...), kind=kOutput, calls=%fused_computation.134 | convolution fusion | flops 8597273600 | bytes 25190400 | tf_op jit(solution)/shard_map/ltf,tof->lo/dot_general | solution.py:222
  338.2 3.3 fusion.75
  341.5 24.7 %fusion.5 = (f32[4,1024]{1,0:T(4,128)}, bf16[1024,4,1024]{2,0,1:T(8,128)(2,1)}, f32[1024,4,1024]{2,0,1:T(8,128)}) fusion(f32[1024,4,1024]{2,0,1:T(8,128)} %get-tuple-element.69, f32[4,1024]{1,0:T(4,128)S(1)} %slice.96, bf16[4,1024,2304]{2,1,0:T(8,128)(2,1)} %bitcast.292, f32[1024,1024]{1,0:T(8,128)S(1)} %get-tuple-element.42), kind=kOutput, calls=%fused_computation.9 | convolution fusion | flops 8645505024 | bytes 54558720 | tf_op jit(solution)/shard_map/lo,tof->ltf/dot_general | solution.py:222
  366.2 20.4 %multiply_reduce_fusion.1 = (f32[1024]{0:T(1024)S(1)}, f32[1024]{0:T(1024)S(1)}, f32[1024]{0:T(1024)S(1)}, f32[1024]{0:T(1024)S(1)}, f32[1024,1024]{1,0:T(8,128)}) fusion(f32[1024,1024]{1,0:T(8,128)} %copy-done.4, f32[1024]{0:T(1024)S(1)} %add_rsqrt_fusion.1, f32[1024]{0:T(1024)S(1)} %broadcast_multiply_fusion.4, f32[1024]{0:T(1024)S(1)} %bitcast.272, ...), kind=kOutput, calls=%fused_computation.35 | convolution fusion | flops 8612999168 | bytes 46166016 | tf_op jit(solution)/shard_map/lth,tah->la/dot_general | solution.py:222
  386.6 4.3 fusion.76
  396.5 5.2 fusion.45
  404.3 119.5 %shard_map.239 = (bf16[1024,1024]{1,0:T(8,128)(2,1)}, bf16[1024,1024]{1,0:T(8,128)(2,1)}, bf16[1024,1024]{1,0:T(8,128)(2,1)}, bf16[1024,2048]{1,0:T(8,128)(2,1)}...) custom-call(bf16[16,1024,1024]{2,1,0:T(8,128)(2,1)} %get-tuple-element.22.p_ref, bf16[1024,1024]{1,0:T(8,128)(2,1)} %copy.192.q_ref, ...), custom_call_target="tpu_custom_call" | custom-call | tf_op jit(solution)/shard_map/pallas_call | solution.py:199
  523.8 5.0 fusion.78
  529.3 5.3 fusion.79
  535.2 4.3 copy.205
  539.6 3.9 copy.206
  543.5 2.9 fusion.64
  546.4 4.0 fusion.34
  550.5 3.7 convolution_convert_fusion.2
  554.4 6.0 fusion.85
  560.4 3.9 copy.204
  569.2 3.8 add_convert_fusion
  576.2 4.7 fusion.84
  585.3 5.9 pad_maximum_fusion
  591.6 16.7 %convolution_convert_fusion = bf16[4,1024,1024]{1,2,0:T(8,128)(2,1)} fusion(bf16[1024,4,1024]{2,0,1:T(8,128)(2,1)} %get-tuple-element.68, f32[1024,1024]{1,0:T(8,128)} %copy-done.7), kind=kOutput, calls=%fused_computation.19 | convolution fusion | flops 8595177472 | bytes 20971520 | tf_op jit(solution)/shard_map/lo,ltf->tof/dot_general | solution.py:222
  608.2 8.3 copy.182
  617.3 22.4 %convolution_convert_fusion.1 = bf16[4,1024,1024]{1,2,0:T(8,128)(2,1)} fusion(f32[1024,1024]{1,0:T(8,128)} %copy-done.4, f32[1024]{0:T(1024)S(1)} %bitcast.284, f32[1024]{0:T(1024)S(1)} %bitcast.274, f32[1024]{0:T(1024)S(1)} %add_rsqrt_fusion.1, f32[1024]{0:T(1024)S(1)} %broadcast_multiply_fusion.4, f32[1024,4,1024]{2,0,1:T(8,128)} %get-tuple-element.72, ...), kind=kOutput, calls=%fused_computation.20 | convolution fusion | flops 8611954688 | bytes 37765120 | tf_op jit(solution)/shard_map/la,lth->tah/dot_general | solution.py:222
  639.6 8.2 copy.180
  648.7 41.0 %reduce-scatter.10.cloned.1.call-done = bf16[1,16,1024]{2,1,0:T(8,128)(2,1)} async-done(((bf16[32,16,1024]{2,1,0:T(8,128)(2,1)}), bf16[1,16,1024]{2,1,0:T(8,128)(2,1)}) %reduce-scatter.10.cloned.1.call-update) | async-done | bytes 32784 | tf_op jit(solution)/shard_map/reduce_scatter | solution.py:348
  691.1 3.3 reshape.215
  696.2 2.7 all-to-all-start.1
  699.2 7.5 fusion.55
  706.7 6.0 fusion.60
  712.6 48.3 %reduce-scatter.12.cloned.1.call-done = bf16[4,1,128,768]{3,2,0,1:T(8,128)(2,1)} async-done(((bf16[4,8,128,768]{3,2,0,1:T(8,128)(2,1)}), bf16[4,1,128,768]{3,2,0,1:T(8,128)(2,1)}) %reduce-scatter.12.cloned.1.call-update) | async-done | bytes 786448 | tf_op jit(solution)/shard_map/reduce_scatter | solution.py:269
  760.9 9.8 fusion.15
  770.7 4.6 reshape.221
  775.3 3.7 copy.164
  779.0 5.1 all-to-all-start.3
  784.1 69.3 %reduce-scatter.24.cloned.1.call-done = bf16[4,1,128,1024]{3,2,0,1:T(8,128)(2,1)} async-done(((bf16[4,8,128,1024]{3,2,0,1:T(8,128)(2,1)}), bf16[4,1,128,1024]{3,2,0,1:T(8,128)(2,1)}) %reduce-scatter.24.cloned.1.call-update) | async-done | bytes 1048592 | tf_op jit(solution)/shard_map/reduce_scatter | solution.py:269
  853.5 74.7 %reduce-scatter.20.cloned.1.call-done = bf16[4,1,128,1024]{3,2,0,1:T(8,128)(2,1)} async-done(((bf16[4,8,128,1024]{3,2,0,1:T(8,128)(2,1)}), bf16[4,1,128,1024]{3,2,0,1:T(8,128)(2,1)}) %reduce-scatter.20.cloned.1.call-update) | async-done | bytes 1048592 | tf_op jit(solution)/shard_map/reduce_scatter | solution.py:269
  928.5 40.6 %all-reduce = (f32[3,1024]{1,0:T(4,128)}, f32[4096]{0:T(1024)}, f32[6,1024]{1,0:T(8,128)}) all-reduce(f32[3,1024]{1,0:T(4,128)S(1)} %maximum_add_fusion, f32[4096]{0:T(1024)S(1)} %bitcast.263, f32[6,1024]{1,0:T(8,128)S(1)} %stack.39), channel_id=1, replica_groups=mesh['dp'=8,'tensor'=4] {'dp','tensor'}, use_global_device_ids=true, to_apply=%region_15.16 | all-reduce | flops 13312 | bytes 106496 | tf_op jit(solution)/shard_map/psum | solution.py:363
  970.6 37.8 %all-gather.17.cloned.1.call-done = f32[1,512,1024]{2,1,0:T(8,128)} async-done(((f32[1,16,1024]{2,1,0:T(8,128)}), f32[1,512,1024]{2,1,0:T(8,128)}) %all-gather.17.cloned.1.call-update) | async-done | bytes 2097168 | tf_op jit(solution)/shard_map/all_gather | solution.py:351
  1008.5 24.5 %reduce-scatter.14.cloned.1.call-done = bf16[1,128,768]{2,1,0:T(8,128)(2,1)} async-done(((bf16[4,128,768]{2,1,0:T(8,128)(2,1)}), bf16[1,128,768]{2,1,0:T(8,128)(2,1)}) %reduce-scatter.14.cloned.1.call-update) | async-done | bytes 196624 | tf_op jit(solution)/shard_map/reduce_scatter | solution.py:270
  1034.6 26.9 %reduce-scatter.26.cloned.1.call-done = bf16[1,128,1024]{2,1,0:T(8,128)(2,1)} async-done(((bf16[4,128,1024]{2,1,0:T(8,128)(2,1)}), bf16[1,128,1024]{2,1,0:T(8,128)(2,1)}) %reduce-scatter.26.cloned.1.call-update) | async-done | bytes 262160 | tf_op jit(solution)/shard_map/reduce_scatter | solution.py:270
  1063.3 26.4 %reduce-scatter.22.cloned.1.call-done = bf16[1,128,1024]{2,1,0:T(8,128)(2,1)} async-done(((bf16[4,128,1024]{2,1,0:T(8,128)(2,1)}), bf16[1,128,1024]{2,1,0:T(8,128)(2,1)}) %reduce-scatter.22.cloned.1.call-update) | async-done | bytes 262160 | tf_op jit(solution)/shard_map/reduce_scatter | solution.py:270
  1092.9 3.2 copy.232
  (157 shorter events, 52.2 us)
Async XLA Ops:
  7.2 0.9 copy-start
  7.2 137.6 %all-gather.13.cloned.1.call-start = ((), (), s32[]{:S(2)}) async-start(), calls=%async_computation.23 | async-start | bytes 1081344 | tf_op jit(solution)/shard_map/all_gather | solution.py:264
  8.7 165.7 %all-gather.11.cloned.1.call-start = ((), (), s32[]{:S(2)}) async-start(), calls=%async_computation.22 | async-start | bytes 6488064 | tf_op jit(solution)/shard_map/all_gather | solution.py:264
  10.4 284.9 %all-gather.15.cloned.1.call-start = ((), (), s32[]{:S(2)}) async-start(), calls=%async_computation.24 | async-start | bytes 19464192 | tf_op jit(solution)/shard_map/all_gather | solution.py:264
  12.4 64.5 %copy-start.28 = (bf16[3,256]{1,0:T(4,128)(2,1)S(1)}, bf16[3,256]{1,0:T(4,128)(2,1)}, u32[]{:S(2)}) copy-start(bf16[3,256]{1,0:T(4,128)(2,1)} %param.24) | copy-start | bytes 4612
  12.4 64.6 %copy-start.29 = (bf16[1024]{0:T(1024)(128)(2,1)S(1)}, bf16[1024]{0:T(1024)(128)(2,1)}, u32[]{:S(2)}) copy-start(bf16[1024]{0:T(1024)(128)(2,1)} %param.27) | copy-start | bytes 6148
  12.4 131.3 %copy-start.25 = (s32[2047]{0:T(1024)S(1)}, s32[2047]{0:T(1024)}, u32[]{:S(2)}) copy-start(s32[2047]{0:T(1024)} %param.19) | copy-start | bytes 24568
  12.4 131.5 %copy-start.19 = (bf16[6,1024]{1,0:T(8,128)(2,1)S(1)}, bf16[6,1024]{1,0:T(8,128)(2,1)}, u32[]{:S(2)}) copy-start(bf16[6,1024]{1,0:T(8,128)(2,1)} %param.29) | copy-start | bytes 36868
  12.5 131.5 %copy-start.30 = (s32[32]{0:T(128)S(1)}, s32[32]{0:T(128)}, u32[]{:S(2)}) copy-start(s32[32]{0:T(128)} %param.17) | copy-start | bytes 388
  12.5 131.5 %copy-start.31 = (s32[32]{0:T(128)S(1)}, s32[32]{0:T(128)}, u32[]{:S(2)}) copy-start(s32[32]{0:T(128)} %param.18) | copy-start | bytes 388
  72.4 90.6 %all-to-all-start.2 = ((bf16[32,128,256]{2,1,0:T(8,128)(2,1)}), bf16[32,128,256]{2,1,0:T(8,128)(2,1)S(1)}, u32[]{:S(2)}, u32[]{:S(2)}) async-start(bf16[32,128,256]{2,1,0:T(8,128)(2,1)} %param.16), calls=%async_computation.2 | async-start | bytes 4194304 | tf_op jit(solution)/shard_map/all_to_all | solution.py:255
  76.9 571.1 %reduce-scatter.16.cloned.1.call-start = ((), (), s32[]{:S(2)}) async-start(), calls=%async_computation.16 | async-start | bytes 2359296 | tf_op jit(solution)/shard_map/reduce_scatter | solution.py:269
  144.7 174.4 %copy-start.26 = (f32[1,1024]{1,0:T(1,128)}, f32[1,1024]{1,0:T(1,128)S(1)}, u32[]{:S(2)}) copy-start(f32[1,1024]{1,0:T(1,128)S(1)} %get-tuple-element.61) | copy-start | bytes 12292
  149.6 56.0 %copy-start.5 = (bf16[512,1024,1]{1,0,2:T(8,128)(2,1)}, bf16[512,1024,1]{1,0,2:T(8,128)(2,1)S(1)}, u32[]{:S(2)}) copy-start(bf16[512,1024,1]{1,0,2:T(8,128)(2,1)S(1)} %reshape.253) | copy-start | bytes 3145732
  168.0 6.4 copy-start.12
  292.7 8.0 copy-start.2
  300.7 18.4 %copy-start.4 = (f32[1024,1024]{1,0:T(8,128)}, f32[1024,1024]{1,0:T(8,128)S(1)}, u32[]{:S(2)}) copy-start(f32[1024,1024]{1,0:T(8,128)S(1)} %get-tuple-element.67) | copy-start | bytes 12582916
  333.7 2.2 copy-start.3
  341.5 24.7 %copy-start.7 = (f32[1024,1024]{1,0:T(8,128)}, f32[1024,1024]{1,0:T(8,128)S(1)}, u32[]{:S(2)}) copy-start(f32[1024,1024]{1,0:T(8,128)S(1)} %get-tuple-element.42) | copy-start | bytes 12582916
  386.6 4.3 copy-start.18
  390.9 2.4 copy-start.8
  396.5 293.3 %reduce-scatter.10.cloned.1.call-start = ((), (), s32[]{:S(2)}) async-start(), calls=%async_computation.13 | async-start | bytes 1081344 | tf_op jit(solution)/shard_map/reduce_scatter | solution.py:348
  529.3 14.2 %copy-start.9 = (bf16[512,1024]{0,1:T(8,128)(2,1)}, bf16[512,1024]{0,1:T(8,128)(2,1)S(1)}, u32[]{:S(2)}) copy-start(bf16[512,1024]{0,1:T(8,128)(2,1)S(1)} %copy.207) | copy-start | bytes 3145732
  535.2 11.2 %copy-start.11 = (bf16[512,1024]{0,1:T(8,128)(2,1)}, bf16[512,1024]{0,1:T(8,128)(2,1)S(1)}, u32[]{:S(2)}) copy-start(bf16[512,1024]{0,1:T(8,128)(2,1)S(1)} %copy.208) | copy-start | bytes 3145732
  546.4 4.1 copy-start.13
  546.4 4.1 copy-start.16
  550.4 4.0 copy-start.14
  554.1 206.8 %reduce-scatter.12.cloned.1.call-start = ((), (), s32[]{:S(2)}) async-start(), calls=%async_computation.14 | async-start | bytes 7077888 | tf_op jit(solution)/shard_map/reduce_scatter | solution.py:269
  564.3 4.9 copy-start.6
  576.2 4.7 copy-start.10
  591.3 262.2 %reduce-scatter.24.cloned.1.call-start = ((), (), s32[]{:S(2)}) async-start(), calls=%async_computation.20 | async-start | bytes 9437184 | tf_op jit(solution)/shard_map/reduce_scatter | solution.py:269
  616.6 0.7 copy-start.27
  616.6 311.6 %reduce-scatter.20.cloned.1.call-start = ((), (), s32[]{:S(2)}) async-start(), calls=%async_computation.18 | async-start | bytes 9437184 | tf_op jit(solution)/shard_map/reduce_scatter | solution.py:269
  647.9 321.2 %reduce-scatter.18.cloned.1.call-start = ((), (), s32[]{:S(2)}) async-start(), calls=%async_computation.17 | async-start | bytes 327680 | tf_op jit(solution)/shard_map/reduce_scatter | solution.py:270
  648.6 359.8 %all-gather.17.cloned.1.call-start = ((), (), s32[]{:S(2)}) async-start(), calls=%async_computation.25 | async-start | bytes 2162688 | tf_op jit(solution)/shard_map/all_gather | solution.py:351
  696.2 82.8 %all-to-all-start.1 = ((bf16[32,128,256]{2,1,0:T(8,128)(2,1)}), bf16[32,128,256]{2,1,0:T(8,128)(2,1)S(1)}, u32[]{:S(2)}, u32[]{:S(2)}) async-start(bf16[32,128,256]{2,1,0:T(8,128)(2,1)} %bitcast.225), calls=%async_computation.1 | async-start | bytes 4194304 | tf_op jit(solution)/shard_map/all_to_all | solution.py:260
  698.9 334.0 %reduce-scatter.14.cloned.1.call-start = ((), (), s32[]{:S(2)}) async-start(), calls=%async_computation.15 | async-start | bytes 983040 | tf_op jit(solution)/shard_map/reduce_scatter | solution.py:270
  699.2 7.5 copy-start.17
  779.0 149.4 %copy-start.23 = (f32[4,256]{1,0:T(4,128)S(1)}, f32[4,256]{1,0:T(4,128)}, u32[]{:S(2)}) copy-start(f32[4,256]{1,0:T(4,128)} %get-tuple-element.35) | copy-start | bytes 12292
  779.0 149.4 %copy-start.24 = (f32[4,1024]{1,0:T(4,128)S(1)}, f32[4,1024]{1,0:T(4,128)}, u32[]{:S(2)}) copy-start(f32[4,1024]{1,0:T(4,128)} %get-tuple-element.45) | copy-start | bytes 49156
  779.0 149.4 %copy-start.21 = (f32[1024]{0:T(1024)S(1)}, f32[1024]{0:T(1024)}, u32[]{:S(2)}) copy-start(f32[1024]{0:T(1024)} %get-tuple-element.30) | copy-start | bytes 12292
  779.0 149.4 %copy-start.22 = (f32[1024]{0:T(1024)S(1)}, f32[1024]{0:T(1024)}, u32[]{:S(2)}) copy-start(f32[1024]{0:T(1024)} %get-tuple-element.41) | copy-start | bytes 12292
  779.0 149.4 %copy-start.20 = (f32[24,1024]{1,0:T(8,128)S(1)}, f32[24,1024]{1,0:T(8,128)}, u32[]{:S(2)}) copy-start(f32[24,1024]{1,0:T(8,128)} %get-tuple-element.29) | copy-start | bytes 294916
  779.0 191.6 %all-to-all-start.3 = ((bf16[32,128,256]{2,1,0:T(8,128)(2,1)}), bf16[32,128,256]{2,1,0:T(8,128)(2,1)}, u32[]{:S(2)}, u32[]{:S(2)}) async-start(bf16[32,128,256]{2,1,0:T(8,128)(2,1)} %bitcast.223), calls=%async_computation.3 | async-start | bytes 4194304 | tf_op jit(solution)/shard_map/all_to_all | solution.py:260
  784.1 277.4 %reduce-scatter.26.cloned.1.call-start = ((), (), s32[]{:S(2)}) async-start(), calls=%async_computation.21 | async-start | bytes 1310720 | tf_op jit(solution)/shard_map/reduce_scatter | solution.py:270
  853.5 236.3 %reduce-scatter.22.cloned.1.call-start = ((), (), s32[]{:S(2)}) async-start(), calls=%async_computation.19 | async-start | bytes 1310720 | tf_op jit(solution)/shard_map/reduce_scatter | solution.py:270
  1091.5 4.6 copy-start.15
  1091.5 5.9 copy-start.1
Sparse Core Ops, SparseCore 0:
  11.5 62.2 all-gather.12
  77.2 83.0 all-gather.10
  163.2 123.1 all-gather.14
  396.6 41.3 reduce-scatter.15
  554.3 135.4 reduce-scatter.9
  693.0 67.9 reduce-scatter.11
  764.8 88.6 reduce-scatter.23
  856.9 71.2 reduce-scatter.19
  930.6 19.7 reduce-scatter.17
  953.7 54.6 all-gather.16
  1010.8 22.1 reduce-scatter.13
  1035.1 26.4 reduce-scatter.25
  1063.9 25.7 reduce-scatter.21

commit v2 on v1

--- a/solution.py
+++ b/solution.py
@@ -102,19 +102,34 @@
         return 0
     lax.fori_loop(0, nb, sblock, 0, unroll=8)
 
-def attn_fwd(length, q, k, v, kf, qf, *, scale):
-    L, C = q.shape
-    col = lambda r: pl.BlockSpec((r,128), lambda h, *_: (0,h))
+
+def attn_fwd(length, qkv, far, *, scale):
+    _, L, C = qkv.shape
+    part = lambda j, r: pl.BlockSpec((None, r, 128), lambda h, *_: (j, 0, h))
     return pl.pallas_call(
         functools.partial(fwd_kernel, L=L, scale=scale),
-        grid_spec=pltpu.PrefetchScalarGridSpec(num_scalar_prefetch=1, grid=(C//128,),
-            in_specs=[col(L),col(L),col(L),col(2*L),col(2*L)],
-            out_specs=[col(L), pl.BlockSpec((2,L,L), lambda h,*_: (h,0,0)), col(L)],
-            scratch_shapes=[pltpu.VMEM((2,L,L),jnp.bfloat16), pltpu.VMEM((2,L,128),jnp.bfloat16), pltpu.VMEM((2,L,128),jnp.bfloat16)]
-              +[pltpu.VMEM((B,L+B),jnp.float32)]*2+[pltpu.VMEM((B,L),jnp.float32)]*2),
-        out_shape=[jax.ShapeDtypeStruct((L,C),jnp.bfloat16), jax.ShapeDtypeStruct((C//64,L,L),jnp.bfloat16), jax.ShapeDtypeStruct((L,C),jnp.float32)],
-        compiler_params=pltpu.CompilerParams(vmem_limit_bytes=50<<20),
-    )(length, q, k, v, kf, qf)
+        grid_spec=pltpu.PrefetchScalarGridSpec(
+            num_scalar_prefetch=1,
+            grid=(C // 128,),
+            in_specs=[part(0, L), part(1, L), part(2, L), part(1, 2 * L), part(0, 2 * L)],
+            out_specs=[
+                pl.BlockSpec((L, 128), lambda h, *_: (0, h)),
+                pl.BlockSpec((2, L, L), lambda h, *_: (h, 0, 0)),
+                pl.BlockSpec((L, 128), lambda h, *_: (0, h)),
+            ],
+            scratch_shapes=[pltpu.VMEM((2, L, L), jnp.bfloat16)]
+            + [pltpu.VMEM((2, L, 128), jnp.bfloat16)] * 2
+            + [pltpu.VMEM((B, L + B), jnp.float32)] * 2
+            + [pltpu.VMEM((B, L), jnp.float32)] * 2,
+        ),
+        out_shape=[
+            jax.ShapeDtypeStruct((L, C), jnp.bfloat16),
+            jax.ShapeDtypeStruct((C // HEAD, L, L), jnp.bfloat16),
+            jax.ShapeDtypeStruct((L, C), jnp.float32),
+        ],
+        compiler_params=pltpu.CompilerParams(vmem_limit_bytes=50 << 20),
+        cost_estimate=pl.CostEstimate(flops=80 * 10**9, bytes_accessed=60 * 10**6, transcendentals=0),
+    )(length, qkv, qkv, qkv, far, far)
 
 
 def unskew(x, a8):
@@ -191,24 +206,40 @@
     dkf_ref[...] = (akf[...]*scale).astype(jnp.bfloat16)
     dqf_ref[...] = (aqf[...]*scale).astype(jnp.bfloat16)
 
-def attn_bwd(p, q, k, v, do, ctx, linv, kf, qf, *, scale):
-    L, C = q.shape
-    col = lambda r: pl.BlockSpec((r,128), lambda h: (0,h))
-    rowb = pl.BlockSpec((128,2*L), lambda h: (h,0))
-    bf=jnp.bfloat16
+
+def attn_bwd(p, qkv, do, ctx, linv, far, *, scale):
+    _, L, C = qkv.shape
+    bf = jnp.bfloat16
+    part = lambda j, r: pl.BlockSpec((None, r, 128), lambda h: (j, 0, h))
+    col = lambda r: pl.BlockSpec((r, 128), lambda h: (0, h))
+    rowb = pl.BlockSpec((128, 2 * L), lambda h: (h, 0))
     return pl.pallas_call(
         functools.partial(bwd_kernel, L=L, scale=scale),
-        grid=(C//128,),
-        in_specs=[pl.BlockSpec((2,L,L), lambda h:(h,0,0))]+[col(L)]*6+[col(2*L)]*2,
-        out_specs=[col(L)]*3+[rowb]*2+[pl.BlockSpec((24,128), lambda h:(0,h))],
-        scratch_shapes=[pltpu.VMEM((2,L,128),bf), pltpu.VMEM((128,L),bf), pltpu.VMEM((128,L),bf), pltpu.VMEM((128,L),bf), pltpu.VMEM((2,L,128),bf),
-            pltpu.VMEM((2,L,L),bf), pltpu.VMEM((B,L+B),bf), pltpu.VMEM((B,L+B),bf), pltpu.VMEM((128,2*L),jnp.float32), pltpu.VMEM((128,2*L),jnp.float32)],
-        out_shape=[jax.ShapeDtypeStruct((L,C),bf)]*3+[jax.ShapeDtypeStruct((C,2*L),bf)]*2+[jax.ShapeDtypeStruct((24,C),jnp.float32)],
-        compiler_params=pltpu.CompilerParams(vmem_limit_bytes=56<<20),
-    )(p, q, k, v, do, ctx, linv, kf, qf)
-
-
-def normalize(z):
+        grid=(C // 128,),
+        in_specs=[pl.BlockSpec((2, L, L), lambda h: (h, 0, 0)), part(0, L), part(1, L), part(2, L)]
+        + [col(L)] * 3
+        + [part(1, 2 * L), part(0, 2 * L)],
+        out_specs=[col(L)] * 3 + [rowb] * 2 + [col(24)],
+        scratch_shapes=[pltpu.VMEM((2, L, 128), bf)]
+        + [pltpu.VMEM((128, L), bf)] * 3
+        + [pltpu.VMEM((2, L, 128), bf), pltpu.VMEM((2, L, L), bf)]
+        + [pltpu.VMEM((B, L + B), bf)] * 2
+        + [pltpu.VMEM((128, 2 * L), jnp.float32)] * 2,
+        out_shape=[jax.ShapeDtypeStruct((L, C), bf)] * 3
+        + [jax.ShapeDtypeStruct((C, 2 * L), bf)] * 2
+        + [jax.ShapeDtypeStruct((24, C), jnp.float32)],
+        compiler_params=pltpu.CompilerParams(vmem_limit_bytes=56 << 20),
+        cost_estimate=pl.CostEstimate(flops=120 * 10**9, bytes_accessed=80 * 10**6, transcendentals=0),
+    )(p, qkv, qkv, qkv, do, ctx, linv, far, far)
+
+
+def spec(block, index, once=False):
+    if once:
+        return pl.BlockSpec(block, index, pipeline_mode=pl.Buffered(1))
+    return pl.BlockSpec(block, index)
+
+
+def norm_rows(z):
     center = z - jnp.mean(z, axis=-1, keepdims=True)
     r = lax.rsqrt(jnp.mean(center * center, axis=-1, keepdims=True) + EPSILON)
     return center * r, r
@@ -218,8 +249,581 @@
     return r * (g - jnp.mean(g, axis=-1, keepdims=True) - n * jnp.mean(g * n, axis=-1, keepdims=True))
 
 
-def mm(spec, a, b):
-    return jnp.einsum(spec, a, b, preferred_element_type=jnp.float32)
+def fold8(v):
+    return jnp.sum(v.reshape(v.shape[0] // 8, 8, v.shape[1]), axis=0)
+
+
+def project_kernel(xd_ref, rel4_ref, w_ref, sh_ref, pl_ref, qkv_ref, far_ref, x_ref, rel_ref, hot_ref):
+    t, j = pl.program_id(0), pl.program_id(1)
+    gn, tn, lg, dt = xd_ref.shape
+    spans = rel_ref.shape[0]
+    rg = spans // gn
+
+    @pl.when((t == 0) & (j == 0))
+    def _():
+        for g in range(gn):
+            for s in range(tn):
+                x_ref[g * lg : (g + 1) * lg, s * dt : (s + 1) * dt] = xd_ref[g, s]
+                rel_ref[g * rg : (g + 1) * rg, s * dt : (s + 1) * dt] = rel4_ref[g, s]
+        rows = hot_ref.shape[0]
+        lanes = lax.broadcasted_iota(jnp.int32, (rows, spans), 1)
+        hot_ref[...] = (pl_ref[...] == lanes).astype(jnp.float32).astype(jnp.bfloat16)
+
+    w = w_ref[:, 0].reshape(x_ref.shape[1], dt)
+    shift = sh_ref[0, pl.ds(j, 1), :]
+    qkv_ref[0] = (dotnn(x_ref[...], w) + shift).astype(jnp.bfloat16)
+
+    @pl.when(j < 2)
+    def _():
+        place = (dotnn(rel_ref[...], w) + shift).astype(jnp.bfloat16)
+        far_ref[0] = dotnn(hot_ref[...], place).astype(jnp.bfloat16)
+
+
+def project(xd, first, shifts, places, per):
+    gn, tn, lg, dt = xd.shape
+    L, D = gn * lg, tn * dt
+    rg = (first.shape[2] - 3 * per - 8)
+    spans = rg * gn
+    bf = jnp.bfloat16
+    return pl.pallas_call(
+        project_kernel,
+        grid=(tn, 3),
+        in_specs=[
+            spec((gn, tn, lg, dt), lambda t, j: (0, 0, 0, 0), True),
+            spec((gn, tn, rg, dt), lambda t, j: (0, 0, 3 * per // rg, 0), True),
+            spec((gn, 1, per, dt), lambda t, j: (0, t, j, 0)),
+            spec((1, 3, dt), lambda t, j: (t, 0, 0)),
+            spec((2 * L, 1), lambda t, j: (0, 0), True),
+        ],
+        out_specs=[
+            spec((1, L, dt), lambda t, j: (j, 0, t)),
+            spec((1, 2 * L, dt), lambda t, j: (jnp.minimum(j, 1), 0, t)),
+            spec((L, D), lambda t, j: (0, 0)),
+            spec((spans, D), lambda t, j: (0, 0)),
+            spec((2 * L, spans), lambda t, j: (0, 0)),
+        ],
+        out_shape=[
+            jax.ShapeDtypeStruct((3, L, D), bf),
+            jax.ShapeDtypeStruct((2, 2 * L, D), bf),
+            jax.ShapeDtypeStruct((L, D), bf),
+            jax.ShapeDtypeStruct((spans, D), bf),
+            jax.ShapeDtypeStruct((2 * L, spans), bf),
+        ],
+        compiler_params=pltpu.CompilerParams(vmem_limit_bytes=50 << 20),
+        cost_estimate=pl.CostEstimate(flops=14 * 10**9, bytes_accessed=30 * 10**6, transcendentals=0),
+    )(xd, first, first, shifts, places)
+
+
+RB = 256
+
+
+def middle_kernel(ctx_ref, x_ref, wm_ref, wi_ref, wo_ref, hb_ref, vec_ref, cot_ref,
+                  hl_ref, n1_ref, r1_ref, act_ref, slope_ref, y_ref, df_ref, sums_ref, acc_ref, h1_ref):
+    t = pl.program_id(0)
+    L, D = x_ref.shape
+    gn, tn, lg, dt = cot_ref.shape
+    f32, bf = jnp.float32, jnp.bfloat16
+
+    @pl.when(t == 0)
+    def _():
+        for r in range(0, L, RB):
+            z1 = vec_ref[0:1] + x_ref[r : r + RB].astype(f32)
+            for s in range(tn):
+                z1 = z1 + dotnt(ctx_ref[r : r + RB, s * dt : (s + 1) * dt], wm_ref[s].reshape(D, dt))
+            n1, r1 = norm_rows(z1)
+            h1 = n1 * vec_ref[1:2] + vec_ref[2:3]
+            h1_ref[r : r + RB] = h1
+            hl_ref[r : r + RB] = h1.astype(bf)
+            n1_ref[r : r + RB] = n1.astype(bf)
+            r1_ref[r : r + RB] = jnp.broadcast_to(r1, (RB, 128))
+
+    wi = wi_ref[0].reshape(D, wi_ref.shape[3])
+    wo = wo_ref[0].reshape(D, wo_ref.shape[3])
+    for r in range(0, L, RB):
+        pre = dotnn(hl_ref[r : r + RB], wi) + hb_ref[0]
+        phi = 0.5 + 0.5 * lax.erf(pre * math.sqrt(0.5))
+        act = (pre * phi).astype(bf)
+        act_ref[r : r + RB] = act
+        bell = jnp.exp(-0.5 * pre * pre) * (1.0 / math.sqrt(2.0 * math.pi))
+        slope_ref[r : r + RB] = (phi + pre * bell).astype(bf)
+        part = dotnt(act, wo)
+
+        @pl.when(t == 0)
+        def _():
+            acc_ref[r : r + RB] = part
+
+        @pl.when(t > 0)
+        def _():
+            acc_ref[r : r + RB] += part
+
+    @pl.when(t == pl.num_programs(0) - 1)
+    def _():
+        s0 = jnp.zeros((8, D), f32)
+        s1 = jnp.zeros((8, D), f32)
+        s2 = jnp.zeros((8, D), f32)
+        for g in range(gn):
+            rows = slice(g * lg, (g + 1) * lg)
+            z2 = acc_ref[rows] + vec_ref[3:4] + h1_ref[rows]
+            n2, r2 = norm_rows(z2)
+            y = (n2 * vec_ref[4:5] + vec_ref[5:6]).astype(bf)
+            for s in range(tn):
+                y_ref[g, s] = y[:, s * dt : (s + 1) * dt]
+            dy = jnp.concatenate([cot_ref[g, s] for s in range(tn)], axis=1).astype(f32)
+            dz2 = norm_back(dy * vec_ref[4:5], n2, r2)
+            df_ref[rows] = dz2.astype(bf)
+            s0, s1, s2 = s0 + fold8(dz2), s1 + fold8(dy * n2), s2 + fold8(dy)
+        sums_ref[0:8], sums_ref[8:16], sums_ref[16:24] = s0, s1, s2
+
+
+def middle(ctx, x, second, hidden_bias, vectors, cot, per):
+    gn, tn, lg, dt = cot.shape
+    L, D = x.shape
+    ff = hidden_bias.shape[2]
+    bf, f32 = jnp.bfloat16, jnp.float32
+    full = lambda shape: spec(shape, lambda t: (0,) * len(shape), True)
+    return pl.pallas_call(
+        middle_kernel,
+        grid=(tn,),
+        in_specs=[
+            full((L, D)),
+            full((L, D)),
+            spec((tn, gn, per, dt), lambda t: (0, 0, 0, 2 * ff // dt), True),
+            spec((1, gn, per, ff), lambda t: (t, 0, 0, 0)),
+            spec((1, gn, per, ff), lambda t: (t, 0, 0, 1)),
+            spec((1, 1, ff), lambda t: (t, 0, 0)),
+            full((6, D)),
+            full((gn, tn, lg, dt)),
+        ],
+        out_specs=[
+            full((L, D)), full((L, D)), full((L, 128)),
+            spec((L, ff), lambda t: (0, t)), spec((L, ff), lambda t: (0, t)),
+            full((gn, tn, lg, dt)), full((L, D)), full((24, D)),
+        ],
+        out_shape=[
+            jax.ShapeDtypeStruct((L, D), bf),
+            jax.ShapeDtypeStruct((L, D), bf),
+            jax.ShapeDtypeStruct((L, 128), f32),
+            jax.ShapeDtypeStruct((L, tn * ff), bf),
+            jax.ShapeDtypeStruct((L, tn * ff), bf),
+            jax.ShapeDtypeStruct((gn, tn, lg, dt), bf),
+            jax.ShapeDtypeStruct((L, D), bf),
+            jax.ShapeDtypeStruct((24, D), f32),
+        ],
+        scratch_shapes=[pltpu.VMEM((L, D), f32), pltpu.VMEM((L, D), f32)],
+        compiler_params=pltpu.CompilerParams(vmem_limit_bytes=58 << 20),
+        cost_estimate=pl.CostEstimate(flops=30 * 10**9, bytes_accessed=60 * 10**6, transcendentals=0),
+    )(ctx, x, second, second, second, hidden_bias, vectors, cot)
+
+
+def ffn_back_kernel(df_ref, hl_ref, n1_ref, r1_ref, act_ref, slope_ref, wi_ref, wo_ref, vec_ref,
+                    pay_ref, hid_ref, da_ref, sums_ref, dft_ref, hlt_ref, acc_ref, dp_ref):
+    t = pl.program_id(0)
+    L, D = df_ref.shape
+    ff = act_ref.shape[1]
+    gn, _, per, _ = pay_ref.shape
+    f32, bf = jnp.float32, jnp.bfloat16
+
+    @pl.when(t == 0)
+    def _():
+        for r in range(0, L, RB):
+            dft_ref[:, r : r + RB] = df_ref[r : r + RB].T
+            hlt_ref[:, r : r + RB] = hl_ref[r : r + RB].T
+            acc_ref[r : r + RB] = df_ref[r : r + RB].astype(f32)
+
+    wi = wi_ref[0].reshape(D, ff)
+    wo = wo_ref[0].reshape(D, ff)
+    hid = jnp.zeros((8, ff), f32)
+    for r in range(0, L, RB):
+        dpre = dotnn(df_ref[r : r + RB], wo) * slope_ref[r : r + RB].astype(f32)
+        hid = hid + fold8(dpre)
+        low = dpre.astype(bf)
+        dp_ref[r : r + RB] = low
+        acc_ref[r : r + RB] += dotnt(low, wi)
+    hid_ref[0] = hid
+    for r in range(0, D, RB):
+        og = dotnn(dft_ref[r : r + RB], act_ref[...]).astype(bf)
+        ig = dotnn(hlt_ref[r : r + RB], dp_ref[...]).astype(bf)
+        for c in range(0, RB, per):
+            pay_ref[(r + c) // per, 0, :, 0:ff] = ig[c : c + per]
+            pay_ref[(r + c) // per, 0, :, ff : 2 * ff] = og[c : c + per]
+
+    @pl.when(t == pl.num_programs(0) - 1)
+    def _():
+        s0 = jnp.zeros((8, D), f32)
+        s1 = jnp.zeros((8, D), f32)
+        s2 = jnp.zeros((8, D), f32)
+        for r in range(0, L, 128):
+            rows = slice(r, r + 128)
+            dh1 = acc_ref[rows]
+            n1 = n1_ref[rows].astype(f32)
+            dz1 = norm_back(dh1 * vec_ref[1:2], n1, r1_ref[rows, 0:1])
+            da_ref[rows] = dz1.astype(bf)
+            s0, s1, s2 = s0 + fold8(dz1), s1 + fold8(dh1 * n1), s2 + fold8(dh1)
+        sums_ref[0:8], sums_ref[8:16], sums_ref[16:24] = s0, s1, s2
+
+
+def ffn_back(dffn, h1_low, n1, r1, act, slope, second, vectors):
+    tn, gn, per, wide = second.shape
+    L, D = dffn.shape
+    ff = act.shape[1] // tn
+    bf, f32 = jnp.bfloat16, jnp.float32
+    full = lambda shape: spec(shape, lambda t: (0,) * len(shape), True)
+    return pl.pallas_call(
+        ffn_back_kernel,
+        grid=(tn,),
+        in_specs=[
+            full((L, D)), full((L, D)), full((L, D)), full((L, 128)),
+            spec((L, ff), lambda t: (0, t)), spec((L, ff), lambda t: (0, t)),
+            spec((1, gn, per, ff), lambda t: (t, 0, 0, 0)),
+            spec((1, gn, per, ff), lambda t: (t, 0, 0, 1)),
+            full((6, D)),
+        ],
+        out_specs=[
+            spec((gn, 1, per, 2 * ff), lambda t: (0, t, 0, 0)),
+            spec((1, 8, ff), lambda t: (t, 0, 0)),
+            full((L, D)), full((24, D)),
+        ],
+        out_shape=[
+            jax.ShapeDtypeStruct((gn, tn, per, wide), bf),
+            jax.ShapeDtypeStruct((tn, 8, ff), f32),
+            jax.ShapeDtypeStruct((L, D), bf),
+            jax.ShapeDtypeStruct((24, D), f32),
+        ],
+        scratch_shapes=[pltpu.VMEM((D, L), bf), pltpu.VMEM((D, L), bf), pltpu.VMEM((L, D), f32), pltpu.VMEM((L, ff), bf)],
+        compiler_params=pltpu.CompilerParams(vmem_limit_bytes=58 << 20),
+        cost_estimate=pl.CostEstimate(flops=40 * 10**9, bytes_accessed=80 * 10**6, transcendentals=0),
+    )(dffn, h1_low, n1, r1, act, slope, second, second, vectors)
+
+
+def merge_back_kernel(da_ref, ctx_ref, wm_ref, pay_in, pay_ref, dctx_ref, dat_ref):
+    t = pl.program_id(0)
+    L, D = da_ref.shape
+    gn, _, per, dt = pay_ref.shape
+
+    @pl.when(t == 0)
+    def _():
+        for r in range(0, L, RB):
+            dat_ref[:, r : r + RB] = da_ref[r : r + RB].T
+
+    dctx_ref[...] = dotnn(da_ref[...], wm_ref[0].reshape(D, dt)).astype(jnp.bfloat16)
+    pay_ref[:, 0] = dotnn(dat_ref[...], ctx_ref[...]).astype(jnp.bfloat16).reshape(gn, per, dt)
+
+
+def merge_back(dattn, ctx, second, payload):
+    tn, gn, per, wide = second.shape
+    L, D = dattn.shape
+    dt = D // tn
+    last = wide // dt - 1
+    bf = jnp.bfloat16
+    return pl.pallas_call(
+        merge_back_kernel,
+        grid=(tn,),
+        in_specs=[
+            spec((L, D), lambda t: (0, 0), True),
+            spec((L, dt), lambda t: (0, t)),
+            spec((1, gn, per, dt), lambda t: (t, 0, 0, last)),
+            pl.BlockSpec(memory_space=pl.ANY),
+        ],
+        out_specs=[
+            spec((gn, 1, per, dt), lambda t: (0, t, 0, last)),
+            spec((L, dt), lambda t: (0, t)),
+        ],
+        out_shape=[
+            jax.ShapeDtypeStruct((gn, tn, per, wide), bf),
+            jax.ShapeDtypeStruct((L, D), bf),
+        ],
+        scratch_shapes=[pltpu.VMEM((D, L), bf)],
+        input_output_aliases={3: 0},
+        compiler_params=pltpu.CompilerParams(vmem_limit_bytes=50 << 20),
+        cost_estimate=pl.CostEstimate(flops=4 * 10**9, bytes_accessed=10 * 10**6, transcendentals=0),
+    )(dattn, ctx, second, payload)
+
+
+def tail_kernel(x_ref, rel_ref, hot_ref, da_ref, dq_ref, dk_ref, dv_ref, dqf_ref, dkf_ref, sm_ref, w_ref, small_ref,
+                pay_ref, dx_ref, xt_ref, acc_ref, ra_ref, *, first_shift):
+    t = pl.program_id(0)
+    L, D = x_ref.shape
+    spans = rel_ref.shape[0]
+    gn, tn, lg, dt = dx_ref.shape
+    per = D // gn
+    rg = spans // gn
+    sr = small_ref.shape[2]
+    f32, bf = jnp.float32, jnp.bfloat16
+
+    @pl.when(t == 0)
+    def _():
+        for r in range(0, L, RB):
+            xt_ref[:, r : r + RB] = x_ref[r : r + RB].T
+            acc_ref[r : r + RB] = da_ref[r : r + RB].astype(f32)
+        for r in range(0, spans, RB):
+            xt_ref[:, L + r : L + r + RB] = rel_ref[r : r + RB].T
+        ra_ref[...] = jnp.zeros_like(ra_ref)
+
+    w = [w_ref[:, 0, j * per : (j + 1) * per, :].reshape(D, dt) for j in range(3)]
+    qp = dotnn(dqf_ref[...], hot_ref[...]).T
+    kp = dotnn(dkf_ref[...], hot_ref[...]).T
+    pos = [qp.astype(bf), kp.astype(bf)]
+    tops = [dq_ref, dk_ref, dv_ref]
+    rows = 3 * per + rg
+    pay_ref[:, t, rows : rows + sr, :] = small_ref[0].astype(bf)
+    for j in range(3):
+        total = jnp.sum(sm_ref[8 * j : 8 * j + 8], axis=0, keepdims=True)
+        if j < 2:
+            total = total + jnp.sum((qp, kp)[j], axis=0, keepdims=True)
+            both = jnp.concatenate([tops[j][...], pos[j]], axis=0)
+            grad = dotnn(xt_ref[...], both)
+            ra_ref[...] += dotnt(pos[j], w[j])
+        else:
+            grad = dotnn(xt_ref[:, 0:L], tops[j][...])
+        pay_ref[:, t, j * per : (j + 1) * per, :] = grad.astype(bf).reshape(gn, per, dt)
+        at = first_shift + j
+        pay_ref[at // sr, t, rows + at % sr : rows + at % sr + 1, :] = total.astype(bf)
+    for r in range(0, L, RB):
+        acc_ref[r : r + RB] += sum(dotnt(tops[j][r : r + RB], w[j]) for j in range(3))
+
+    @pl.when(t == pl.num_programs(0) - 1)
+    def _():
+        for g in range(gn):
+            for s in range(tn):
+                cols = slice(s * dt, (s + 1) * dt)
+                pay_ref[g, s, 3 * per : rows, :] = ra_ref[g * rg : (g + 1) * rg, cols].astype(bf)
+                dx_ref[g, s] = acc_ref[g * lg : (g + 1) * lg, cols].astype(bf)
+
+
+def tail(x, rel, hot, dattn, dq, dk, dv, dqf, dkf, sums, first, small, first_shift):
+    gn, tn, wide, dt = first.shape
+    L, D = x.shape
+    spans = rel.shape[0]
+    rows = 3 * D // gn + spans // gn + small.shape[2]
+    bf, f32 = jnp.bfloat16, jnp.float32
+    full = lambda shape: spec(shape, lambda t: (0,) * len(shape), True)
+    col = lambda: spec((L, dt), lambda t: (0, t))
+    return pl.pallas_call(
+        functools.partial(tail_kernel, first_shift=first_shift),
+        grid=(tn,),
+        in_specs=[
+            full((L, D)), full((spans, D)), full((2 * L, spans)), full((L, D)),
+            col(), col(), col(),
+            spec((dt, 2 * L), lambda t: (t, 0)), spec((dt, 2 * L), lambda t: (t, 0)),
+            spec((24, dt), lambda t: (0, t)),
+            spec((gn, 1, wide, dt), lambda t: (0, t, 0, 0)),
+            spec((1,) + small.shape[1:], lambda t: (t, 0, 0, 0)),
+        ],
+        out_specs=[full((gn, tn, rows, dt)), full((gn, tn, L // gn, dt))],
+        out_shape=[
+            jax.ShapeDtypeStruct((gn, tn, rows, dt), bf),
+            jax.ShapeDtypeStruct((gn, tn, L // gn, dt), bf),
+        ],
+        scratch_shapes=[pltpu.VMEM((D, L + spans), bf), pltpu.VMEM((L, D), f32), pltpu.VMEM((spans, D), f32)],
+        compiler_params=pltpu.CompilerParams(vmem_limit_bytes=56 << 20),
+        cost_estimate=pl.CostEstimate(flops=20 * 10**9, bytes_accessed=40 * 10**6, transcendentals=0),
+    )(x, rel, hot, dattn, dq, dk, dv, dqf, dkf, sums, first, small)
+
+
+MESH = pl.DeviceIdType.MESH
+
+
+def bit_of(place, i):
+    return (place // (1 << i)) % 2
+
+
+def flipped(place, flips):
+    for i in flips:
+        place = place + (1 << i) * (1 - 2 * bit_of(place, i))
+    return place
+
+
+def subsets(bits):
+    out = [()]
+    for i in bits:
+        out += [s + (i,) for s in out]
+    return out
+
+
+def orders(bits):
+    return bits[1:] + bits[:1], bits[:0:-1] + bits[:1]
+
+
+def greet(tn, gn):
+    t, g = lax.axis_index("tensor"), lax.axis_index("dp")
+    barrier = pltpu.get_barrier_semaphore()
+    bits = list(range(gn.bit_length() - 1))
+    for d in range(1, tn):
+        pl.semaphore_signal(barrier, inc=1, device_id={"tensor": lax.rem(t + d, tn)}, device_id_type=MESH)
+    for i in bits:
+        pl.semaphore_signal(barrier, inc=1, device_id={"dp": flipped(g, (i,))}, device_id_type=MESH)
+    pl.semaphore_wait(barrier, tn - 1 + len(bits))
+
+
+def spread(src_ref, out_ref, sems, tn, gn):
+    local, send, recv = sems
+    t, g = lax.axis_index("tensor"), lax.axis_index("dp")
+    bits = list(range(gn.bit_length() - 1))
+    own = pltpu.make_async_copy(src_ref, out_ref.at[g, t], local)
+    own.start()
+    first = []
+    for d in range(1, tn):
+        c = pltpu.make_async_remote_copy(
+            src_ref, out_ref.at[g, t], send.at[d - 1], recv.at[d - 1],
+            device_id={"tensor": lax.rem(t + d, tn)}, device_id_type=MESH,
+        )
+        c.start()
+        first.append(c)
+    own.wait()
+    for c in first:
+        c.wait()
+    at = tn - 1
+    half = tn // 2
+    halves = [(0, half), (half, half)]
+    plans = orders(bits)
+    for step in range(len(bits)):
+        copies = []
+        for (lo, size), plan in zip(halves, plans):
+            for s in subsets(plan[:step]):
+                part = out_ref.at[flipped(g, s), pl.ds(lo, size)]
+                c = pltpu.make_async_remote_copy(
+                    part, part, send.at[at], recv.at[at],
+                    device_id={"dp": flipped(g, (plan[step],))}, device_id_type=MESH,
+                )
+                c.start()
+                copies.append(c)
+                at += 1
+        for c in copies:
+            c.wait()
+
+
+def spread_count(tn, gn):
+    return tn - 1 + 2 * (gn - 1)
+
+
+def gather_kernel(src_ref, out_ref, local, send, recv, *, tn, gn):
+    greet(tn, gn)
+    spread(src_ref, out_ref, (local, send, recv), tn, gn)
+
+
+def gather_all(w, tn, gn, number):
+    n = spread_count(tn, gn)
+    size = w.size * 2
+    return pl.pallas_call(
+        functools.partial(gather_kernel, tn=tn, gn=gn),
+        in_specs=[pl.BlockSpec(memory_space=pl.ANY)],
+        out_specs=pl.BlockSpec(memory_space=pl.ANY),
+        out_shape=jax.ShapeDtypeStruct((gn, tn) + w.shape, w.dtype),
+        scratch_shapes=[pltpu.SemaphoreType.DMA(()), pltpu.SemaphoreType.DMA((n,)), pltpu.SemaphoreType.DMA((n,))],
+        compiler_params=pltpu.CompilerParams(collective_id=number, has_side_effects=True),
+        cost_estimate=pl.CostEstimate(flops=0, bytes_accessed=size * tn * gn * 8, transcendentals=0),
+    )(w)
+
+
+def reduce_kernel(pay_ref, q_ref, k_ref, v_ref, rel_ref, small_ref, all_ref, acc_ref, rx_ref, rz_ref, rest_ref,
+                  local, asend, arecv, bsend, brecv, *, tn, gn, keep):
+    t, g = lax.axis_index("tensor"), lax.axis_index("dp")
+    bits = list(range(gn.bit_length() - 1))
+    f32, bf = jnp.float32, jnp.bfloat16
+    greet(tn, gn)
+    rest_bits = bits[1:]
+    masks = subsets(rest_bits)
+    index = {s: n for n, s in enumerate(masks)}
+    sends, locals_ = [], []
+    for n, s in enumerate(masks):
+        c = pltpu.make_async_remote_copy(
+            pay_ref.at[flipped(g, (0,) + s)], rx_ref.at[n], bsend.at[n], brecv.at[n],
+            device_id={"dp": flipped(g, (0,))}, device_id_type=MESH,
+        )
+        c.start()
+        sends.append(c)
+    for n, s in enumerate(masks):
+        c = pltpu.make_async_copy(pay_ref.at[flipped(g, s)], acc_ref.at[n], local.at[n])
+        c.start()
+        locals_.append(c)
+
+    def add(dst, lo, size, src_ref, slot):
+        for i in range(size):
+            acc_ref[dst, lo + i] = (acc_ref[dst, lo + i].astype(f32) + src_ref[slot, i].astype(f32)).astype(bf)
+
+    half = tn // 2
+    for n in range(len(masks)):
+        locals_[n].wait()
+        sends[n].wait()
+        for i in range(tn):
+            acc_ref[n, i] = (acc_ref[n, i].astype(f32) + rx_ref[n, i].astype(f32)).astype(bf)
+    at = len(masks)
+    plans = [rest_bits, rest_bits[::-1]]
+    base = 0
+    for step in range(len(rest_bits)):
+        flight = []
+        for lo, plan in zip((0, half), plans):
+            bit = plan[step]
+            left = [s for s in masks if not any(i in plan[: step + 1] for i in s)]
+            for s in left:
+                src = tuple(i for i in rest_bits if i in s or i == bit)
+                c = pltpu.make_async_remote_copy(
+                    acc_ref.at[index[src], pl.ds(lo, half)], rz_ref.at[base], bsend.at[at], brecv.at[at],
+                    device_id={"dp": flipped(g, (bit,))}, device_id_type=MESH,
+                )
+                c.start()
+                flight.append((c, index[s], lo, base))
+                at += 1
+                base += 1
+        for c, n, lo, slot in flight:
+            c.wait()
+            add(n, lo, half, rz_ref, slot)
+    flight = []
+    for d in range(1, tn):
+        to = lax.rem(t + d, tn)
+        c = pltpu.make_async_remote_copy(
+            acc_ref.at[0, to], rx_ref.at[len(masks), d - 1], bsend.at[at], brecv.at[at],
+            device_id={"tensor": to}, device_id_type=MESH,
+        )
+        c.start()
+        flight.append(c)
+        at += 1
+    total = acc_ref[0, t].astype(f32)
+    for d, c in enumerate(flight):
+        c.wait()
+        total = total + rx_ref[len(masks), d].astype(f32)
+    per = keep // 3
+    for j, out in enumerate((q_ref, k_ref, v_ref)):
+        out[...] = total[j * per : (j + 1) * per]
+    rest_ref[...] = total[keep:].astype(bf)
+    spread(rest_ref, all_ref, (local.at[len(masks)], asend, arecv), tn, gn)
+    dt = q_ref.shape[1]
+    rg = rel_ref.shape[0] // gn
+    for s in range(tn):
+        cols = slice(s * dt, (s + 1) * dt)
+        for i in range(gn):
+            rel_ref[i * rg : (i + 1) * rg, cols] = all_ref[i, s, :rg].astype(f32)
+        small_ref[:, cols] = all_ref[0, s, rg:].astype(f32)
+
+
+def reduce_all(pay, keep, spans, number):
+    gn, tn, rows, dt = pay.shape
+    bf, f32 = jnp.bfloat16, jnp.float32
+    n = spread_count(tn, gn)
+    m = gn // 2
+    pieces = 2 * (m - 1)
+    count = m + pieces + tn - 1
+    dma = lambda k: pltpu.SemaphoreType.DMA((k,))
+    return pl.pallas_call(
+        functools.partial(reduce_kernel, tn=tn, gn=gn, keep=keep),
+        in_specs=[pl.BlockSpec(memory_space=pl.ANY)],
+        out_specs=[pl.BlockSpec(memory_space=pltpu.VMEM)] * 5,
+        out_shape=[jax.ShapeDtypeStruct((keep // 3, dt), f32)] * 3
+        + [
+            jax.ShapeDtypeStruct((spans, tn * dt), f32),
+            jax.ShapeDtypeStruct((rows - keep - spans // gn, tn * dt), f32),
+        ],
+        scratch_shapes=[
+            pltpu.VMEM((gn, tn, rows - keep, dt), bf),
+            pltpu.VMEM((m, tn, rows, dt), bf),
+            pltpu.VMEM((m + 1, tn, rows, dt), bf),
+            pltpu.VMEM((pieces, tn // 2, rows, dt), bf),
+            pltpu.VMEM((rows - keep, dt), bf),
+            dma(m + 1), dma(n), dma(n), dma(count), dma(count),
+        ],
+        compiler_params=pltpu.CompilerParams(collective_id=number, has_side_effects=True, vmem_limit_bytes=40 << 20),
+        cost_estimate=pl.CostEstimate(flops=0, bytes_accessed=200 * 10**6, transcendentals=0),
+    )(pay)
 
 
 def shards(
@@ -244,6 +848,9 @@
     me = lax.axis_index("dp") * tn + lax.axis_index("tensor")
     count, lg, dt = inputs.shape
     L, D = lg * gn, dt * tn
+    per = query_weight.shape[0]
+    rg = rel_embed.shape[0]
+    spans = rg * gn
     assert count == tn * gn
     bf = jnp.bfloat16
     f32 = jnp.float32
@@ -251,129 +858,83 @@
     seq_axes = ("dp", "tensor")
     w_axes = ("tensor", "dp")
 
-    def deal(a):
-        a = lax.all_to_all(a, seq_axes, split_axis=0, concat_axis=0, tiled=True)
-        return a.reshape(gn, tn, lg, dt).transpose(0, 2, 1, 3).reshape(L, D)
-
-    def undeal(a):
-        a = a.reshape(gn, lg, tn, dt).transpose(0, 2, 1, 3).reshape(count, lg, dt)
+    def swap(a):
         return lax.all_to_all(a, seq_axes, split_axis=0, concat_axis=0, tiled=True)
 
     def gather(w):
-        rows, cols = w.shape
-        return lax.all_gather(w, w_axes, axis=0, tiled=False).reshape(tn, gn * rows, cols)
-
-    def scatter(g):
-        t, rows, cols = g.shape
-        g = g.astype(bf).reshape(t, gn, rows // gn, cols)
-        g = lax.psum_scatter(g, "dp", scatter_dimension=1, tiled=False)
-        return lax.psum_scatter(g, "tensor", scatter_dimension=0, tiled=False)
-
-    x = deal(inputs)
+        return lax.all_gather(w, w_axes, axis=0, tiled=False).reshape((tn, gn) + w.shape)
+
     rel_cols = lax.dynamic_slice_in_dim(rel_embed, lax.axis_index("tensor") * dt, dt, 1)
-    first = gather(jnp.concatenate([query_weight, key_weight, value_weight], axis=1))
-    rel4 = gather(rel_cols)
-    wq, wk, wv = first[:, :, :dt], first[:, :, dt : 2 * dt], first[:, :, 2 * dt :]
-    ff = inner_weight.shape[1]
+    first = gather_all(
+        jnp.concatenate(
+            [
+                query_weight,
+                key_weight,
+                value_weight,
+                rel_cols,
+                proj_shifts,
+                hidden_shift.reshape(-1, dt),
+                jnp.zeros((1, dt), bf),
+            ],
+            axis=0,
+        ),
+        tn,
+        gn,
+        0,
+    )
+    xd = swap(inputs).reshape(gn, tn, lg, dt)
     second = gather(jnp.concatenate([inner_weight, outer_weight, merge_weight], axis=1))
-    wi, wo, wm = second[:, :, :ff], second[:, :, ff : 2 * ff], second[:, :, 2 * ff :]
-    cot = deal(cotangent)
-    biases = lax.all_gather(
-        jnp.concatenate([proj_shifts.reshape(-1), hidden_shift]), "tensor", axis=0, tiled=False
-    ).astype(f32)
-    shifts = biases[:, : 3 * dt].reshape(tn, 3, dt)
-    hidden_bias = biases[:, 3 * dt :]
+    cot = swap(cotangent).reshape(gn, tn, lg, dt)
+    biases = first[0, :, 3 * per + rg :].astype(f32)
+    shifts = biases[:, :3]
+    hidden_bias = biases[:, 3:7].reshape(tn, 1, -1)
     vectors = layer_vectors.astype(f32)
     length = jnp.sum(jnp.where(dealing == me, lengths, 0)).reshape(1)
-    spans = rel4.shape[1]
-    places = jnp.concatenate([buckets[::-1], jnp.full((1,), -1, jnp.int32)])
-    onehot = (places[:, None] == jnp.arange(spans, dtype=jnp.int32)[None, :]).astype(bf)
-    rel = rel4.transpose(1, 0, 2).reshape(spans, D)
-
-    q = (mm("lk,tkc->ltc", x, wq) + shifts[:, 0]).astype(bf).reshape(L, D)
-    k = (mm("lk,tkc->ltc", x, wk) + shifts[:, 1]).astype(bf).reshape(L, D)
-    v = (mm("lk,tkc->ltc", x, wv) + shifts[:, 2]).astype(bf).reshape(L, D)
-    qpos = (mm("lk,tkc->ltc", rel, wq) + shifts[:, 0]).astype(bf).reshape(spans, D)
-    kpos = (mm("lk,tkc->ltc", rel, wk) + shifts[:, 1]).astype(bf).reshape(spans, D)
-    qf = mm("ms,sd->md", onehot, qpos).astype(bf)
-    kf = mm("ms,sd->md", onehot, kpos).astype(bf)
-    ctx, probs, inv = attn_fwd(length, q, k, v, kf, qf, scale=scale)
-    ctx4 = ctx.reshape(L, tn, dt)
-    z1 = mm("ltc,toc->lo", ctx4, wm) + vectors[0] + x.astype(f32)
-    n1, r1 = normalize(z1)
-    h1 = n1 * vectors[1] + vectors[2]
-    h1_low = h1.astype(bf)
-    pre = mm("la,tah->lth", h1_low, wi) + hidden_bias
-    phi = 0.5 + 0.5 * lax.erf(pre * math.sqrt(0.5))
-    act = (pre * phi).astype(bf)
-    slope = phi + pre * jnp.exp(-0.5 * pre * pre) * (1.0 / math.sqrt(2.0 * math.pi))
-    slope = slope.astype(bf)
-    z2 = mm("ltf,tof->lo", act, wo) + vectors[3] + h1
-    n2, r2 = normalize(z2)
-    y = n2 * vectors[4] + vectors[5]
-    out = undeal(y.astype(bf))
-    dy = cot.astype(f32)
-    dz2 = norm_back(dy * vectors[4], n2, r2)
-    dffn = dz2.astype(bf)
-    outer_part = mm("lo,ltf->tof", dffn, act)
-    dact = mm("lo,tof->ltf", dffn, wo)
-    dpre = dact * slope.astype(f32)
-    dpre_low = dpre.astype(bf)
-    hidden_sum = jnp.sum(dpre, axis=0).reshape(-1)
-    inner_part = mm("la,lth->tah", h1_low, dpre_low)
-    dh1 = dz2 + mm("lth,tah->la", dpre_low, wi)
-    dz1 = norm_back(dh1 * vectors[1], n1, r1)
-    dattn = dz1.astype(bf)
-    merge_part = mm("lo,ltc->toc", dattn, ctx4)
-    dctx = mm("lo,toc->ltc", dattn, wm).astype(bf).reshape(L, D)
-    outer_grad = scatter(outer_part)
-    inner_grad = scatter(inner_part)
-    merge_grad = scatter(merge_part)
-    dq, dk, dv, dkf, dqf, sums = attn_bwd(probs, q, k, v, dctx, ctx, inv, kf, qf, scale=scale)
-    dkpos = mm("dm,ms->sd", dkf, onehot)
-    dqpos = mm("dm,ms->sd", dqf, onehot)
-    sums = sums.reshape(3, 8, D).sum(axis=1)
-    shift_sum = sums + jnp.stack(
-        [jnp.sum(dqpos, axis=0), jnp.sum(dkpos, axis=0), jnp.zeros((D,), f32)]
+    places = jnp.concatenate([buckets[::-1], jnp.full((1,), -1, jnp.int32)])[:, None]
+
+    qkv, far, x, rel, hot = project(xd, first, shifts, places, per)
+    ctx, probs, inv = attn_fwd(length, qkv, far, scale=scale)
+    h1_low, n1, r1, act, slope, y, dffn, sums2 = middle(
+        ctx, x, second, hidden_bias, vectors, cot, per
     )
-    dq4, dk4, dv4 = (a.reshape(L, tn, dt) for a in (dq, dk, dv))
-    dqp4, dkp4 = (a.astype(bf).reshape(spans, tn, dt) for a in (dqpos, dkpos))
-    dx = dz1 + mm("ltj,tej->le", dq4, wq) + mm("ltj,tej->le", dk4, wk) + mm("ltj,tej->le", dv4, wv)
-    grad_in = undeal(dx.astype(bf))
-    query_part = mm("le,ltj->tej", x, dq4) + mm("se,stj->tej", rel, dqp4)
-    key_part = mm("le,ltj->tej", x, dk4) + mm("se,stj->tej", rel, dkp4)
-    value_part = mm("le,ltj->tej", x, dv4)
-    rel_part = mm("stj,tej->se", dqp4, wq) + mm("stj,tej->se", dkp4, wk)
-    qkv = scatter(jnp.concatenate([query_part, key_part, value_part], axis=2)).astype(f32)
-    rel_mine = lax.psum_scatter(
-        rel_part.astype(bf).reshape(count, spans // count, D), seq_axes, scatter_dimension=0, tiled=False
+    out = swap(y.reshape(count, lg, dt))
+    payload, hidden, dattn, sums1 = ffn_back(dffn, h1_low, n1, r1, act, slope, second, vectors)
+    payload, dctx = merge_back(dattn, ctx, second, payload)
+    wide_grads = lax.psum_scatter(payload, "dp", scatter_dimension=0, tiled=False)
+    dq, dk, dv, dkf, dqf, sums = attn_bwd(probs, qkv, dctx, ctx, inv, far, scale=scale)
+    dq, out, wide_grads = lax.optimization_barrier((dq, out, wide_grads))
+    wide_grads = lax.psum_scatter(wide_grads, "tensor", scatter_dimension=0, tiled=False)
+    ff = hidden.shape[2]
+    small = jnp.concatenate(
+        [
+            jnp.sum(sums1.reshape(3, 8, D), axis=1),
+            jnp.sum(sums2.reshape(3, 8, D), axis=1),
+            jnp.sum(hidden, axis=1).reshape(-1, D),
+        ],
+        axis=0,
     )
-    rel_grad = lax.all_gather(rel_mine.astype(f32), seq_axes, axis=0, tiled=True)
-    vector_sum = jnp.stack(
-        [
-            jnp.sum(dz1, axis=0),
-            jnp.sum(dh1 * n1, axis=0),
-            jnp.sum(dh1, axis=0),
-            jnp.sum(dz2, axis=0),
-            jnp.sum(dy * n2, axis=0),
-            jnp.sum(dy, axis=0),
-        ]
-    )
-    hidden_sum, vector_sum = lax.psum((hidden_sum, vector_sum), seq_axes)
-    shift_sum = lax.psum(shift_sum, seq_axes)
+    first_shift = small.shape[0]
+    sr = 16
+    small = jnp.pad(small, ((0, sr - first_shift), (0, 0)))
+    small = small.reshape(sr, tn, dt).transpose(1, 0, 2)[:, None]
+    small = jnp.pad(small, ((0, 0), (0, gn - 1), (0, 0), (0, 0)))
+    pay, dx = tail(x, rel, hot, dattn, dq, dk, dv, dqf, dkf, sums, first, small, first_shift)
+    grad_in = swap(dx.reshape(count, lg, dt))
+    wide_grads = wide_grads.astype(f32)
+    query_grad, key_grad, value_grad, rel_grad, rest = reduce_all(pay, 3 * per, spans, 1)
     return (
         out,
         grad_in,
         rel_grad,
-        qkv[:, :dt],
-        qkv[:, dt : 2 * dt],
-        qkv[:, 2 * dt :],
-        shift_sum,
-        merge_grad.astype(f32),
-        inner_grad.astype(f32),
-        hidden_sum,
-        outer_grad.astype(f32),
-        vector_sum,
+        query_grad,
+        key_grad,
+        value_grad,
+        rest[first_shift : first_shift + 3],
+        wide_grads[:, 2 * ff :],
+        wide_grads[:, :ff],
+        rest[6:first_shift].reshape(-1),
+        wide_grads[:, ff : 2 * ff],
+        rest[:6],
     )
 
 

time: 1110 us -> 708 us (0.64)
  Pallas kernels: 196 us -> 626 us
  waiting for transfers between devices: 350 us -> 3.6 us
  matrix products: 219 us -> 0 us
  blocking collectives: 167 us -> 0 us
  local copies, waits for them, and re-layouts: 108 us -> 23.5 us
  other arithmetic: 35.6 us -> 5.44 us
  starting transfers between devices: 14 us -> 27 us
    pallas_call x0 -> x7, Pallas kernels: none -> 430 us  [the longest x1 170 us: gather_all(): pl.pallas_call(functools.partial(gather_kernel, tn=tn, gn=gn), in_specs=[...]
    reduce_scatter x9 -> x2, waiting for transfers between devices: 311 us -> 3.54 us  [the longest x1 3.54 us: shards(): lax.psum_scatter(payload, 'dp', scatter_dimension=0, tiled=False)]
    dot_general x28 -> x0, matrix products: 219 us -> none  [mm(): return jnp.einsum(spec, a, b, preferred_element_type=jnp.float32)]
    reshape x20 -> x3, local copies, waits for them, and re-layouts: 72.3 us -> 0.65 us  [the longest x1 0.64 us: shards(): hidden_bias = biases[:, 3:7].reshape(tn, 1, -1)]
    all_gather x1 -> x0, blocking collectives: 66.7 us -> none  [shards(): lax.all_gather(jnp.concatenate([proj_shifts.reshape(-1), hidden_shift]),...]
    all_to_all x1 -> x0, blocking collectives: 59.9 us -> none  [deal(): a = lax.all_to_all(a, seq_axes, split_axis=0, concat_axis=0, tiled=True)]
    psum x1 -> x0, blocking collectives: 40.6 us -> none  [shards(): shift_sum = lax.psum(shift_sum, seq_axes)]
    all_gather x4 -> x1, waiting for transfers between devices: 37.9 us -> 0.01 us  [gather(): lax.all_gather(w, w_axes, axis=0, tiled=False).reshape((tn, gn) + w.shape)]
  transfers between devices with their start and end apart: 16 -> 7, of which waited for: 8 -> 1; matrix products, arithmetic and copies ran while one was open for 23% -> 1% of each run, Pallas kernels for 18% -> 75%
where the time goes in v2:
time: 708 us; the launch traced here: 700 us
  Pallas kernels  626 us (88%)
  starting transfers between devices  27 us (4%)
  local copies, waits for them, and re-layouts  23.5 us (3%)
  between operations  14.3 us (2%)
    pallas_call x1, Pallas kernels, gather_all(): pl.pallas_call(functools.partial(gather_kernel, tn=tn, gn=gn), in_specs=[...  170 us
    pallas_call x1, Pallas kernels, attn_bwd(): pl.pallas_call(functools.partial(bwd_kernel, L=L, scale=scale), grid=(C /...  120 us
    pallas_call x1, Pallas kernels, reduce_all(): pl.pallas_call(functools.partial(reduce_kernel, tn=tn, gn=gn, keep=keep),...  98.9 us
    pallas_call x1, Pallas kernels, attn_fwd(): pl.pallas_call(functools.partial(fwd_kernel, L=L, scale=scale), grid_spec...  76.1 us
    pallas_call x1, Pallas kernels, ffn_back(): pl.pallas_call(ffn_back_kernel, grid=(tn,), in_specs=[full((L, D)), full(...  48.6 us
    pallas_call x1, Pallas kernels, middle(): pl.pallas_call(middle_kernel, grid=(tn,), in_specs=[full((L, D)), full((L...  41.7 us
    pallas_call x1, Pallas kernels, tail(): pl.pallas_call(functools.partial(tail_kernel, first_shift=first_shift), g...  32.7 us
    pallas_call x1, Pallas kernels, project(): pl.pallas_call(project_kernel, grid=(tn, 3), in_specs=[spec((gn, tn, lg,...  28.4 us
  transfers between devices with their start and end apart: 7, of which 1 were waited for; matrix products, arithmetic and copies ran while one was open for 1% of the time, Pallas kernels for 75%

profile of v2, /device:TPU:0, one launch (start us, length us, event | category | flops | bytes accessed | tf_op | source)
XLA Modules:
  0.0 699.6 jit_solution(13109533249849579815)
XLA Ops:
  7.2 0.0 copy-start
  7.2 0.0 all-gather.3.cloned.1.call-start
  7.2 1.9 pad_maximum_fusion
  9.2 0.0 all-gather.3.cloned.1.call-update
  9.2 0.0 copy-start.18
  9.2 0.0 copy-start.12
  9.2 0.0 copy-start.13
  9.2 0.0 copy-start.14
  9.3 0.0 copy-start.17
  9.3 7.3 %all-to-all-start = ((bf16[32,128,256]{2,1,0:T(8,128)(2,1)}), bf16[32,128,256]{2,1,0:T(8,128)(2,1)S(1)}, u32[]{:S(2)}, u32[]{:S(2)}) async-start(bf16[32,128,256]{2,1,0:T(8,128)(2,1)} %param.15), calls=%async_computation | async-start | bytes 4194304 | tf_op jit(solution)/shard_map/all_to_all | solution.py:862
  16.7 3.1 concatenate.12.src_ref
  19.8 170.4 %shard_map.238.rel4_ref.w_ref = bf16[8,4,456,256]{3,2,1,0:T(8,128)(2,1)} custom-call(bf16[456,256]{1,0:T(8,128)(2,1)} %concatenate.12.src_ref), custom_call_target="tpu_custom_call" | custom-call | bytes 59768832 | tf_op jit(solution)/shard_map/pallas_call | solution.py:707
  190.2 0.7 bitcast_convert_fusion.1
  191.0 0.1 reverse
  191.1 0.1 slice.43
  191.2 0.6 convert_element_type.21.vec_ref
  191.8 0.1 pad_add_fusion
  191.9 0.4 copy.28.pl_ref
  192.2 0.6 reshape.68.hb_ref
  192.9 0.0 copy-done.19
  192.9 0.6 fusion
  193.5 0.0 all-to-all-done
  193.5 9.1 %all-to-all-start.1 = ((bf16[32,128,256]{2,1,0:T(8,128)(2,1)}), bf16[32,128,256]{2,1,0:T(8,128)(2,1)}, u32[]{:S(2)}, u32[]{:S(2)}) async-start(bf16[32,128,256]{2,1,0:T(8,128)(2,1)} %param.16), calls=%async_computation.1 | async-start | bytes 4194304 | tf_op jit(solution)/shard_map/all_to_all | solution.py:862
  202.6 0.0 reduce-scatter.3.cloned.1.call-start
  202.7 0.0 copy-done.8
  202.7 28.4 %shard_map.239 = (bf16[3,1024,1024]{2,1,0:T(8,128)(2,1)}, bf16[2,2048,1024]{2,1,0:T(8,128)(2,1)}, bf16[1024,1024]{1,0:T(8,128)(2,1)}, bf16[512,1024]{1,0:T(8,128)(2,1)S(1)}, bf16[2048,512]{1,0:T(8,128)(2,1)}) custom-call(bf16[8,4,128,256]{3,2,1,0:T(8,128)(2,1)} %bitcast.40, bf16[8,4,456,256]{3,2,1,0:T(8,128)(2,1)} %shard_map.238.rel4_ref.w_ref, ...), custom_call_target="tpu_custom_call" | custom-call | flops 14000000000 | bytes 30000000 | tf_op jit(solution)/shard_map/pallas_call | solution.py:288
  231.1 1.0 copy-done.5
  232.1 76.1 %shard_map.240 = (bf16[1024,1024]{1,0:T(8,128)(2,1)S(1)}, bf16[16,1024,1024]{2,1,0:T(8,128)(2,1)}, f32[1024,1024]{1,0:T(8,128)}) custom-call(s32[1]{0:T(128)} %bitcast.len_ref, bf16[3,1024,1024]{2,1,0:T(8,128)(2,1)} %get-tuple-element.50.q_ref.k_ref.v_ref, bf16[3,1024,1024]{2,1,0:T(8,128)(2,1)} %get-tuple-element.50.q_ref.k_ref.v_ref, ...), custom_call_target="tpu_custom_call" | custom-call | flops 80000000000 | bytes 60000000 | tf_op jit(solution)/shard_map/pallas_call | solution.py:109
  308.2 1.3 copy-done.3
  309.5 0.0 all-to-all-done.1
  309.5 41.7 %shard_map.241 = (bf16[1024,1024]{1,0:T(8,128)(2,1)}, bf16[1024,1024]{1,0:T(8,128)(2,1)}, f32[1024,128]{1,0:T(8,128)}, bf16[1024,4096]{1,0:T(8,128)(2,1)}, bf16[...) custom-call(bf16[1024,1024]{1,0:T(8,128)(2,1)} %copy-done.3, ...), custom_call_target="tpu_custom_call" | custom-call | flops 30000001024 | bytes 60000000 | tf_op jit(solution)/shard_map/pallas_call | solution.py:384
  351.2 48.6 %shard_map.242 = (bf16[8,4,128,2304]{3,2,1,0:T(8,128)(2,1)}, f32[4,8,1024]{2,1,0:T(8,128)}, bf16[1024,1024]{1,0:T(8,128)(2,1)}, f32[24,1024]{1,0:T(8,128)}) custom-call(bf16[1024,1024]{1,0:T(8,128)(2,1)} %get-tuple-element.55.df_ref, bf16[1024,1024]{1,0:T(8,128)(2,1)} %get-tuple-element.56.hl_ref, bf16[1024,1024]{1,0:T(8,128)(2,1)} %get-tuple-element.57.n1_ref, ...), custom_call_target="tpu_custom_call" | custom-call | flops 40000000000 | bytes 80000000 | tf_op jit(solution)/shard_map/pallas_call | solution.py:471
  399.9 8.9 %shard_map.243 = (bf16[8,4,128,2304]{3,2,1,0:T(8,128)(2,1)}, bf16[1024,1024]{1,0:T(8,128)(2,1)S(1)}) custom-call(bf16[1024,1024]{1,0:T(8,128)(2,1)} %get-tuple-element.61.da_ref, bf16[1024,1024]{1,0:T(8,128)(2,1)} %copy-done.3, bf16[4,8,128,2304]{3,2,1,0:T(8,128)(2,1)} %bitcast.38, ...), custom_call_target="tpu_custom_call", output_to_operand_aliasing={{0}: (3, {})} | custom-call | flops 4000000000 | bytes 10000000 | tf_op jit(solution)/shard_map/pallas_call | solution.py:518
  408.7 1.4 copy-done.4
  410.1 0.0 reduce-scatter.3.cloned.1.call-update
  410.1 5.7 all-to-all-start.2
  415.9 0.0 reduce-scatter.5.cloned.1.call-start
  415.9 0.0 copy-start.9
  415.9 0.0 copy-start.11
  415.9 0.0 copy-start.10
  416.0 120.1 %shard_map.244 = (bf16[1024,1024]{1,0:T(8,128)(2,1)}, bf16[1024,1024]{1,0:T(8,128)(2,1)}, bf16[1024,1024]{1,0:T(8,128)(2,1)}, bf16[1024,2048]{1,0:T(8,128)(2,1)}...) custom-call(bf16[16,1024,1024]{2,1,0:T(8,128)(2,1)} %get-tuple-element.52.p_ref, ...), custom_call_target="tpu_custom_call" | custom-call | flops 120000004096 | bytes 80000000 | tf_op jit(solution)/shard_map/pallas_call | solution.py:216
  536.0 0.0 copy-done.9
  536.2 0.9 pad.9.small_ref
  537.1 0.0 all-to-all-done.2
  537.1 3.5 reduce-scatter.3.cloned.1.call-done
  540.6 0.0 reduce-scatter.5.cloned.1.call-update
  540.6 32.7 %shard_map.245 = (bf16[8,4,464,256]{3,2,1,0:T(8,128)(2,1)}, bf16[8,4,128,256]{3,2,1,0:T(8,128)(2,1)}) custom-call(bf16[1024,1024]{1,0:T(8,128)(2,1)} %get-tuple-element.54.x_ref, bf16[512,1024]{1,0:T(8,128)(2,1)} %copy-done.5, bf16[2048,512]{1,0:T(8,128)(2,1)} %get-tuple-element.70.hot_ref, bf16[1024,1024]{1,0:T(8,128)(2,1)} %get-tuple-element.61.da_ref, ...), custom_call_target="tpu_custom_call" | custom-call | flops 20000000000 | bytes 40000000 | tf_op jit(solution)/shard_map/pallas_call | solution.py:601
  573.4 0.0 copy-done.6
  573.4 4.7 all-to-all-start.3
  578.1 3.1 copy-done.2
  581.3 98.9 %shard_map.246 = (f32[128,256]{1,0:T(8,128)S(1)}, f32[128,256]{1,0:T(8,128)S(1)}, f32[128,256]{1,0:T(8,128)S(1)}, f32[512,1024]{1,0:T(8,128)S(1)}, f32[16,1024]{1,0:T(8,128)S(1)}) custom-call(bf16[8,4,464,256]{3,2,1,0:T(8,128)(2,1)S(1)} %copy-done.2), custom_call_target="tpu_custom_call" | custom-call | bytes 200000000 | tf_op jit(solution)/shard_map/pallas_call | solution.py:807
  680.2 0.6 slice.30
  680.8 0.6 slice.35
  681.4 0.6 copy.35
  682.0 0.0 all-to-all-done.3
  682.0 1.3 bitcast_convert_fusion
  683.3 0.7 slice.38
  684.0 1.1 fusion.1
  685.1 1.3 copy.43
  686.4 3.2 copy.44
  689.6 1.3 copy.45
  690.9 0.7 copy.46
  691.5 0.7 copy.47
  692.2 0.7 copy.48
  (38 shorter events, 0.3 us)
Async XLA Ops:
  7.2 9.4 %copy-start = (bf16[64,1024]{1,0:T(8,128)(2,1)S(1)}, bf16[64,1024]{1,0:T(8,128)(2,1)}, u32[]{:S(2)}) copy-start(bf16[64,1024]{1,0:T(8,128)(2,1)} %param.20) | copy-start | bytes 393220
  7.2 302.3 %all-gather.3.cloned.1.call-start = ((), (), s32[]{:S(2)}) async-start(), calls=%async_computation.8 | async-start | bytes 19464192 | tf_op jit(solution)/shard_map/all_gather | solution.py:865
  9.2 7.4 %copy-start.18 = (bf16[1024]{0:T(1024)(128)(2,1)S(1)}, bf16[1024]{0:T(1024)(128)(2,1)}, u32[]{:S(2)}) copy-start(bf16[1024]{0:T(1024)(128)(2,1)} %param.27) | copy-start | bytes 6148
  9.2 7.4 %copy-start.12 = (bf16[128,256]{1,0:T(8,128)(2,1)S(1)}, bf16[128,256]{1,0:T(8,128)(2,1)}, u32[]{:S(2)}) copy-start(bf16[128,256]{1,0:T(8,128)(2,1)} %param.21) | copy-start | bytes 196612
  9.2 7.4 %copy-start.13 = (bf16[128,256]{1,0:T(8,128)(2,1)S(1)}, bf16[128,256]{1,0:T(8,128)(2,1)}, u32[]{:S(2)}) copy-start(bf16[128,256]{1,0:T(8,128)(2,1)} %param.22) | copy-start | bytes 196612
  9.2 7.4 %copy-start.14 = (bf16[128,256]{1,0:T(8,128)(2,1)S(1)}, bf16[128,256]{1,0:T(8,128)(2,1)}, u32[]{:S(2)}) copy-start(bf16[128,256]{1,0:T(8,128)(2,1)} %param.23) | copy-start | bytes 196612
  9.3 7.4 %copy-start.17 = (bf16[3,256]{1,0:T(4,128)(2,1)S(1)}, bf16[3,256]{1,0:T(4,128)(2,1)}, u32[]{:S(2)}) copy-start(bf16[3,256]{1,0:T(4,128)(2,1)} %param.24) | copy-start | bytes 4612
  9.3 184.2 %all-to-all-start = ((bf16[32,128,256]{2,1,0:T(8,128)(2,1)}), bf16[32,128,256]{2,1,0:T(8,128)(2,1)S(1)}, u32[]{:S(2)}, u32[]{:S(2)}) async-start(bf16[32,128,256]{2,1,0:T(8,128)(2,1)} %param.15), calls=%async_computation | async-start | bytes 4194304 | tf_op jit(solution)/shard_map/all_to_all | solution.py:862
  19.8 171.2 %copy-start.16 = (s32[2047]{0:T(1024)S(1)}, s32[2047]{0:T(1024)}, u32[]{:S(2)}) copy-start(s32[2047]{0:T(1024)} %param.19) | copy-start | bytes 24568
  19.8 171.3 %copy-start.15 = (bf16[6,1024]{1,0:T(8,128)(2,1)S(1)}, bf16[6,1024]{1,0:T(8,128)(2,1)}, u32[]{:S(2)}) copy-start(bf16[6,1024]{1,0:T(8,128)(2,1)} %param.29) | copy-start | bytes 36868
  19.8 173.0 %copy-start.19 = (s32[32]{0:T(128)S(1)}, s32[32]{0:T(128)}, u32[]{:S(2)}) copy-start(s32[32]{0:T(128)} %param.17) | copy-start | bytes 388
  19.8 173.0 %copy-start.20 = (s32[32]{0:T(128)S(1)}, s32[32]{0:T(128)}, u32[]{:S(2)}) copy-start(s32[32]{0:T(128)} %param.18) | copy-start | bytes 388
  193.5 9.2 %copy-start.8 = (bf16[32,128,256]{2,1,0:T(8,128)(2,1)}, bf16[32,128,256]{2,1,0:T(8,128)(2,1)S(1)}, u32[]{:S(2)}) copy-start(bf16[32,128,256]{2,1,0:T(8,128)(2,1)S(1)} %all-to-all-done) | copy-start | bytes 6291460
  193.5 116.0 %all-to-all-start.1 = ((bf16[32,128,256]{2,1,0:T(8,128)(2,1)}), bf16[32,128,256]{2,1,0:T(8,128)(2,1)}, u32[]{:S(2)}, u32[]{:S(2)}) async-start(bf16[32,128,256]{2,1,0:T(8,128)(2,1)} %param.16), calls=%async_computation.1 | async-start | bytes 4194304 | tf_op jit(solution)/shard_map/all_to_all | solution.py:862
  202.6 338.0 %reduce-scatter.3.cloned.1.call-start = ((), (), s32[]{:S(2)}) async-start(), calls=%async_computation.6 | async-start | bytes 21233664 | tf_op jit(solution)/shard_map/reduce_scatter | solution.py:903
  231.0 1.0 copy-start.5
  308.2 1.3 copy-start.3
  408.7 1.4 copy-start.4
  410.1 127.0 %all-to-all-start.2 = ((bf16[32,128,256]{2,1,0:T(8,128)(2,1)}), bf16[32,128,256]{2,1,0:T(8,128)(2,1)S(1)}, u32[]{:S(2)}, u32[]{:S(2)}) async-start(bf16[32,128,256]{2,1,0:T(8,128)(2,1)} %bitcast.41), calls=%async_computation.2 | async-start | bytes 4194304 | tf_op jit(solution)/shard_map/all_to_all | solution.py:862
  415.9 266.1 %reduce-scatter.5.cloned.1.call-start = ((), (), s32[]{:S(2)}) async-start(), calls=%async_computation.7 | async-start | bytes 2949120 | tf_op jit(solution)/shard_map/reduce_scatter | solution.py:906
  415.9 120.1 %copy-start.9 = (f32[4,8,1024]{2,1,0:T(8,128)S(1)}, f32[4,8,1024]{2,1,0:T(8,128)}, u32[]{:S(2)}) copy-start(f32[4,8,1024]{2,1,0:T(8,128)} %get-tuple-element.79) | copy-start | bytes 393220
  415.9 120.2 %copy-start.11 = (f32[24,1024]{1,0:T(8,128)S(1)}, f32[24,1024]{1,0:T(8,128)}, u32[]{:S(2)}) copy-start(f32[24,1024]{1,0:T(8,128)} %get-tuple-element.77) | copy-start | bytes 294916
  415.9 120.2 %copy-start.10 = (f32[24,1024]{1,0:T(8,128)S(1)}, f32[24,1024]{1,0:T(8,128)}, u32[]{:S(2)}) copy-start(f32[24,1024]{1,0:T(8,128)} %get-tuple-element.78) | copy-start | bytes 294916
  537.1 36.3 %copy-start.6 = (bf16[32,128,256]{2,1,0:T(8,128)(2,1)}, bf16[32,128,256]{2,1,0:T(8,128)(2,1)S(1)}, u32[]{:S(2)}) copy-start(bf16[32,128,256]{2,1,0:T(8,128)(2,1)S(1)} %all-to-all-done.2) | copy-start | bytes 6291460
  573.4 108.6 %all-to-all-start.3 = ((bf16[32,128,256]{2,1,0:T(8,128)(2,1)}), bf16[32,128,256]{2,1,0:T(8,128)(2,1)}, u32[]{:S(2)}, u32[]{:S(2)}) async-start(bf16[32,128,256]{2,1,0:T(8,128)(2,1)} %bitcast.42), calls=%async_computation.4 | async-start | bytes 4194304 | tf_op jit(solution)/shard_map/all_to_all | solution.py:862
  578.1 3.2 copy-start.2
  682.0 3.1 copy-start.7
  686.4 6.5 copy-start.1
Sparse Core Ops, SparseCore 0:
  10.9 201.2 all-gather.2
  410.2 130.3 reduce-scatter.2
  542.9 54.6 reduce-scatter.4

commit v3 on v2

--- a/solution.py
+++ b/solution.py
@@ -539,12 +539,55 @@
     )(dattn, ctx, second, payload)
 
 
-def tail_kernel(x_ref, rel_ref, hot_ref, da_ref, dq_ref, dk_ref, dv_ref, dqf_ref, dkf_ref, sm_ref, w_ref, small_ref,
-                pay_ref, dx_ref, xt_ref, acc_ref, ra_ref, *, first_shift):
+def input_back_kernel(da_ref, dq_ref, dk_ref, dv_ref, w_ref, dx_ref, acc_ref):
+    t = pl.program_id(0)
+    L, D = da_ref.shape
+    gn, tn, lg, dt = dx_ref.shape
+    per = D // gn
+
+    @pl.when(t == 0)
+    def _():
+        acc_ref[...] = da_ref[...].astype(jnp.float32)
+
+    w = [w_ref[:, 0, j * per : (j + 1) * per, :].reshape(D, dt) for j in range(3)]
+    tops = [dq_ref, dk_ref, dv_ref]
+    for r in range(0, L, RB):
+        acc_ref[r : r + RB] += sum(dotnt(tops[j][r : r + RB], w[j]) for j in range(3))
+
+    @pl.when(t == pl.num_programs(0) - 1)
+    def _():
+        for g in range(gn):
+            for s in range(tn):
+                cols = slice(s * dt, (s + 1) * dt)
+                dx_ref[g, s] = acc_ref[g * lg : (g + 1) * lg, cols].astype(jnp.bfloat16)
+
+
+def input_back(dattn, dq, dk, dv, first):
+    gn, tn, wide, dt = first.shape
+    L, D = dattn.shape
+    col = lambda: spec((L, dt), lambda t: (0, t))
+    return pl.pallas_call(
+        input_back_kernel,
+        grid=(tn,),
+        in_specs=[
+            spec((L, D), lambda t: (0, 0), True),
+            col(), col(), col(),
+            spec((gn, 1, wide, dt), lambda t: (0, t, 0, 0)),
+        ],
+        out_specs=spec((gn, tn, L // gn, dt), lambda t: (0, 0, 0, 0), True),
+        out_shape=jax.ShapeDtypeStruct((gn, tn, L // gn, dt), jnp.bfloat16),
+        scratch_shapes=[pltpu.VMEM((L, D), jnp.float32)],
+        compiler_params=pltpu.CompilerParams(vmem_limit_bytes=50 << 20),
+        cost_estimate=pl.CostEstimate(flops=7 * 10**9, bytes_accessed=20 * 10**6, transcendentals=0),
+    )(dattn, dq, dk, dv, first)
+
+
+def tail_kernel(x_ref, rel_ref, hot_ref, dq_ref, dk_ref, dv_ref, dqf_ref, dkf_ref, sm_ref, w_ref, small_ref,
+                pay_ref, xt_ref, ra_ref, *, first_shift):
     t = pl.program_id(0)
     L, D = x_ref.shape
     spans = rel_ref.shape[0]
-    gn, tn, lg, dt = dx_ref.shape
+    gn, tn, _, dt = pay_ref.shape
     per = D // gn
     rg = spans // gn
     sr = small_ref.shape[2]
@@ -554,7 +597,6 @@
     def _():
         for r in range(0, L, RB):
             xt_ref[:, r : r + RB] = x_ref[r : r + RB].T
-            acc_ref[r : r + RB] = da_ref[r : r + RB].astype(f32)
         for r in range(0, spans, RB):
             xt_ref[:, L + r : L + r + RB] = rel_ref[r : r + RB].T
         ra_ref[...] = jnp.zeros_like(ra_ref)
@@ -578,19 +620,15 @@
         pay_ref[:, t, j * per : (j + 1) * per, :] = grad.astype(bf).reshape(gn, per, dt)
         at = first_shift + j
         pay_ref[at // sr, t, rows + at % sr : rows + at % sr + 1, :] = total.astype(bf)
-    for r in range(0, L, RB):
-        acc_ref[r : r + RB] += sum(dotnt(tops[j][r : r + RB], w[j]) for j in range(3))
-
     @pl.when(t == pl.num_programs(0) - 1)
     def _():
         for g in range(gn):
             for s in range(tn):
                 cols = slice(s * dt, (s + 1) * dt)
                 pay_ref[g, s, 3 * per : rows, :] = ra_ref[g * rg : (g + 1) * rg, cols].astype(bf)
-                dx_ref[g, s] = acc_ref[g * lg : (g + 1) * lg, cols].astype(bf)
-
-
-def tail(x, rel, hot, dattn, dq, dk, dv, dqf, dkf, sums, first, small, first_shift):
+
+
+def tail(x, rel, hot, dq, dk, dv, dqf, dkf, sums, first, small, first_shift):
     gn, tn, wide, dt = first.shape
     L, D = x.shape
     spans = rel.shape[0]
@@ -602,22 +640,19 @@
         functools.partial(tail_kernel, first_shift=first_shift),
         grid=(tn,),
         in_specs=[
-            full((L, D)), full((spans, D)), full((2 * L, spans)), full((L, D)),
+            full((L, D)), full((spans, D)), full((2 * L, spans)),
             col(), col(), col(),
             spec((dt, 2 * L), lambda t: (t, 0)), spec((dt, 2 * L), lambda t: (t, 0)),
             spec((24, dt), lambda t: (0, t)),
             spec((gn, 1, wide, dt), lambda t: (0, t, 0, 0)),
             spec((1,) + small.shape[1:], lambda t: (t, 0, 0, 0)),
         ],
-        out_specs=[full((gn, tn, rows, dt)), full((gn, tn, L // gn, dt))],
-        out_shape=[
-            jax.ShapeDtypeStruct((gn, tn, rows, dt), bf),
-            jax.ShapeDtypeStruct((gn, tn, L // gn, dt), bf),
-        ],
-        scratch_shapes=[pltpu.VMEM((D, L + spans), bf), pltpu.VMEM((L, D), f32), pltpu.VMEM((spans, D), f32)],
+        out_specs=full((gn, tn, rows, dt)),
+        out_shape=jax.ShapeDtypeStruct((gn, tn, rows, dt), bf),
+        scratch_shapes=[pltpu.VMEM((D, L + spans), bf), pltpu.VMEM((spans, D), f32)],
         compiler_params=pltpu.CompilerParams(vmem_limit_bytes=56 << 20),
-        cost_estimate=pl.CostEstimate(flops=20 * 10**9, bytes_accessed=40 * 10**6, transcendentals=0),
-    )(x, rel, hot, dattn, dq, dk, dv, dqf, dkf, sums, first, small)
+        cost_estimate=pl.CostEstimate(flops=13 * 10**9, bytes_accessed=40 * 10**6, transcendentals=0),
+    )(x, rel, hot, dq, dk, dv, dqf, dkf, sums, first, small)
 
 
 MESH = pl.DeviceIdType.MESH
@@ -883,7 +918,9 @@
         0,
     )
     xd = swap(inputs).reshape(gn, tn, lg, dt)
-    second = gather(jnp.concatenate([inner_weight, outer_weight, merge_weight], axis=1))
+    wide = jnp.concatenate([inner_weight, outer_weight, merge_weight], axis=1)
+    first, xd, wide, cotangent = lax.optimization_barrier((first, xd, wide, cotangent))
+    second = gather(wide)
     cot = swap(cotangent).reshape(gn, tn, lg, dt)
     biases = first[0, :, 3 * per + rg :].astype(f32)
     shifts = biases[:, :3]
@@ -918,7 +955,9 @@
     small = jnp.pad(small, ((0, sr - first_shift), (0, 0)))
     small = small.reshape(sr, tn, dt).transpose(1, 0, 2)[:, None]
     small = jnp.pad(small, ((0, 0), (0, gn - 1), (0, 0), (0, 0)))
-    pay, dx = tail(x, rel, hot, dattn, dq, dk, dv, dqf, dkf, sums, first, small, first_shift)
+    dx = input_back(dattn, dq, dk, dv, first)
+    dx, dq = lax.optimization_barrier((dx, dq))
+    pay = tail(x, rel, hot, dq, dk, dv, dqf, dkf, sums, first, small, first_shift)
     grad_in = swap(dx.reshape(count, lg, dt))
     wide_grads = wide_grads.astype(f32)
     query_grad, key_grad, value_grad, rel_grad, rest = reduce_all(pay, 3 * per, spans, 1)

time: 708 us -> 677 us (0.956)
  Pallas kernels: 626 us -> 555 us
  waiting for transfers between devices: 3.6 us -> 47.8 us
    pallas_call x1, Pallas kernels: 170 us -> 101 us  [gather_all(): pl.pallas_call(functools.partial(gather_kernel, tn=tn, gn=gn), in_specs=[...]
    all_gather x1, waiting for transfers between devices: 0.01 us -> 43 us  [gather(): lax.all_gather(w, w_axes, axis=0, tiled=False).reshape((tn, gn) + w.shape)]
    pallas_call x0 -> x1, Pallas kernels: none -> 12.4 us  [input_back(): pl.pallas_call(input_back_kernel, grid=(tn,), in_specs=[spec((L, D), lamb...]
    pallas_call x1, Pallas kernels: 32.7 us -> 24.4 us  [tail(): pl.pallas_call(functools.partial(tail_kernel, first_shift=first_shift), g...]
    unnamed x52 -> x58, local copies, waits for them, and re-layouts: 15.5 us -> 15.5 us
  transfers between devices with their start and end apart: 7 -> 7, of which waited for: 1 -> 2; matrix products, arithmetic and copies ran while one was open for 1% -> 2% of each run, Pallas kernels for 75% -> 68%
where the time goes in v3:
time: 677 us; the launch traced here: 669 us
  Pallas kernels  555 us (82%)
  waiting for transfers between devices  47.8 us (7%)
  local copies, waits for them, and re-layouts  23.6 us (3%)
  starting transfers between devices  22.9 us (3%)
  between operations  14.4 us (2%)
    pallas_call x1, Pallas kernels, attn_bwd(): pl.pallas_call(functools.partial(bwd_kernel, L=L, scale=scale), grid=(C /...  120 us
    pallas_call x1, Pallas kernels, gather_all(): pl.pallas_call(functools.partial(gather_kernel, tn=tn, gn=gn), in_specs=[...  101 us
    pallas_call x1, Pallas kernels, reduce_all(): pl.pallas_call(functools.partial(reduce_kernel, tn=tn, gn=gn, keep=keep),...  94.1 us
    pallas_call x1, Pallas kernels, attn_fwd(): pl.pallas_call(functools.partial(fwd_kernel, L=L, scale=scale), grid_spec...  76.1 us
    pallas_call x1, Pallas kernels, ffn_back(): pl.pallas_call(ffn_back_kernel, grid=(tn,), in_specs=[full((L, D)), full(...  48.6 us
    all_gather x1, waiting for transfers between devices, gather(): lax.all_gather(w, w_axes, axis=0, tiled=False).reshape((tn, gn) + w.shape)  43 us
    pallas_call x1, Pallas kernels, middle(): pl.pallas_call(middle_kernel, grid=(tn,), in_specs=[full((L, D)), full((L...  41.7 us
    pallas_call x1, Pallas kernels, project(): pl.pallas_call(project_kernel, grid=(tn, 3), in_specs=[spec((gn, tn, lg,...  28.5 us
  transfers between devices with their start and end apart: 7, of which 2 were waited for; matrix products, arithmetic and copies ran while one was open for 2% of the time, Pallas kernels for 68%

profile of v3, /device:TPU:0, one launch (start us, length us, event | category | flops | bytes accessed | tf_op | source)
XLA Modules:
  0.0 668.7 jit_solution(10380704736602126149)
XLA Ops:
  7.2 0.0 copy-start
  7.2 0.0 copy-start.21
  7.2 7.3 %all-to-all-start = ((bf16[32,128,256]{2,1,0:T(8,128)(2,1)}), bf16[32,128,256]{2,1,0:T(8,128)(2,1)S(1)}, u32[]{:S(2)}, u32[]{:S(2)}) async-start(bf16[32,128,256]{2,1,0:T(8,128)(2,1)} %param.15), calls=%async_computation | async-start | bytes 4194304 | tf_op jit(solution)/shard_map/all_to_all | solution.py:897
  14.6 0.0 all-gather.3.cloned.1.call-start
  14.7 3.1 concatenate.12.src_ref
  17.9 0.0 copy-start.18
  17.9 100.8 %shard_map.238.rel4_ref.w_ref = bf16[8,4,456,256]{3,2,1,0:T(8,128)(2,1)} custom-call(bf16[456,256]{1,0:T(8,128)(2,1)} %concatenate.12.src_ref), custom_call_target="tpu_custom_call" | custom-call | bytes 59768832 | tf_op jit(solution)/shard_map/pallas_call | solution.py:742
  118.7 0.0 copy-start.22
  118.7 0.0 copy-start.23
  118.7 0.8 pad_maximum_fusion
  119.6 0.0 all-to-all-done
  119.6 0.0 all-gather.3.cloned.1.call-update
  119.6 0.0 copy-done.19
  119.6 0.1 reverse
  119.7 0.1 slice.43
  119.8 0.0 copy-done.18
  119.8 0.9 convert_element_type.21.vec_ref
  120.7 0.1 pad_add_fusion
  120.7 0.4 copy.28.pl_ref
  121.1 0.6 fusion
  121.8 0.7 bitcast_convert_fusion.1
  122.5 8.3 %all-to-all-start.1 = ((bf16[32,128,256]{2,1,0:T(8,128)(2,1)}), bf16[32,128,256]{2,1,0:T(8,128)(2,1)}, u32[]{:S(2)}, u32[]{:S(2)}) async-start(bf16[32,128,256]{2,1,0:T(8,128)(2,1)} %param.16), calls=%async_computation.1 | async-start | bytes 4194304 | tf_op jit(solution)/shard_map/all_to_all | solution.py:897
  130.8 0.0 reduce-scatter.3.cloned.1.call-start
  130.9 0.6 reshape.68.hb_ref
  131.5 28.5 %shard_map.239 = (bf16[3,1024,1024]{2,1,0:T(8,128)(2,1)}, bf16[2,2048,1024]{2,1,0:T(8,128)(2,1)}, bf16[1024,1024]{1,0:T(8,128)(2,1)}, bf16[512,1024]{1,0:T(8,128)(2,1)S(1)}, bf16[2048,512]{1,0:T(8,128)(2,1)}) custom-call(bf16[8,4,128,256]{3,2,1,0:T(8,128)(2,1)} %bitcast.40, bf16[8,4,456,256]{3,2,1,0:T(8,128)(2,1)} %shard_map.238.rel4_ref.w_ref, ...), custom_call_target="tpu_custom_call" | custom-call | flops 14000000000 | bytes 30000000 | tf_op jit(solution)/shard_map/pallas_call | solution.py:288
  160.0 1.0 copy-done.5
  161.0 76.1 %shard_map.240 = (bf16[1024,1024]{1,0:T(8,128)(2,1)S(1)}, bf16[16,1024,1024]{2,1,0:T(8,128)(2,1)}, f32[1024,1024]{1,0:T(8,128)}) custom-call(s32[1]{0:T(128)} %bitcast.len_ref, bf16[3,1024,1024]{2,1,0:T(8,128)(2,1)} %get-tuple-element.56.q_ref.k_ref.v_ref, bf16[3,1024,1024]{2,1,0:T(8,128)(2,1)} %get-tuple-element.56.q_ref.k_ref.v_ref, ...), custom_call_target="tpu_custom_call" | custom-call | flops 80000000000 | bytes 60000000 | tf_op jit(solution)/shard_map/pallas_call | solution.py:109
  237.2 1.3 copy-done.3
  238.5 0.0 all-to-all-done.1
  238.5 43.0 %all-gather.3.cloned.1.call-done = bf16[4096,2304]{1,0:T(8,128)(2,1)} async-done(((bf16[128,2304]{1,0:T(8,128)(2,1)}), bf16[4096,2304]{1,0:T(8,128)(2,1)}) %all-gather.3.cloned.1.call-update) | async-done | bytes 18874384 | tf_op jit(solution)/shard_map/all_gather | solution.py:900
  281.5 41.7 %shard_map.241 = (bf16[1024,1024]{1,0:T(8,128)(2,1)}, bf16[1024,1024]{1,0:T(8,128)(2,1)}, f32[1024,128]{1,0:T(8,128)}, bf16[1024,4096]{1,0:T(8,128)(2,1)}, bf16[...) custom-call(bf16[1024,1024]{1,0:T(8,128)(2,1)} %copy-done.3, ...), custom_call_target="tpu_custom_call" | custom-call | flops 30000001024 | bytes 60000000 | tf_op jit(solution)/shard_map/pallas_call | solution.py:384
  323.2 48.6 %shard_map.242 = (bf16[8,4,128,2304]{3,2,1,0:T(8,128)(2,1)}, f32[4,8,1024]{2,1,0:T(8,128)}, bf16[1024,1024]{1,0:T(8,128)(2,1)}, f32[24,1024]{1,0:T(8,128)}) custom-call(bf16[1024,1024]{1,0:T(8,128)(2,1)} %get-tuple-element.63.df_ref, bf16[1024,1024]{1,0:T(8,128)(2,1)} %get-tuple-element.64.hl_ref, bf16[1024,1024]{1,0:T(8,128)(2,1)} %get-tuple-element.65.n1_ref, ...), custom_call_target="tpu_custom_call" | custom-call | flops 40000000000 | bytes 80000000 | tf_op jit(solution)/shard_map/pallas_call | solution.py:471
  371.8 8.9 %shard_map.243 = (bf16[8,4,128,2304]{3,2,1,0:T(8,128)(2,1)}, bf16[1024,1024]{1,0:T(8,128)(2,1)S(1)}) custom-call(bf16[1024,1024]{1,0:T(8,128)(2,1)} %get-tuple-element.69.da_ref, bf16[1024,1024]{1,0:T(8,128)(2,1)} %copy-done.3, bf16[4,8,128,2304]{3,2,1,0:T(8,128)(2,1)} %bitcast.38, ...), custom_call_target="tpu_custom_call", output_to_operand_aliasing={{0}: (3, {})} | custom-call | flops 4000000000 | bytes 10000000 | tf_op jit(solution)/shard_map/pallas_call | solution.py:518
  380.7 1.4 copy-done.4
  382.1 0.0 reduce-scatter.3.cloned.1.call-update
  382.1 2.8 all-to-all-start.2
  384.9 0.0 reduce-scatter.5.cloned.1.call-start
  384.9 119.9 %shard_map.244 = (bf16[1024,1024]{1,0:T(8,128)(2,1)}, bf16[1024,1024]{1,0:T(8,128)(2,1)}, bf16[1024,1024]{1,0:T(8,128)(2,1)}, bf16[1024,2048]{1,0:T(8,128)(2,1)}...) custom-call(bf16[16,1024,1024]{2,1,0:T(8,128)(2,1)} %get-tuple-element.58.p_ref, ...), custom_call_target="tpu_custom_call" | custom-call | flops 120000004096 | bytes 80000000 | tf_op jit(solution)/shard_map/pallas_call | solution.py:216
  504.8 0.0 all-to-all-done.2
  504.8 0.0 copy-start.6
  504.8 4.8 reduce-scatter.3.cloned.1.call-done
  509.6 0.0 reduce-scatter.5.cloned.1.call-update
  509.6 12.4 %shard_map.245 = bf16[8,4,128,256]{3,2,1,0:T(8,128)(2,1)} custom-call(bf16[1024,1024]{1,0:T(8,128)(2,1)} %get-tuple-element.69.da_ref, bf16[1024,1024]{1,0:T(8,128)(2,1)} %get-tuple-element.83.dq_ref, bf16[1024,1024]{1,0:T(8,128)(2,1)} %get-tuple-element.78.dk_ref, bf16[1024,1024]{1,0:T(8,128)(2,1)} %get-tuple-element.79.dv_ref, ...), custom_call_target="tpu_custom_call" | custom-call | flops 7000000000 | bytes 20000000 | tf_op jit(solution)/shard_map/pallas_call | solution.py:569
  522.0 0.0 copy-start.13
  522.0 0.0 copy-start.12
  522.0 4.4 all-to-all-start.3
  526.5 0.0 copy-done.11
  526.7 0.9 pad.9.small_ref
  527.5 24.4 %shard_map.246.pay_ref = bf16[8,4,464,256]{3,2,1,0:T(8,128)(2,1)} custom-call(bf16[1024,1024]{1,0:T(8,128)(2,1)} %get-tuple-element.60.x_ref, bf16[512,1024]{1,0:T(8,128)(2,1)} %copy-done.5, bf16[2048,512]{1,0:T(8,128)(2,1)} %get-tuple-element.82.hot_ref, bf16[1024,1024]{1,0:T(8,128)(2,1)} %get-tuple-element.83.dq_ref, ...), custom_call_target="tpu_custom_call" | custom-call | flops 12999999488 | bytes 40000000 | tf_op jit(solution)/shard_map/pallas_call | solution.py:639
  552.0 3.2 copy-done.2
  555.2 94.1 %shard_map.247 = (f32[128,256]{1,0:T(8,128)S(1)}, f32[128,256]{1,0:T(8,128)S(1)}, f32[128,256]{1,0:T(8,128)S(1)}, f32[512,1024]{1,0:T(8,128)S(1)}, f32[16,1024]{1,0:T(8,128)S(1)}) custom-call(bf16[8,4,464,256]{3,2,1,0:T(8,128)(2,1)S(1)} %copy-done.2), custom_call_target="tpu_custom_call" | custom-call | bytes 200000000 | tf_op jit(solution)/shard_map/pallas_call | solution.py:842
  649.3 0.6 slice.30
  649.9 0.6 slice.35
  650.5 0.6 copy.35
  651.1 0.0 all-to-all-done.3
  651.1 1.3 bitcast_convert_fusion
  652.4 0.7 slice.38
  653.1 1.1 fusion.1
  654.2 1.3 copy.43
  655.5 3.2 copy.44
  658.7 1.3 copy.45
  660.0 0.7 copy.46
  660.7 0.7 copy.47
  661.3 0.7 copy.48
  (45 shorter events, 0.3 us)
Async XLA Ops:
  7.2 7.5 %copy-start = (bf16[64,1024]{1,0:T(8,128)(2,1)S(1)}, bf16[64,1024]{1,0:T(8,128)(2,1)}, u32[]{:S(2)}) copy-start(bf16[64,1024]{1,0:T(8,128)(2,1)} %param.20) | copy-start | bytes 393220
  7.2 7.4 %copy-start.21 = (bf16[1024]{0:T(1024)(128)(2,1)S(1)}, bf16[1024]{0:T(1024)(128)(2,1)}, u32[]{:S(2)}) copy-start(bf16[1024]{0:T(1024)(128)(2,1)} %param.27) | copy-start | bytes 6148
  7.2 7.5 %copy-start.20 = (bf16[3,256]{1,0:T(4,128)(2,1)S(1)}, bf16[3,256]{1,0:T(4,128)(2,1)}, u32[]{:S(2)}) copy-start(bf16[3,256]{1,0:T(4,128)(2,1)} %param.24) | copy-start | bytes 4612
  7.2 7.5 %copy-start.16 = (bf16[128,256]{1,0:T(8,128)(2,1)S(1)}, bf16[128,256]{1,0:T(8,128)(2,1)}, u32[]{:S(2)}) copy-start(bf16[128,256]{1,0:T(8,128)(2,1)} %param.23) | copy-start | bytes 196612
  7.2 7.5 %copy-start.15 = (bf16[128,256]{1,0:T(8,128)(2,1)S(1)}, bf16[128,256]{1,0:T(8,128)(2,1)}, u32[]{:S(2)}) copy-start(bf16[128,256]{1,0:T(8,128)(2,1)} %param.22) | copy-start | bytes 196612
  7.2 7.5 %copy-start.14 = (bf16[128,256]{1,0:T(8,128)(2,1)S(1)}, bf16[128,256]{1,0:T(8,128)(2,1)}, u32[]{:S(2)}) copy-start(bf16[128,256]{1,0:T(8,128)(2,1)} %param.21) | copy-start | bytes 196612
  7.2 112.4 %all-to-all-start = ((bf16[32,128,256]{2,1,0:T(8,128)(2,1)}), bf16[32,128,256]{2,1,0:T(8,128)(2,1)S(1)}, u32[]{:S(2)}, u32[]{:S(2)}) async-start(bf16[32,128,256]{2,1,0:T(8,128)(2,1)} %param.15), calls=%async_computation | async-start | bytes 4194304 | tf_op jit(solution)/shard_map/all_to_all | solution.py:897
  14.6 266.9 %all-gather.3.cloned.1.call-start = ((), (), s32[]{:S(2)}) async-start(), calls=%async_computation.8 | async-start | bytes 19464192 | tf_op jit(solution)/shard_map/all_gather | solution.py:900
  17.9 100.8 %copy-start.9 = (bf16[128,1024]{1,0:T(8,128)(2,1)S(1)}, bf16[128,1024]{1,0:T(8,128)(2,1)}, u32[]{:S(2)}) copy-start(bf16[128,1024]{1,0:T(8,128)(2,1)} %param.28) | copy-start | bytes 786436
  17.9 100.9 %copy-start.10 = (bf16[128,1024]{1,0:T(8,128)(2,1)S(1)}, bf16[128,1024]{1,0:T(8,128)(2,1)}, u32[]{:S(2)}) copy-start(bf16[128,1024]{1,0:T(8,128)(2,1)} %param.26) | copy-start | bytes 786436
  17.9 100.9 %copy-start.17 = (bf16[128,256]{1,0:T(8,128)(2,1)S(1)}, bf16[128,256]{1,0:T(8,128)(2,1)}, u32[]{:S(2)}) copy-start(bf16[128,256]{1,0:T(8,128)(2,1)} %param.25) | copy-start | bytes 196612
  17.9 101.8 %copy-start.19 = (s32[2047]{0:T(1024)S(1)}, s32[2047]{0:T(1024)}, u32[]{:S(2)}) copy-start(s32[2047]{0:T(1024)} %param.19) | copy-start | bytes 24568
  17.9 101.9 %copy-start.18 = (bf16[6,1024]{1,0:T(8,128)(2,1)S(1)}, bf16[6,1024]{1,0:T(8,128)(2,1)}, u32[]{:S(2)}) copy-start(bf16[6,1024]{1,0:T(8,128)(2,1)} %param.29) | copy-start | bytes 36868
  118.7 2.4 copy-start.22
  118.7 2.4 copy-start.23
  119.6 2.9 copy-start.8
  122.5 116.0 %all-to-all-start.1 = ((bf16[32,128,256]{2,1,0:T(8,128)(2,1)}), bf16[32,128,256]{2,1,0:T(8,128)(2,1)}, u32[]{:S(2)}, u32[]{:S(2)}) async-start(bf16[32,128,256]{2,1,0:T(8,128)(2,1)} %param.16), calls=%async_computation.1 | async-start | bytes 4194304 | tf_op jit(solution)/shard_map/all_to_all | solution.py:897
  130.8 378.8 %reduce-scatter.3.cloned.1.call-start = ((), (), s32[]{:S(2)}) async-start(), calls=%async_computation.6 | async-start | bytes 21233664 | tf_op jit(solution)/shard_map/reduce_scatter | solution.py:940
  160.0 1.0 copy-start.5
  237.2 1.3 copy-start.3
  380.7 1.4 copy-start.4
  382.1 122.7 %all-to-all-start.2 = ((bf16[32,128,256]{2,1,0:T(8,128)(2,1)}), bf16[32,128,256]{2,1,0:T(8,128)(2,1)S(1)}, u32[]{:S(2)}, u32[]{:S(2)}) async-start(bf16[32,128,256]{2,1,0:T(8,128)(2,1)} %bitcast.41), calls=%async_computation.2 | async-start | bytes 4194304 | tf_op jit(solution)/shard_map/all_to_all | solution.py:897
  384.9 266.3 %reduce-scatter.5.cloned.1.call-start = ((), (), s32[]{:S(2)}) async-start(), calls=%async_computation.7 | async-start | bytes 2949120 | tf_op jit(solution)/shard_map/reduce_scatter | solution.py:943
  504.8 17.2 %copy-start.6 = (bf16[32,128,256]{2,1,0:T(8,128)(2,1)}, bf16[32,128,256]{2,1,0:T(8,128)(2,1)S(1)}, u32[]{:S(2)}) copy-start(bf16[32,128,256]{2,1,0:T(8,128)(2,1)S(1)} %all-to-all-done.2) | copy-start | bytes 6291460
  522.0 4.5 copy-start.11
  522.0 4.5 copy-start.13
  522.0 4.5 copy-start.12
  522.0 129.1 %all-to-all-start.3 = ((bf16[32,128,256]{2,1,0:T(8,128)(2,1)}), bf16[32,128,256]{2,1,0:T(8,128)(2,1)}, u32[]{:S(2)}, u32[]{:S(2)}) async-start(bf16[32,128,256]{2,1,0:T(8,128)(2,1)} %bitcast.9), calls=%async_computation.4 | async-start | bytes 4194304 | tf_op jit(solution)/shard_map/all_to_all | solution.py:897
  552.0 3.2 copy-start.2
  651.1 3.1 copy-start.7
  655.5 6.5 copy-start.1
Sparse Core Ops, SparseCore 0:
  119.7 161.6 all-gather.2
  382.2 127.3 reduce-scatter.2
  511.9 74.9 reduce-scatter.4

commit v4 on v3

--- a/solution.py
+++ b/solution.py
@@ -253,7 +253,7 @@
     return jnp.sum(v.reshape(v.shape[0] // 8, 8, v.shape[1]), axis=0)
 
 
-def project_kernel(xd_ref, rel4_ref, w_ref, sh_ref, pl_ref, qkv_ref, far_ref, x_ref, rel_ref, hot_ref):
+def project_kernel(xd_ref, rel4_ref, wa_ref, wb_ref, sh_ref, pl_ref, qkv_ref, far_ref, x_ref, rel_ref, hot_ref):
     t, j = pl.program_id(0), pl.program_id(1)
     gn, tn, lg, dt = xd_ref.shape
     spans = rel_ref.shape[0]
@@ -269,7 +269,7 @@
         lanes = lax.broadcasted_iota(jnp.int32, (rows, spans), 1)
         hot_ref[...] = (pl_ref[...] == lanes).astype(jnp.float32).astype(jnp.bfloat16)
 
-    w = w_ref[:, 0].reshape(x_ref.shape[1], dt)
+    w = jnp.where(j < 2, wa_ref[:, 0], wb_ref[:, 0]).reshape(x_ref.shape[1], dt)
     shift = sh_ref[0, pl.ds(j, 1), :]
     qkv_ref[0] = (dotnn(x_ref[...], w) + shift).astype(jnp.bfloat16)
 
@@ -279,10 +279,10 @@
         far_ref[0] = dotnn(hot_ref[...], place).astype(jnp.bfloat16)
 
 
-def project(xd, first, shifts, places, per):
+def project(xd, first, later, shifts, places, per):
     gn, tn, lg, dt = xd.shape
     L, D = gn * lg, tn * dt
-    rg = (first.shape[2] - 3 * per - 8)
+    rg = later.shape[2] - per - 8
     spans = rg * gn
     bf = jnp.bfloat16
     return pl.pallas_call(
@@ -290,8 +290,9 @@
         grid=(tn, 3),
         in_specs=[
             spec((gn, tn, lg, dt), lambda t, j: (0, 0, 0, 0), True),
-            spec((gn, tn, rg, dt), lambda t, j: (0, 0, 3 * per // rg, 0), True),
-            spec((gn, 1, per, dt), lambda t, j: (0, t, j, 0)),
+            spec((gn, tn, rg, dt), lambda t, j: (0, 0, per // rg, 0), True),
+            spec((gn, 1, per, dt), lambda t, j: (0, t, jnp.minimum(j, 1), 0)),
+            spec((gn, 1, per, dt), lambda t, j: (0, t, 0, 0)),
             spec((1, 3, dt), lambda t, j: (t, 0, 0)),
             spec((2 * L, 1), lambda t, j: (0, 0), True),
         ],
@@ -311,143 +312,108 @@
         ],
         compiler_params=pltpu.CompilerParams(vmem_limit_bytes=50 << 20),
         cost_estimate=pl.CostEstimate(flops=14 * 10**9, bytes_accessed=30 * 10**6, transcendentals=0),
-    )(xd, first, first, shifts, places)
+    )(xd, later, first, later, shifts, places)
 
 
 RB = 256
 
 
+MB = 256
+
+
 def middle_kernel(ctx_ref, x_ref, wm_ref, wi_ref, wo_ref, hb_ref, vec_ref, cot_ref,
-                  hl_ref, n1_ref, r1_ref, act_ref, slope_ref, y_ref, df_ref, sums_ref, acc_ref, h1_ref):
-    t = pl.program_id(0)
+                  y_ref, pay_ref, hid_ref, da_ref, sums_ref,
+                  act_ref, slope_ref, hl_ref, hlt_ref, r1_ref, df_ref, acc_ref, sem):
+    step = pl.program_id(0)
     L, D = x_ref.shape
     gn, tn, lg, dt = cot_ref.shape
+    _, _, per, ff = wi_ref.shape[0], 0, wi_ref.shape[2], wi_ref.shape[3]
     f32, bf = jnp.float32, jnp.bfloat16
 
-    @pl.when(t == 0)
-    def _():
-        for r in range(0, L, RB):
-            z1 = vec_ref[0:1] + x_ref[r : r + RB].astype(f32)
+    slots = D // ff
+
+    @pl.when(step == 0)
+    def _():
+        copies = []
+        for n, src in enumerate((ctx_ref, x_ref)):
+            for u in range(slots):
+                at = n * slots + u
+                c = pltpu.make_async_copy(src.at[:, pl.ds(u * ff, ff)], slope_ref.at[1 + at], sem.at[at])
+                c.start()
+                copies.append(c)
+        for c in copies:
+            c.wait()
+        for r in range(0, L, MB):
+            rows = slice(r, r + MB)
+            z1 = jnp.concatenate([slope_ref[1 + slots + u, rows] for u in range(slots)], axis=1)
+            z1 = vec_ref[0:1] + z1.astype(f32)
             for s in range(tn):
-                z1 = z1 + dotnt(ctx_ref[r : r + RB, s * dt : (s + 1) * dt], wm_ref[s].reshape(D, dt))
+                at = s * dt % ff
+                part = slope_ref[1 + s * dt // ff, rows, at : at + dt]
+                z1 = z1 + dotnt(part, wm_ref[s].reshape(D, dt))
             n1, r1 = norm_rows(z1)
             h1 = n1 * vec_ref[1:2] + vec_ref[2:3]
-            h1_ref[r : r + RB] = h1
-            hl_ref[r : r + RB] = h1.astype(bf)
-            n1_ref[r : r + RB] = n1.astype(bf)
-            r1_ref[r : r + RB] = jnp.broadcast_to(r1, (RB, 128))
-
-    wi = wi_ref[0].reshape(D, wi_ref.shape[3])
-    wo = wo_ref[0].reshape(D, wo_ref.shape[3])
-    for r in range(0, L, RB):
-        pre = dotnn(hl_ref[r : r + RB], wi) + hb_ref[0]
-        phi = 0.5 + 0.5 * lax.erf(pre * math.sqrt(0.5))
-        act = (pre * phi).astype(bf)
-        act_ref[r : r + RB] = act
-        bell = jnp.exp(-0.5 * pre * pre) * (1.0 / math.sqrt(2.0 * math.pi))
-        slope_ref[r : r + RB] = (phi + pre * bell).astype(bf)
-        part = dotnt(act, wo)
-
-        @pl.when(t == 0)
-        def _():
-            acc_ref[r : r + RB] = part
-
-        @pl.when(t > 0)
-        def _():
-            acc_ref[r : r + RB] += part
-
-    @pl.when(t == pl.num_programs(0) - 1)
+            low = h1.astype(bf)
+            acc_ref[rows] = h1 + vec_ref[3:4]
+            hl_ref[rows] = low
+            hlt_ref[:, rows] = low.T
+            da_ref[rows] = n1.astype(bf)
+            high = r1.astype(bf).astype(f32)
+            first_lane = lax.broadcasted_iota(jnp.int32, (MB, 128), 1) == 0
+            r1_ref[rows] = jnp.where(first_lane, high, r1 - high).astype(bf)
+
+    @pl.when(step < tn)
+    def _():
+        for r in range(0, L, MB):
+            rows = slice(r, r + MB)
+            pre = dotnn(hl_ref[rows], wi_ref[0].reshape(D, ff)) + hb_ref[0]
+            phi = 0.5 + 0.5 * lax.erf(pre * math.sqrt(0.5))
+            act = (pre * phi).astype(bf)
+            act_ref[step, rows] = act
+            bell = jnp.exp(-0.5 * pre * pre) * (1.0 / math.sqrt(2.0 * math.pi))
+            slope_ref[step, rows] = (phi + pre * bell).astype(bf)
+            acc_ref[rows] += dotnt(act, wo_ref[0].reshape(D, ff))
+
+    @pl.when(step == tn - 1)
     def _():
         s0 = jnp.zeros((8, D), f32)
         s1 = jnp.zeros((8, D), f32)
         s2 = jnp.zeros((8, D), f32)
         for g in range(gn):
             rows = slice(g * lg, (g + 1) * lg)
-            z2 = acc_ref[rows] + vec_ref[3:4] + h1_ref[rows]
-            n2, r2 = norm_rows(z2)
+            n2, r2 = norm_rows(acc_ref[rows])
             y = (n2 * vec_ref[4:5] + vec_ref[5:6]).astype(bf)
             for s in range(tn):
                 y_ref[g, s] = y[:, s * dt : (s + 1) * dt]
             dy = jnp.concatenate([cot_ref[g, s] for s in range(tn)], axis=1).astype(f32)
             dz2 = norm_back(dy * vec_ref[4:5], n2, r2)
             df_ref[rows] = dz2.astype(bf)
+            acc_ref[rows] = dz2
             s0, s1, s2 = s0 + fold8(dz2), s1 + fold8(dy * n2), s2 + fold8(dy)
-        sums_ref[0:8], sums_ref[8:16], sums_ref[16:24] = s0, s1, s2
-
-
-def middle(ctx, x, second, hidden_bias, vectors, cot, per):
-    gn, tn, lg, dt = cot.shape
-    L, D = x.shape
-    ff = hidden_bias.shape[2]
-    bf, f32 = jnp.bfloat16, jnp.float32
-    full = lambda shape: spec(shape, lambda t: (0,) * len(shape), True)
-    return pl.pallas_call(
-        middle_kernel,
-        grid=(tn,),
-        in_specs=[
-            full((L, D)),
-            full((L, D)),
-            spec((tn, gn, per, dt), lambda t: (0, 0, 0, 2 * ff // dt), True),
-            spec((1, gn, per, ff), lambda t: (t, 0, 0, 0)),
-            spec((1, gn, per, ff), lambda t: (t, 0, 0, 1)),
-            spec((1, 1, ff), lambda t: (t, 0, 0)),
-            full((6, D)),
-            full((gn, tn, lg, dt)),
-        ],
-        out_specs=[
-            full((L, D)), full((L, D)), full((L, 128)),
-            spec((L, ff), lambda t: (0, t)), spec((L, ff), lambda t: (0, t)),
-            full((gn, tn, lg, dt)), full((L, D)), full((24, D)),
-        ],
-        out_shape=[
-            jax.ShapeDtypeStruct((L, D), bf),
-            jax.ShapeDtypeStruct((L, D), bf),
-            jax.ShapeDtypeStruct((L, 128), f32),
-            jax.ShapeDtypeStruct((L, tn * ff), bf),
-            jax.ShapeDtypeStruct((L, tn * ff), bf),
-            jax.ShapeDtypeStruct((gn, tn, lg, dt), bf),
-            jax.ShapeDtypeStruct((L, D), bf),
-            jax.ShapeDtypeStruct((24, D), f32),
-        ],
-        scratch_shapes=[pltpu.VMEM((L, D), f32), pltpu.VMEM((L, D), f32)],
-        compiler_params=pltpu.CompilerParams(vmem_limit_bytes=58 << 20),
-        cost_estimate=pl.CostEstimate(flops=30 * 10**9, bytes_accessed=60 * 10**6, transcendentals=0),
-    )(ctx, x, second, second, second, hidden_bias, vectors, cot)
-
-
-def ffn_back_kernel(df_ref, hl_ref, n1_ref, r1_ref, act_ref, slope_ref, wi_ref, wo_ref, vec_ref,
-                    pay_ref, hid_ref, da_ref, sums_ref, dft_ref, hlt_ref, acc_ref, dp_ref):
-    t = pl.program_id(0)
-    L, D = df_ref.shape
-    ff = act_ref.shape[1]
-    gn, _, per, _ = pay_ref.shape
-    f32, bf = jnp.float32, jnp.bfloat16
-
-    @pl.when(t == 0)
-    def _():
+        sums_ref[24:32], sums_ref[32:40], sums_ref[40:48] = s0, s1, s2
         for r in range(0, L, RB):
-            dft_ref[:, r : r + RB] = df_ref[r : r + RB].T
-            hlt_ref[:, r : r + RB] = hl_ref[r : r + RB].T
-            acc_ref[r : r + RB] = df_ref[r : r + RB].astype(f32)
-
-    wi = wi_ref[0].reshape(D, ff)
-    wo = wo_ref[0].reshape(D, ff)
-    hid = jnp.zeros((8, ff), f32)
-    for r in range(0, L, RB):
-        dpre = dotnn(df_ref[r : r + RB], wo) * slope_ref[r : r + RB].astype(f32)
-        hid = hid + fold8(dpre)
-        low = dpre.astype(bf)
-        dp_ref[r : r + RB] = low
-        acc_ref[r : r + RB] += dotnt(low, wi)
-    hid_ref[0] = hid
-    for r in range(0, D, RB):
-        og = dotnn(dft_ref[r : r + RB], act_ref[...]).astype(bf)
-        ig = dotnn(hlt_ref[r : r + RB], dp_ref[...]).astype(bf)
-        for c in range(0, RB, per):
-            pay_ref[(r + c) // per, 0, :, 0:ff] = ig[c : c + per]
-            pay_ref[(r + c) // per, 0, :, ff : 2 * ff] = og[c : c + per]
-
-    @pl.when(t == pl.num_programs(0) - 1)
+            hl_ref[:, r : r + RB] = df_ref[r : r + RB].T
+
+    @pl.when(step >= tn)
+    def _():
+        t = 2 * tn - 1 - step
+        hid = jnp.zeros((8, ff), f32)
+        for r in range(0, L, MB):
+            rows = slice(r, r + MB)
+            dpre = dotnn(df_ref[rows], wo_ref[0].reshape(D, ff)) * slope_ref[t, rows].astype(f32)
+            hid = hid + fold8(dpre)
+            low = dpre.astype(bf)
+            slope_ref[t, rows] = low
+            acc_ref[rows] += dotnt(low, wi_ref[0].reshape(D, ff))
+        hid_ref[0] = hid
+        for r in range(0, D, RB):
+            og = dotnn(hl_ref[r : r + RB], act_ref[t]).astype(bf)
+            ig = dotnn(hlt_ref[r : r + RB], slope_ref[t]).astype(bf)
+            for c in range(0, RB, per):
+                pay_ref[(r + c) // per, 0, :, 0:ff] = ig[c : c + per]
+                pay_ref[(r + c) // per, 0, :, ff : 2 * ff] = og[c : c + per]
+
+    @pl.when(step == 2 * tn - 1)
     def _():
         s0 = jnp.zeros((8, D), f32)
         s1 = jnp.zeros((8, D), f32)
@@ -455,44 +421,60 @@
         for r in range(0, L, 128):
             rows = slice(r, r + 128)
             dh1 = acc_ref[rows]
-            n1 = n1_ref[rows].astype(f32)
-            dz1 = norm_back(dh1 * vec_ref[1:2], n1, r1_ref[rows, 0:1])
+            n1 = da_ref[rows].astype(f32)
+            r1 = r1_ref[rows, 0:1].astype(f32) + r1_ref[rows, 1:2].astype(f32)
+            dz1 = norm_back(dh1 * vec_ref[1:2], n1, r1)
             da_ref[rows] = dz1.astype(bf)
             s0, s1, s2 = s0 + fold8(dz1), s1 + fold8(dh1 * n1), s2 + fold8(dh1)
         sums_ref[0:8], sums_ref[8:16], sums_ref[16:24] = s0, s1, s2
 
 
-def ffn_back(dffn, h1_low, n1, r1, act, slope, second, vectors):
-    tn, gn, per, wide = second.shape
-    L, D = dffn.shape
-    ff = act.shape[1] // tn
+def middle(ctx, x, second, hidden_bias, vectors, cot):
+    gn, tn, lg, dt = cot.shape
+    per, wide = second.shape[2:]
+    L, D = x.shape
+    assert L == D
+    ff = hidden_bias.shape[2]
     bf, f32 = jnp.bfloat16, jnp.float32
-    full = lambda shape: spec(shape, lambda t: (0,) * len(shape), True)
+    full = lambda shape: spec(shape, lambda i: (0,) * len(shape), True)
+    place = lambda i: jnp.minimum(i, 2 * tn - 1 - i)
+    back = lambda i: jnp.minimum(2 * tn - 1 - i, tn - 1)
     return pl.pallas_call(
-        ffn_back_kernel,
-        grid=(tn,),
+        middle_kernel,
+        grid=(2 * tn,),
         in_specs=[
-            full((L, D)), full((L, D)), full((L, D)), full((L, 128)),
-            spec((L, ff), lambda t: (0, t)), spec((L, ff), lambda t: (0, t)),
-            spec((1, gn, per, ff), lambda t: (t, 0, 0, 0)),
-            spec((1, gn, per, ff), lambda t: (t, 0, 0, 1)),
+            pl.BlockSpec(memory_space=pl.ANY),
+            pl.BlockSpec(memory_space=pl.ANY),
+            spec((tn, gn, per, dt), lambda i: (0, 0, 0, 2 * ff // dt), True),
+            spec((1, gn, per, ff), lambda i: (place(i), 0, 0, 0)),
+            spec((1, gn, per, ff), lambda i: (place(i), 0, 0, 1)),
+            spec((1, 1, ff), lambda i: (place(i), 0, 0)),
             full((6, D)),
+            full((gn, tn, lg, dt)),
         ],
         out_specs=[
-            spec((gn, 1, per, 2 * ff), lambda t: (0, t, 0, 0)),
-            spec((1, 8, ff), lambda t: (t, 0, 0)),
-            full((L, D)), full((24, D)),
+            full((gn, tn, lg, dt)),
+            spec((gn, 1, per, 2 * ff), lambda i: (0, back(i), 0, 0)),
+            spec((1, 8, ff), lambda i: (back(i), 0, 0)),
+            full((L, D)),
+            full((48, D)),
         ],
         out_shape=[
+            jax.ShapeDtypeStruct((gn, tn, lg, dt), bf),
             jax.ShapeDtypeStruct((gn, tn, per, wide), bf),
             jax.ShapeDtypeStruct((tn, 8, ff), f32),
             jax.ShapeDtypeStruct((L, D), bf),
-            jax.ShapeDtypeStruct((24, D), f32),
-        ],
-        scratch_shapes=[pltpu.VMEM((D, L), bf), pltpu.VMEM((D, L), bf), pltpu.VMEM((L, D), f32), pltpu.VMEM((L, ff), bf)],
-        compiler_params=pltpu.CompilerParams(vmem_limit_bytes=58 << 20),
-        cost_estimate=pl.CostEstimate(flops=40 * 10**9, bytes_accessed=80 * 10**6, transcendentals=0),
-    )(dffn, h1_low, n1, r1, act, slope, second, second, vectors)
+            jax.ShapeDtypeStruct((48, D), f32),
+        ],
+        scratch_shapes=[
+            pltpu.VMEM((tn, L, ff), bf), pltpu.VMEM((tn, L, ff), bf),
+            pltpu.VMEM((L, D), bf), pltpu.VMEM((D, L), bf), pltpu.VMEM((L, 128), bf),
+            pltpu.VMEM((L, D), bf), pltpu.VMEM((L, D), f32),
+            pltpu.SemaphoreType.DMA((2 * (D // ff),)),
+        ],
+        compiler_params=pltpu.CompilerParams(vmem_limit_bytes=61 << 20),
+        cost_estimate=pl.CostEstimate(flops=75 * 10**9, bytes_accessed=100 * 10**6, transcendentals=0),
+    )(ctx, x, second, second, second, hidden_bias, vectors, cot)
 
 
 def merge_back_kernel(da_ref, ctx_ref, wm_ref, pay_in, pay_ref, dctx_ref, dat_ref):
@@ -539,7 +521,7 @@
     )(dattn, ctx, second, payload)
 
 
-def input_back_kernel(da_ref, dq_ref, dk_ref, dv_ref, w_ref, dx_ref, acc_ref):
+def input_back_kernel(da_ref, dq_ref, dk_ref, dv_ref, wa_ref, wb_ref, dx_ref, acc_ref):
     t = pl.program_id(0)
     L, D = da_ref.shape
     gn, tn, lg, dt = dx_ref.shape
@@ -549,7 +531,8 @@
     def _():
         acc_ref[...] = da_ref[...].astype(jnp.float32)
 
-    w = [w_ref[:, 0, j * per : (j + 1) * per, :].reshape(D, dt) for j in range(3)]
+    w = [wa_ref[:, 0, j * per : (j + 1) * per, :].reshape(D, dt) for j in range(2)]
+    w.append(wb_ref[:, 0].reshape(D, dt))
     tops = [dq_ref, dk_ref, dv_ref]
     for r in range(0, L, RB):
         acc_ref[r : r + RB] += sum(dotnt(tops[j][r : r + RB], w[j]) for j in range(3))
@@ -562,7 +545,7 @@
                 dx_ref[g, s] = acc_ref[g * lg : (g + 1) * lg, cols].astype(jnp.bfloat16)
 
 
-def input_back(dattn, dq, dk, dv, first):
+def input_back(dattn, dq, dk, dv, first, later):
     gn, tn, wide, dt = first.shape
     L, D = dattn.shape
     col = lambda: spec((L, dt), lambda t: (0, t))
@@ -573,13 +556,14 @@
             spec((L, D), lambda t: (0, 0), True),
             col(), col(), col(),
             spec((gn, 1, wide, dt), lambda t: (0, t, 0, 0)),
+            spec((gn, 1, D // gn, dt), lambda t: (0, t, 0, 0)),
         ],
         out_specs=spec((gn, tn, L // gn, dt), lambda t: (0, 0, 0, 0), True),
         out_shape=jax.ShapeDtypeStruct((gn, tn, L // gn, dt), jnp.bfloat16),
         scratch_shapes=[pltpu.VMEM((L, D), jnp.float32)],
         compiler_params=pltpu.CompilerParams(vmem_limit_bytes=50 << 20),
         cost_estimate=pl.CostEstimate(flops=7 * 10**9, bytes_accessed=20 * 10**6, transcendentals=0),
-    )(dattn, dq, dk, dv, first)
+    )(dattn, dq, dk, dv, first, later)
 
 
 def tail_kernel(x_ref, rel_ref, hot_ref, dq_ref, dk_ref, dv_ref, dqf_ref, dkf_ref, sm_ref, w_ref, small_ref,
@@ -601,7 +585,7 @@
             xt_ref[:, L + r : L + r + RB] = rel_ref[r : r + RB].T
         ra_ref[...] = jnp.zeros_like(ra_ref)
 
-    w = [w_ref[:, 0, j * per : (j + 1) * per, :].reshape(D, dt) for j in range(3)]
+    w = [w_ref[:, 0, j * per : (j + 1) * per, :].reshape(D, dt) for j in range(2)]
     qp = dotnn(dqf_ref[...], hot_ref[...]).T
     kp = dotnn(dkf_ref[...], hot_ref[...]).T
     pos = [qp.astype(bf), kp.astype(bf)]
@@ -675,10 +659,6 @@
     return out
 
 
-def orders(bits):
-    return bits[1:] + bits[:1], bits[:0:-1] + bits[:1]
-
-
 def greet(tn, gn):
     t, g = lax.axis_index("tensor"), lax.axis_index("dp")
     barrier = pltpu.get_barrier_semaphore()
@@ -690,138 +670,203 @@
     pl.semaphore_wait(barrier, tn - 1 + len(bits))
 
 
-def spread(src_ref, out_ref, sems, tn, gn):
-    local, send, recv = sems
+class Wire:
+    def __init__(self, send, recv):
+        self.send, self.recv, self.at = send, recv, 0
+
+    def push(self, src, dst, **device):
+        c = pltpu.make_async_remote_copy(
+            src, dst, self.send.at[self.at], self.recv.at[self.at], device_id=device, device_id_type=MESH
+        )
+        self.at += 1
+        c.start()
+        return c
+
+
+def run_waves(chunks):
+    waves = max(len(stages) + c for c, stages in enumerate(chunks)) + 1
+    flight = {}
+    for w in range(waves):
+        for c, stages in enumerate(chunks):
+            s = w - c
+            if 0 < s <= len(stages):
+                stages[s - 1][1](flight.pop((c, s - 1)))
+            if 0 <= s < len(stages):
+                flight[c, s] = stages[s][0]()
+
+
+def wait_all(copies):
+    for c in copies:
+        c.wait()
+
+
+def spread_stages(src, out, local, wire, tn, gn):
     t, g = lax.axis_index("tensor"), lax.axis_index("dp")
     bits = list(range(gn.bit_length() - 1))
-    own = pltpu.make_async_copy(src_ref, out_ref.at[g, t], local)
-    own.start()
-    first = []
-    for d in range(1, tn):
-        c = pltpu.make_async_remote_copy(
-            src_ref, out_ref.at[g, t], send.at[d - 1], recv.at[d - 1],
-            device_id={"tensor": lax.rem(t + d, tn)}, device_id_type=MESH,
-        )
-        c.start()
-        first.append(c)
-    own.wait()
-    for c in first:
-        c.wait()
-    at = tn - 1
     half = tn // 2
-    halves = [(0, half), (half, half)]
-    plans = orders(bits)
-    for step in range(len(bits)):
-        copies = []
-        for (lo, size), plan in zip(halves, plans):
-            for s in subsets(plan[:step]):
-                part = out_ref.at[flipped(g, s), pl.ds(lo, size)]
-                c = pltpu.make_async_remote_copy(
-                    part, part, send.at[at], recv.at[at],
-                    device_id={"dp": flipped(g, (plan[step],))}, device_id_type=MESH,
-                )
-                c.start()
-                copies.append(c)
-                at += 1
-        for c in copies:
-            c.wait()
+    plans = [(0, bits[1:] + bits[:1]), (half, bits[:0:-1] + bits[:1])]
+
+    def first():
+        own = pltpu.make_async_copy(src(), out(g, pl.ds(t, 1)), local)
+        own.start()
+        copies = [
+            wire.push(src(), out(g, pl.ds(t, 1)), tensor=lax.rem(t + d, tn)) for d in range(1, tn)
+        ]
+        return [own] + copies
+
+    def later(step):
+        def start():
+            copies = []
+            for lo, plan in plans:
+                for s in subsets(plan[:step]):
+                    part = out(flipped(g, s), pl.ds(lo, half))
+                    copies.append(wire.push(part, part, dp=flipped(g, (plan[step],))))
+            return copies
+
+        return start
+
+    return [(first, wait_all)] + [(later(step), wait_all) for step in range(len(bits))]
 
 
 def spread_count(tn, gn):
     return tn - 1 + 2 * (gn - 1)
 
 
-def gather_kernel(src_ref, out_ref, local, send, recv, *, tn, gn):
+def gather_kernel(src_ref, out_ref, local, send, recv, *, tn, gn, cuts):
     greet(tn, gn)
-    spread(src_ref, out_ref, (local, send, recv), tn, gn)
+    wire = Wire(send, recv)
+    chunks = []
+    for n, (lo, hi) in enumerate(cuts):
+        rows = pl.ds(lo, hi - lo)
+        chunks.append(
+            spread_stages(
+                lambda rows=rows: src_ref.at[:, rows],
+                lambda g, s, rows=rows: out_ref.at[g, s, rows],
+                local.at[n], wire, tn, gn,
+            )
+        )
+    run_waves(chunks)
 
 
 def gather_all(w, tn, gn, number):
-    n = spread_count(tn, gn)
-    size = w.size * 2
+    rows = w.shape[0]
+    mid = rows // 32 * 16
+    cuts = [(0, mid), (mid, rows)]
+    n = spread_count(tn, gn) * len(cuts)
+    dma = lambda k: pltpu.SemaphoreType.DMA((k,))
     return pl.pallas_call(
-        functools.partial(gather_kernel, tn=tn, gn=gn),
+        functools.partial(gather_kernel, tn=tn, gn=gn, cuts=cuts),
         in_specs=[pl.BlockSpec(memory_space=pl.ANY)],
         out_specs=pl.BlockSpec(memory_space=pl.ANY),
         out_shape=jax.ShapeDtypeStruct((gn, tn) + w.shape, w.dtype),
-        scratch_shapes=[pltpu.SemaphoreType.DMA(()), pltpu.SemaphoreType.DMA((n,)), pltpu.SemaphoreType.DMA((n,))],
+        scratch_shapes=[dma(len(cuts)), dma(n), dma(n)],
         compiler_params=pltpu.CompilerParams(collective_id=number, has_side_effects=True),
-        cost_estimate=pl.CostEstimate(flops=0, bytes_accessed=size * tn * gn * 8, transcendentals=0),
-    )(w)
-
-
-def reduce_kernel(pay_ref, q_ref, k_ref, v_ref, rel_ref, small_ref, all_ref, acc_ref, rx_ref, rz_ref, rest_ref,
-                  local, asend, arecv, bsend, brecv, *, tn, gn, keep):
+        cost_estimate=pl.CostEstimate(flops=0, bytes_accessed=w.size * tn * gn * 16, transcendentals=0),
+    )(w[None])
+
+
+def reduce_kernel(pay_ref, q_ref, k_ref, v_ref, rel_ref, small_ref, all_ref, acc_ref, rx_ref, ry_ref, rz_ref, rest_ref,
+                  local, send, recv, *, tn, gn, keep):
     t, g = lax.axis_index("tensor"), lax.axis_index("dp")
     bits = list(range(gn.bit_length() - 1))
     f32, bf = jnp.float32, jnp.bfloat16
+    rows = acc_ref.shape[2]
+    per = keep // 3
     greet(tn, gn)
-    rest_bits = bits[1:]
-    masks = subsets(rest_bits)
+    wire = Wire(send, recv)
+    outer = bits[1:]
+    masks = subsets(outer)
     index = {s: n for n, s in enumerate(masks)}
-    sends, locals_ = [], []
-    for n, s in enumerate(masks):
-        c = pltpu.make_async_remote_copy(
-            pay_ref.at[flipped(g, (0,) + s)], rx_ref.at[n], bsend.at[n], brecv.at[n],
-            device_id={"dp": flipped(g, (0,))}, device_id_type=MESH,
-        )
-        c.start()
-        sends.append(c)
-    for n, s in enumerate(masks):
-        c = pltpu.make_async_copy(pay_ref.at[flipped(g, s)], acc_ref.at[n], local.at[n])
-        c.start()
-        locals_.append(c)
-
-    def add(dst, lo, size, src_ref, slot):
-        for i in range(size):
-            acc_ref[dst, lo + i] = (acc_ref[dst, lo + i].astype(f32) + src_ref[slot, i].astype(f32)).astype(bf)
-
     half = tn // 2
-    for n in range(len(masks)):
-        locals_[n].wait()
-        sends[n].wait()
-        for i in range(tn):
-            acc_ref[n, i] = (acc_ref[n, i].astype(f32) + rx_ref[n, i].astype(f32)).astype(bf)
-    at = len(masks)
-    plans = [rest_bits, rest_bits[::-1]]
-    base = 0
-    for step in range(len(rest_bits)):
-        flight = []
-        for lo, plan in zip((0, half), plans):
-            bit = plan[step]
-            left = [s for s in masks if not any(i in plan[: step + 1] for i in s)]
-            for s in left:
-                src = tuple(i for i in rest_bits if i in s or i == bit)
-                c = pltpu.make_async_remote_copy(
-                    acc_ref.at[index[src], pl.ds(lo, half)], rz_ref.at[base], bsend.at[at], brecv.at[at],
-                    device_id={"dp": flipped(g, (bit,))}, device_id_type=MESH,
-                )
+    plans = [(0, outer), (half, outer[::-1])]
+    grads = (q_ref, k_ref, v_ref)
+
+    def reduce_stages(n, lo, hi):
+        span = pl.ds(lo, hi - lo)
+
+        def add(dst, first, size, src_ref, slot):
+            for i in range(size):
+                acc_ref[dst, first + i, lo:hi] = (
+                    acc_ref[dst, first + i, lo:hi].astype(f32) + src_ref[slot, i, lo:hi].astype(f32)
+                ).astype(bf)
+
+        def first():
+            copies = []
+            for i, s in enumerate(masks):
+                copies.append(wire.push(pay_ref.at[flipped(g, (0,) + s), :, span], rx_ref.at[i, :, span], dp=flipped(g, (0,))))
+            for i, s in enumerate(masks):
+                c = pltpu.make_async_copy(pay_ref.at[flipped(g, s), :, span], acc_ref.at[i, :, span], local.at[n, i])
                 c.start()
-                flight.append((c, index[s], lo, base))
-                at += 1
-                base += 1
-        for c, n, lo, slot in flight:
-            c.wait()
-            add(n, lo, half, rz_ref, slot)
-    flight = []
-    for d in range(1, tn):
-        to = lax.rem(t + d, tn)
-        c = pltpu.make_async_remote_copy(
-            acc_ref.at[0, to], rx_ref.at[len(masks), d - 1], bsend.at[at], brecv.at[at],
-            device_id={"tensor": to}, device_id_type=MESH,
-        )
-        c.start()
-        flight.append(c)
-        at += 1
-    total = acc_ref[0, t].astype(f32)
-    for d, c in enumerate(flight):
-        c.wait()
-        total = total + rx_ref[len(masks), d].astype(f32)
-    per = keep // 3
-    for j, out in enumerate((q_ref, k_ref, v_ref)):
-        out[...] = total[j * per : (j + 1) * per]
-    rest_ref[...] = total[keep:].astype(bf)
-    spread(rest_ref, all_ref, (local.at[len(masks)], asend, arecv), tn, gn)
+                copies.append(c)
+            return copies
+
+        def first_done(copies):
+            for i in range(len(masks)):
+                copies[len(masks) + i].wait()
+                copies[i].wait()
+                add(i, 0, tn, rx_ref, i)
+
+        def outer_stage(step, base):
+            def start():
+                flight = []
+                slot = base
+                for place, plan in plans:
+                    bit = plan[step]
+                    for s in masks:
+                        if any(i in plan[: step + 1] for i in s):
+                            continue
+                        src = tuple(i for i in outer if i in s or i == bit)
+                        c = wire.push(
+                            acc_ref.at[index[src], pl.ds(place, half), span], ry_ref.at[slot, :, span],
+                            dp=flipped(g, (bit,)),
+                        )
+                        flight.append((c, index[s], place, slot))
+                        slot += 1
+                return flight
+
+            def done(flight):
+                for c, dst, place, slot in flight:
+                    c.wait()
+                    add(dst, place, half, ry_ref, slot)
+
+            return start, done
+
+        def last():
+            return [
+                wire.push(acc_ref.at[0, lax.rem(t + d, tn), span], rz_ref.at[d - 1, span], tensor=lax.rem(t + d, tn))
+                for d in range(1, tn)
+            ]
+
+        def last_done(copies):
+            total = acc_ref[0, t, lo:hi].astype(f32)
+            for d, c in enumerate(copies):
+                c.wait()
+                total = total + rz_ref[d, lo:hi].astype(f32)
+            if lo >= keep:
+                rest_ref[0] = total.astype(bf)
+            else:
+                for j in range(3):
+                    a, b = max(lo, j * per), min(hi, (j + 1) * per)
+                    if a < b:
+                        grads[j][a - j * per : b - j * per] = total[a - lo : b - lo]
+
+        stages = [(first, first_done)]
+        base = 0
+        for step in range(len(outer)):
+            stages.append(outer_stage(step, base))
+            base += 2 * (gn // 4 >> step)
+        return stages + [(last, last_done)]
+
+    cut = keep // 32 * 16
+    chunks = [
+        reduce_stages(0, keep, rows)
+        + spread_stages(
+            lambda: rest_ref, lambda i, s: all_ref.at[i, s], local.at[3, 0], wire, tn, gn
+        ),
+        reduce_stages(1, 0, cut),
+        reduce_stages(2, cut, keep),
+    ]
+    run_waves(chunks)
     dt = q_ref.shape[1]
     rg = rel_ref.shape[0] // gn
     for s in range(tn):
@@ -834,11 +879,10 @@
 def reduce_all(pay, keep, spans, number):
     gn, tn, rows, dt = pay.shape
     bf, f32 = jnp.bfloat16, jnp.float32
-    n = spread_count(tn, gn)
     m = gn // 2
     pieces = 2 * (m - 1)
-    count = m + pieces + tn - 1
-    dma = lambda k: pltpu.SemaphoreType.DMA((k,))
+    count = 3 * (m + pieces + tn - 1) + spread_count(tn, gn)
+    dma = lambda *k: pltpu.SemaphoreType.DMA(k)
     return pl.pallas_call(
         functools.partial(reduce_kernel, tn=tn, gn=gn, keep=keep),
         in_specs=[pl.BlockSpec(memory_space=pl.ANY)],
@@ -851,10 +895,11 @@
         scratch_shapes=[
             pltpu.VMEM((gn, tn, rows - keep, dt), bf),
             pltpu.VMEM((m, tn, rows, dt), bf),
-            pltpu.VMEM((m + 1, tn, rows, dt), bf),
+            pltpu.VMEM((m, tn, rows, dt), bf),
             pltpu.VMEM((pieces, tn // 2, rows, dt), bf),
-            pltpu.VMEM((rows - keep, dt), bf),
-            dma(m + 1), dma(n), dma(n), dma(count), dma(count),
+            pltpu.VMEM((tn - 1, rows, dt), bf),
+            pltpu.VMEM((1, rows - keep, dt), bf),
+            dma(4, m), dma(count), dma(count),
         ],
         compiler_params=pltpu.CompilerParams(collective_id=number, has_side_effects=True, vmem_limit_bytes=40 << 20),
         cost_estimate=pl.CostEstimate(flops=0, bytes_accessed=200 * 10**6, transcendentals=0),
@@ -900,42 +945,28 @@
         return lax.all_gather(w, w_axes, axis=0, tiled=False).reshape((tn, gn) + w.shape)
 
     rel_cols = lax.dynamic_slice_in_dim(rel_embed, lax.axis_index("tensor") * dt, dt, 1)
-    first = gather_all(
-        jnp.concatenate(
-            [
-                query_weight,
-                key_weight,
-                value_weight,
-                rel_cols,
-                proj_shifts,
-                hidden_shift.reshape(-1, dt),
-                jnp.zeros((1, dt), bf),
-            ],
-            axis=0,
-        ),
-        tn,
-        gn,
-        0,
+    early = jnp.concatenate([query_weight, key_weight], axis=0)
+    late = jnp.concatenate(
+        [value_weight, rel_cols, proj_shifts, hidden_shift.reshape(-1, dt), jnp.zeros((1, dt), bf)], axis=0
     )
+    first = gather_all(early, tn, gn, 0)
     xd = swap(inputs).reshape(gn, tn, lg, dt)
     wide = jnp.concatenate([inner_weight, outer_weight, merge_weight], axis=1)
-    first, xd, wide, cotangent = lax.optimization_barrier((first, xd, wide, cotangent))
+    first, xd, late, wide, cotangent = lax.optimization_barrier((first, xd, late, wide, cotangent))
     second = gather(wide)
+    later = gather_all(late, tn, gn, 2)
     cot = swap(cotangent).reshape(gn, tn, lg, dt)
-    biases = first[0, :, 3 * per + rg :].astype(f32)
+    biases = later[0, :, per + rg :].astype(f32)
     shifts = biases[:, :3]
     hidden_bias = biases[:, 3:7].reshape(tn, 1, -1)
     vectors = layer_vectors.astype(f32)
     length = jnp.sum(jnp.where(dealing == me, lengths, 0)).reshape(1)
     places = jnp.concatenate([buckets[::-1], jnp.full((1,), -1, jnp.int32)])[:, None]
 
-    qkv, far, x, rel, hot = project(xd, first, shifts, places, per)
+    qkv, far, x, rel, hot = project(xd, first, later, shifts, places, per)
     ctx, probs, inv = attn_fwd(length, qkv, far, scale=scale)
-    h1_low, n1, r1, act, slope, y, dffn, sums2 = middle(
-        ctx, x, second, hidden_bias, vectors, cot, per
-    )
+    y, payload, hidden, dattn, sums12 = middle(ctx, x, second, hidden_bias, vectors, cot)
     out = swap(y.reshape(count, lg, dt))
-    payload, hidden, dattn, sums1 = ffn_back(dffn, h1_low, n1, r1, act, slope, second, vectors)
     payload, dctx = merge_back(dattn, ctx, second, payload)
     wide_grads = lax.psum_scatter(payload, "dp", scatter_dimension=0, tiled=False)
     dq, dk, dv, dkf, dqf, sums = attn_bwd(probs, qkv, dctx, ctx, inv, far, scale=scale)
@@ -944,8 +975,7 @@
     ff = hidden.shape[2]
     small = jnp.concatenate(
         [
-            jnp.sum(sums1.reshape(3, 8, D), axis=1),
-            jnp.sum(sums2.reshape(3, 8, D), axis=1),
+            jnp.sum(sums12.reshape(6, 8, D), axis=1),
             jnp.sum(hidden, axis=1).reshape(-1, D),
         ],
         axis=0,
@@ -955,7 +985,7 @@
     small = jnp.pad(small, ((0, sr - first_shift), (0, 0)))
     small = small.reshape(sr, tn, dt).transpose(1, 0, 2)[:, None]
     small = jnp.pad(small, ((0, 0), (0, gn - 1), (0, 0), (0, 0)))
-    dx = input_back(dattn, dq, dk, dv, first)
+    dx = input_back(dattn, dq, dk, dv, first, later)
     dx, dq = lax.optimization_barrier((dx, dq))
     pay = tail(x, rel, hot, dq, dk, dv, dqf, dkf, sums, first, small, first_shift)
     grad_in = swap(dx.reshape(count, lg, dt))

time: 677 us -> 632 us (0.934)
  waiting for transfers between devices: 47.8 us -> 17.4 us
  Pallas kernels: 555 us -> 541 us
    all_gather x1, waiting for transfers between devices: 43 us -> 12.5 us  [gather(): lax.all_gather(w, w_axes, axis=0, tiled=False).reshape((tn, gn) + w.shape)]
    pallas_call x1, Pallas kernels: 94.1 us -> 75.6 us  [reduce_all(): pl.pallas_call(functools.partial(reduce_kernel, tn=tn, gn=gn, keep=keep),...]
    unnamed x58 -> x56, local copies, waits for them, and re-layouts: 15.5 us -> 15.4 us
  transfers between devices with their start and end apart: 7 -> 7, of which waited for: 2 -> 2; matrix products, arithmetic and copies ran while one was open for 2% -> 2% of each run, Pallas kernels for 68% -> 71%
where the time goes in v4:
time: 632 us; the launch traced here: 623 us
  Pallas kernels  541 us (86%)
  starting transfers between devices  22.4 us (4%)
  local copies, waits for them, and re-layouts  22.2 us (4%)
  waiting for transfers between devices  17.4 us (3%)
  between operations  14.5 us (2%)
    pallas_call x1, Pallas kernels, attn_bwd(): pl.pallas_call(functools.partial(bwd_kernel, L=L, scale=scale), grid=(C /...  120 us
    pallas_call x2, Pallas kernels, gather_all(): pl.pallas_call(functools.partial(gather_kernel, tn=tn, gn=gn, cuts=cuts),...  108 us
    pallas_call x1, Pallas kernels, middle(): pl.pallas_call(middle_kernel, grid=(2 * tn,), in_specs=[pl.BlockSpec(memo...  87.9 us
    pallas_call x1, Pallas kernels, attn_fwd(): pl.pallas_call(functools.partial(fwd_kernel, L=L, scale=scale), grid_spec...  76.1 us
    pallas_call x1, Pallas kernels, reduce_all(): pl.pallas_call(functools.partial(reduce_kernel, tn=tn, gn=gn, keep=keep),...  75.6 us
    pallas_call x1, Pallas kernels, project(): pl.pallas_call(project_kernel, grid=(tn, 3), in_specs=[spec((gn, tn, lg,...  29 us
    pallas_call x1, Pallas kernels, tail(): pl.pallas_call(functools.partial(tail_kernel, first_shift=first_shift), g...  24.2 us
    all_to_all x4, starting transfers between devices, swap(): return lax.all_to_all(a, seq_axes, split_axis=0, concat_axis=0, tiled=True)  22.3 us
  transfers between devices with their start and end apart: 7, of which 2 were waited for; matrix products, arithmetic and copies ran while one was open for 2% of the time, Pallas kernels for 71%

profile of v4, /device:TPU:0, one launch (start us, length us, event | category | flops | bytes accessed | tf_op | source)
XLA Modules:
  0.0 623.2 jit_solution(16686172678304983142)
XLA Ops:
  7.2 0.0 copy-start
  7.2 7.3 %all-to-all-start = ((bf16[32,128,256]{2,1,0:T(8,128)(2,1)}), bf16[32,128,256]{2,1,0:T(8,128)(2,1)S(1)}, u32[]{:S(2)}, u32[]{:S(2)}) async-start(bf16[32,128,256]{2,1,0:T(8,128)(2,1)} %param.15), calls=%async_computation | async-start | bytes 4194304 | tf_op jit(solution)/shard_map/all_to_all | solution.py:942
  14.5 0.0 all-gather.3.cloned.1.call-start
  14.6 0.0 copy-done.20
  14.6 0.7 maximum_bitcast_fusion.src_ref
  15.3 0.0 copy-start.14
  15.3 0.0 copy-start.18
  15.3 76.3 %shard_map.238.wa_ref.w_ref = bf16[8,4,256,256]{3,2,1,0:T(8,128)(2,1)} custom-call(bf16[1,256,256]{2,1,0:T(8,128)(2,1)} %maximum_bitcast_fusion.src_ref), custom_call_target="tpu_custom_call" | custom-call | bytes 33554432 | tf_op jit(solution)/shard_map/pallas_call | solution.py:757
  91.7 0.0 copy-start.17
  91.7 0.0 copy-start.21
  91.7 0.0 copy-start.22
  91.8 1.9 concatenate.16
  93.6 0.9 pad_maximum_fusion
  94.5 0.0 all-to-all-done
  94.5 0.0 all-gather.3.cloned.1.call-update
  94.6 0.1 reverse
  94.6 0.1 slice.43
  94.7 0.9 convert_element_type.21.vec_ref
  95.6 0.1 pad_add_fusion
  95.7 0.4 copy.28.pl_ref
  96.1 0.6 fusion
  96.7 31.5 %shard_map.239.rel4_ref.wb_ref = bf16[8,4,200,256]{3,2,1,0:T(8,128)(2,1)} custom-call(bf16[1,200,256]{2,1,0:T(8,128)(2,1)} %bitcast.41), custom_call_target="tpu_custom_call" | custom-call | bytes 26214400 | tf_op jit(solution)/shard_map/pallas_call | solution.py:757
  128.2 0.7 bitcast_convert_fusion.1
  128.9 6.8 %all-to-all-start.1 = ((bf16[32,128,256]{2,1,0:T(8,128)(2,1)}), bf16[32,128,256]{2,1,0:T(8,128)(2,1)}, u32[]{:S(2)}, u32[]{:S(2)}) async-start(bf16[32,128,256]{2,1,0:T(8,128)(2,1)} %param.16), calls=%async_computation.1 | async-start | bytes 4194304 | tf_op jit(solution)/shard_map/all_to_all | solution.py:942
  135.7 0.0 reduce-scatter.3.cloned.1.call-start
  135.8 0.6 reshape.65.hb_ref
  136.4 29.0 %shard_map.240 = (bf16[3,1024,1024]{2,1,0:T(8,128)(2,1)}, bf16[2,2048,1024]{2,1,0:T(8,128)(2,1)}, bf16[1024,1024]{1,0:T(8,128)(2,1)}, bf16[512,1024]{1,0:T(8,128)(2,1)S(1)}, bf16[2048,512]{1,0:T(8,128)(2,1)}) custom-call(bf16[8,4,128,256]{3,2,1,0:T(8,128)(2,1)} %bitcast.39, bf16[8,4,200,256]{3,2,1,0:T(8,128)(2,1)} %shard_map.239.rel4_ref.wb_ref, ...), custom_call_target="tpu_custom_call" | custom-call | flops 14000000000 | bytes 30000000 | tf_op jit(solution)/shard_map/pallas_call | solution.py:288
  165.5 1.0 copy-done.5
  166.4 76.1 %shard_map.241 = (bf16[1024,1024]{1,0:T(8,128)(2,1)S(1)}, bf16[16,1024,1024]{2,1,0:T(8,128)(2,1)}, f32[1024,1024]{1,0:T(8,128)}) custom-call(s32[1]{0:T(128)} %bitcast.len_ref, bf16[3,1024,1024]{2,1,0:T(8,128)(2,1)} %get-tuple-element.51.q_ref.k_ref.v_ref, bf16[3,1024,1024]{2,1,0:T(8,128)(2,1)} %get-tuple-element.51.q_ref.k_ref.v_ref, ...), custom_call_target="tpu_custom_call" | custom-call | flops 80000000000 | bytes 60000000 | tf_op jit(solution)/shard_map/pallas_call | solution.py:109
  242.6 1.3 copy-done.3
  243.9 0.0 all-to-all-done.1
  243.9 12.5 %all-gather.3.cloned.1.call-done = bf16[4096,2304]{1,0:T(8,128)(2,1)} async-done(((bf16[128,2304]{1,0:T(8,128)(2,1)}), bf16[4096,2304]{1,0:T(8,128)(2,1)}) %all-gather.3.cloned.1.call-update) | async-done | bytes 18874384 | tf_op jit(solution)/shard_map/all_gather | solution.py:945
  256.3 87.9 %shard_map.242 = (bf16[8,4,128,256]{3,2,1,0:T(8,128)(2,1)}, bf16[8,4,128,2304]{3,2,1,0:T(8,128)(2,1)}, f32[4,8,1024]{2,1,0:T(8,128)}, bf16[1024,1024]{1,0:T(8,128)(2,1)}, f32[48,1024]{1,0:T(8,128)}) custom-call(bf16[1024,1024]{1,0:T(8,128)(2,1)} %copy-done.3, bf16[1024,1024]{1,0:T(8,128)(2,1)} %get-tuple-element.55.x_ref, ...), custom_call_target="tpu_custom_call" | custom-call | flops 74999996416 | bytes 100000000 | tf_op jit(solution)/shard_map/pallas_call | solution.py:442
  344.3 8.9 %shard_map.243 = (bf16[8,4,128,2304]{3,2,1,0:T(8,128)(2,1)}, bf16[1024,1024]{1,0:T(8,128)(2,1)S(1)}) custom-call(bf16[1024,1024]{1,0:T(8,128)(2,1)} %get-tuple-element.58.da_ref, bf16[1024,1024]{1,0:T(8,128)(2,1)} %copy-done.3, bf16[4,8,128,2304]{3,2,1,0:T(8,128)(2,1)} %bitcast.37, ...), custom_call_target="tpu_custom_call", output_to_operand_aliasing={{0}: (3, {})} | custom-call | flops 4000000000 | bytes 10000000 | tf_op jit(solution)/shard_map/pallas_call | solution.py:500
  353.2 1.3 copy-done.4
  354.5 0.0 reduce-scatter.3.cloned.1.call-update
  354.5 3.6 all-to-all-start.2
  358.1 0.0 reduce-scatter.5.cloned.1.call-start
  358.2 119.8 %shard_map.244 = (bf16[1024,1024]{1,0:T(8,128)(2,1)}, bf16[1024,1024]{1,0:T(8,128)(2,1)}, bf16[1024,1024]{1,0:T(8,128)(2,1)}, bf16[1024,2048]{1,0:T(8,128)(2,1)}...) custom-call(bf16[16,1024,1024]{2,1,0:T(8,128)(2,1)} %get-tuple-element.53.p_ref, ...), custom_call_target="tpu_custom_call" | custom-call | flops 120000004096 | bytes 80000000 | tf_op jit(solution)/shard_map/pallas_call | solution.py:216
  478.0 0.0 all-to-all-done.2
  478.0 0.0 copy-start.6
  478.0 4.9 reduce-scatter.3.cloned.1.call-done
  482.9 0.0 reduce-scatter.5.cloned.1.call-update
  482.9 12.1 %shard_map.245 = bf16[8,4,128,256]{3,2,1,0:T(8,128)(2,1)} custom-call(bf16[1024,1024]{1,0:T(8,128)(2,1)} %get-tuple-element.58.da_ref, bf16[1024,1024]{1,0:T(8,128)(2,1)} %get-tuple-element.72.dq_ref, bf16[1024,1024]{1,0:T(8,128)(2,1)} %get-tuple-element.67.dk_ref, bf16[1024,1024]{1,0:T(8,128)(2,1)} %get-tuple-element.68.dv_ref, ...), custom_call_target="tpu_custom_call" | custom-call | flops 7000000000 | bytes 20000000 | tf_op jit(solution)/shard_map/pallas_call | solution.py:552
  495.0 0.0 copy-start.11
  495.0 4.6 all-to-all-start.3
  499.6 0.1 bitcast_reduce_fusion
  499.7 0.9 pad.9.small_ref
  500.6 24.2 %shard_map.246.pay_ref = bf16[8,4,464,256]{3,2,1,0:T(8,128)(2,1)} custom-call(bf16[1024,1024]{1,0:T(8,128)(2,1)} %get-tuple-element.55.x_ref, bf16[512,1024]{1,0:T(8,128)(2,1)} %copy-done.5, bf16[2048,512]{1,0:T(8,128)(2,1)} %get-tuple-element.71.hot_ref, bf16[1024,1024]{1,0:T(8,128)(2,1)} %get-tuple-element.72.dq_ref, ...), custom_call_target="tpu_custom_call" | custom-call | flops 12999999488 | bytes 40000000 | tf_op jit(solution)/shard_map/pallas_call | solution.py:623
  524.8 3.2 copy-done.2
  528.0 75.6 %shard_map.247 = (f32[128,256]{1,0:T(8,128)S(1)}, f32[128,256]{1,0:T(8,128)S(1)}, f32[128,256]{1,0:T(8,128)S(1)}, f32[512,1024]{1,0:T(8,128)S(1)}, f32[16,1024]{1,0:T(8,128)S(1)}) custom-call(bf16[8,4,464,256]{3,2,1,0:T(8,128)(2,1)S(1)} %copy-done.2), custom_call_target="tpu_custom_call" | custom-call | bytes 200000000 | tf_op jit(solution)/shard_map/pallas_call | solution.py:886
  603.6 0.6 slice.30
  604.2 0.6 slice.35
  604.9 0.6 copy.35
  605.5 0.0 all-to-all-done.3
  605.5 1.3 bitcast_convert_fusion
  606.8 0.7 slice.38
  607.4 1.1 fusion.1
  608.5 1.3 copy.43
  609.9 3.2 copy.44
  613.0 1.3 copy.45
  614.3 0.7 copy.46
  615.0 0.7 copy.47
  615.6 0.7 copy.48
  (43 shorter events, 0.2 us)
Async XLA Ops:
  7.2 84.5 %copy-start = (bf16[64,1024]{1,0:T(8,128)(2,1)S(1)}, bf16[64,1024]{1,0:T(8,128)(2,1)}, u32[]{:S(2)}) copy-start(bf16[64,1024]{1,0:T(8,128)(2,1)} %param.20) | copy-start | bytes 393220
  7.2 7.4 %copy-start.20 = (bf16[1024]{0:T(1024)(128)(2,1)S(1)}, bf16[1024]{0:T(1024)(128)(2,1)}, u32[]{:S(2)}) copy-start(bf16[1024]{0:T(1024)(128)(2,1)} %param.27) | copy-start | bytes 6148
  7.2 7.4 %copy-start.15 = (bf16[128,256]{1,0:T(8,128)(2,1)S(1)}, bf16[128,256]{1,0:T(8,128)(2,1)}, u32[]{:S(2)}) copy-start(bf16[128,256]{1,0:T(8,128)(2,1)} %param.22) | copy-start | bytes 196612
  7.2 7.4 %copy-start.16 = (bf16[128,256]{1,0:T(8,128)(2,1)S(1)}, bf16[128,256]{1,0:T(8,128)(2,1)}, u32[]{:S(2)}) copy-start(bf16[128,256]{1,0:T(8,128)(2,1)} %param.21) | copy-start | bytes 196612
  7.2 87.3 %all-to-all-start = ((bf16[32,128,256]{2,1,0:T(8,128)(2,1)}), bf16[32,128,256]{2,1,0:T(8,128)(2,1)S(1)}, u32[]{:S(2)}, u32[]{:S(2)}) async-start(bf16[32,128,256]{2,1,0:T(8,128)(2,1)} %param.15), calls=%async_computation | async-start | bytes 4194304 | tf_op jit(solution)/shard_map/all_to_all | solution.py:942
  14.5 241.8 %all-gather.3.cloned.1.call-start = ((), (), s32[]{:S(2)}) async-start(), calls=%async_computation.8 | async-start | bytes 19464192 | tf_op jit(solution)/shard_map/all_gather | solution.py:945
  15.3 76.5 %copy-start.13 = (bf16[128,256]{1,0:T(8,128)(2,1)S(1)}, bf16[128,256]{1,0:T(8,128)(2,1)}, u32[]{:S(2)}) copy-start(bf16[128,256]{1,0:T(8,128)(2,1)} %param.23) | copy-start | bytes 196612
  15.3 76.5 %copy-start.19 = (bf16[3,256]{1,0:T(4,128)(2,1)S(1)}, bf16[3,256]{1,0:T(4,128)(2,1)}, u32[]{:S(2)}) copy-start(bf16[3,256]{1,0:T(4,128)(2,1)} %param.24) | copy-start | bytes 4612
  15.3 78.3 %copy-start.9 = (bf16[128,1024]{1,0:T(8,128)(2,1)S(1)}, bf16[128,1024]{1,0:T(8,128)(2,1)}, u32[]{:S(2)}) copy-start(bf16[128,1024]{1,0:T(8,128)(2,1)} %param.28) | copy-start | bytes 786436
  15.3 78.3 %copy-start.10 = (bf16[128,1024]{1,0:T(8,128)(2,1)S(1)}, bf16[128,1024]{1,0:T(8,128)(2,1)}, u32[]{:S(2)}) copy-start(bf16[128,1024]{1,0:T(8,128)(2,1)} %param.26) | copy-start | bytes 786436
  15.3 78.3 %copy-start.14 = (bf16[128,256]{1,0:T(8,128)(2,1)S(1)}, bf16[128,256]{1,0:T(8,128)(2,1)}, u32[]{:S(2)}) copy-start(bf16[128,256]{1,0:T(8,128)(2,1)} %param.25) | copy-start | bytes 196612
  15.3 79.2 %copy-start.18 = (s32[2047]{0:T(1024)S(1)}, s32[2047]{0:T(1024)}, u32[]{:S(2)}) copy-start(s32[2047]{0:T(1024)} %param.19) | copy-start | bytes 24568
  91.7 3.0 copy-start.17
  91.7 4.3 copy-start.21
  91.7 4.3 copy-start.22
  94.5 33.6 %copy-start.8 = (bf16[32,128,256]{2,1,0:T(8,128)(2,1)}, bf16[32,128,256]{2,1,0:T(8,128)(2,1)S(1)}, u32[]{:S(2)}) copy-start(bf16[32,128,256]{2,1,0:T(8,128)(2,1)S(1)} %all-to-all-done) | copy-start | bytes 6291460
  128.9 115.0 %all-to-all-start.1 = ((bf16[32,128,256]{2,1,0:T(8,128)(2,1)}), bf16[32,128,256]{2,1,0:T(8,128)(2,1)}, u32[]{:S(2)}, u32[]{:S(2)}) async-start(bf16[32,128,256]{2,1,0:T(8,128)(2,1)} %param.16), calls=%async_computation.1 | async-start | bytes 4194304 | tf_op jit(solution)/shard_map/all_to_all | solution.py:942
  135.7 347.2 %reduce-scatter.3.cloned.1.call-start = ((), (), s32[]{:S(2)}) async-start(), calls=%async_computation.6 | async-start | bytes 21233664 | tf_op jit(solution)/shard_map/reduce_scatter | solution.py:971
  165.5 1.0 copy-start.5
  242.6 1.3 copy-start.3
  353.2 1.3 copy-start.4
  354.5 123.5 %all-to-all-start.2 = ((bf16[32,128,256]{2,1,0:T(8,128)(2,1)}), bf16[32,128,256]{2,1,0:T(8,128)(2,1)S(1)}, u32[]{:S(2)}, u32[]{:S(2)}) async-start(bf16[32,128,256]{2,1,0:T(8,128)(2,1)} %bitcast.40), calls=%async_computation.2 | async-start | bytes 4194304 | tf_op jit(solution)/shard_map/all_to_all | solution.py:942
  358.1 247.4 %reduce-scatter.5.cloned.1.call-start = ((), (), s32[]{:S(2)}) async-start(), calls=%async_computation.7 | async-start | bytes 2949120 | tf_op jit(solution)/shard_map/reduce_scatter | solution.py:974
  478.0 17.0 %copy-start.6 = (bf16[32,128,256]{2,1,0:T(8,128)(2,1)}, bf16[32,128,256]{2,1,0:T(8,128)(2,1)S(1)}, u32[]{:S(2)}) copy-start(bf16[32,128,256]{2,1,0:T(8,128)(2,1)S(1)} %all-to-all-done.2) | copy-start | bytes 6291460
  495.0 4.6 copy-start.12
  495.0 4.7 copy-start.11
  495.0 110.5 %all-to-all-start.3 = ((bf16[32,128,256]{2,1,0:T(8,128)(2,1)}), bf16[32,128,256]{2,1,0:T(8,128)(2,1)}, u32[]{:S(2)}, u32[]{:S(2)}) async-start(bf16[32,128,256]{2,1,0:T(8,128)(2,1)} %bitcast.11), calls=%async_computation.4 | async-start | bytes 4194304 | tf_op jit(solution)/shard_map/all_to_all | solution.py:942
  524.8 3.2 copy-start.2
  605.5 3.1 copy-start.7
  609.9 6.5 %copy-start.1 = (bf16[64,1024]{1,0:T(8,128)(2,1)S(1)}, bf16[64,1024]{1,0:T(8,128)(2,1)}, u32[]{:S(2)}) copy-start(bf16[64,1024]{1,0:T(8,128)(2,1)} %param.20) | copy-start | bytes 393220
Sparse Core Ops, SparseCore 0:
  94.7 161.6 all-gather.2
  354.6 128.2 reduce-scatter.2
  485.2 75.1 reduce-scatter.4

commit v5 on v4

--- a/solution.py
+++ b/solution.py
@@ -12,7 +12,6 @@
 HEAD = 64
 B = 128
 SR = 16
-UN = 8
 NT = (((1,), (1,)), ((), ()))
 
 
@@ -132,19 +131,55 @@
     )(length, qkv, qkv, qkv, far, far)
 
 
+FAR = 3
+
+
 def unskew(x, a8):
-    nb = x.shape[1]//B
-    sub = lax.broadcasted_iota(jnp.int32,(8,128),0)
-    lane = lax.broadcasted_iota(jnp.int32,(8,128),1)
-    keep = lane >= (127-a8) - sub
-    idx=(lane-(127-a8)+sub)&127
-    rot=[jnp.take_along_axis(x[:,t*128:t*128+128], idx, axis=1) for t in range(nb)]
-    zero = jnp.zeros((8,128), x.dtype)
-    return jnp.concatenate([jnp.where(keep, rot[t] if t<nb else zero, rot[t-1] if t>0 else zero) for t in range(nb+1)], axis=1)
+    nb = x.shape[1] // B
+    sub = lax.broadcasted_iota(jnp.int32, (8, 128), 0)
+    lane = lax.broadcasted_iota(jnp.int32, (8, 128), 1)
+    keep = lane >= (127 - a8) - sub
+    idx = (lane - (127 - a8) + sub) & 127
+    rot = [jnp.take_along_axis(x[:, t * 128 : t * 128 + 128], idx, axis=1) for t in range(nb)]
+    zero = jnp.zeros((8, 128), x.dtype)
+    return jnp.concatenate(
+        [jnp.where(keep, rot[t] if t < nb else zero, rot[t - 1] if t > 0 else zero) for t in range(nb + 1)], axis=1
+    )
+
+
+def fold_tiles(x, lo, hi):
+    return sum(x[:, t * 128 : t * 128 + 128] for t in range(lo, hi))
+
+
+def place_back(rows8, d_ref, a, b, nb):
+    lo, hi = max(0, b - FAR), min(nb, b + FAR + 1)
+    near = jnp.concatenate([unskew(x[:, lo * 128 : hi * 128], a + 8 * n) for n, x in enumerate(rows8)], axis=0)
+    d_ref[a : a + SR, 256 : 256 + near.shape[1]] = near.astype(jnp.bfloat16)
+    if lo > 0:
+        far = jnp.concatenate([fold_tiles(x, 0, lo) for x in rows8], axis=0)
+        d_ref[a : a + SR, 0:128] = far.astype(jnp.bfloat16)
+    if hi < nb:
+        far = jnp.concatenate([fold_tiles(x, hi, nb) for x in rows8], axis=0)
+        d_ref[a : a + SR, 128:256] = far.astype(jnp.bfloat16)
+
+
+def window_products(d_ref, table_ref, ends_ref, e, lhs, acc_ref, sums_ref, rows, b, nb):
+    lo, hi = max(0, b - FAR), min(nb, b + FAR + 1)
+    base, size = (nb - 1 - b + lo) * B, (hi - lo + 1) * B
+    near = d_ref[:, 256 : 256 + size]
+    out = dotnn(near, table_ref[base : base + size, :])
+    acc_ref[rows, base : base + size] += dotnn(lhs, near)
+    for there, k in ((lo > 0, 0), (hi < nb, 1)):
+        if there:
+            far = d_ref[:, k * 128 : k * 128 + 128]
+            out = out + dotnn(far, ends_ref[e + k])
+            sums_ref[e + k, rows, :] += dotnn(lhs, far)
+    return out
+
 
 def bwd_kernel(p_ref, q_ref, k_ref, v_ref, do_ref, ctx_ref, li_ref, kf_ref, qf_ref,
                dq_ref, dk_ref, dv_ref, dkf_ref, dqf_ref, sums_ref,
-               dox_ref, dot_ref, qt_ref, kt_ref, vx_ref, ds_ref, d0, d1, akf, aqf, *, L, scale):
+               dox_ref, dot_ref, qt_ref, kt_ref, vx_ref, ds_ref, d0, d1, akf, aqf, ends, far, *, L, scale):
     W = L + B
     nb = L // B
     dd=(d0,d1)
@@ -165,37 +200,51 @@
     kt_ref[...] = k_ref[...].T
     akf[...] = jnp.zeros_like(akf)
     aqf[...] = jnp.zeros_like(aqf)
-    def iblock(b, sq):
-        r0 = pl.multiple_of(b*B, B)
-        base = pl.multiple_of(L - B - b*B, B)
-        outs=[]
+    far[...] = jnp.zeros_like(far)
+    last = 2 * L - 2
+    for e, table in ((0, kf_ref), (2, qf_ref)):
+        ends[e] = jnp.broadcast_to(table[0:1, :], (128, 128))
+        ends[e + 1] = jnp.broadcast_to(table[last : last + 1, :], (128, 128))
+    sq = jnp.zeros((8, 128), jnp.float32)
+    for b in range(nb):
+        r0 = b * B
+        outs = []
         for h in range(2):
-            dp = dotnt(dox_ref[h, pl.ds(r0,B), :], vx_ref[h])
+            rows = slice(h * 64, h * 64 + 64)
+            dp = dotnt(dox_ref[h, r0 : r0 + B, :], vx_ref[h])
             for a in range(0, B, SR):
-                ds = p_ref[h, pl.ds(r0+a,SR), :].astype(jnp.float32) * dp[a:a+SR]
-                ds_ref[h, pl.ds(r0+a,SR), :] = ds.astype(jnp.bfloat16)
-                dd[h][a:a+SR, :] = jnp.concatenate([unskew(ds[s:s+8], a+s) for s in range(0,SR,8)],axis=0).astype(jnp.bfloat16)
-            outs.append(dotnn(ds_ref[h, pl.ds(r0,B), :], k_ref[...]) + dotnn(dd[h][...], kf_ref[pl.ds(base, W), :]))
-            akf[h*64:h*64+64, pl.ds(base, W)] += dotnn(qt_ref[h*64:h*64+64, pl.ds(r0,B)], dd[h][...])
+                ds = p_ref[h, r0 + a : r0 + a + SR, :].astype(jnp.float32) * dp[a : a + SR]
+                ds_ref[h, r0 + a : r0 + a + SR, :] = ds.astype(jnp.bfloat16)
+                place_back([ds[s : s + 8] for s in range(0, SR, 8)], dd[h], a, b, nb)
+            outs.append(
+                dotnn(ds_ref[h, r0 : r0 + B, :], k_ref[...])
+                + window_products(dd[h], kf_ref, ends, 0, qt_ref[rows, r0 : r0 + B], akf, far, rows, b, nb)
+            )
         dq = jnp.where(mine[0], outs[0], outs[1]) * scale
-        dq_ref[pl.ds(r0,B),:] = dq.astype(jnp.bfloat16)
-        return sq + jnp.sum(dq.reshape(B//8,8,128), axis=0)
-    sq = lax.fori_loop(0, nb, iblock, jnp.zeros((8,128),jnp.float32), unroll=UN)
-    def jblock(b, sk):
-        r0 = pl.multiple_of(b*B, B)
-        base = pl.multiple_of(L - B - b*B, B)
-        outs=[]
+        dq_ref[r0 : r0 + B, :] = dq.astype(jnp.bfloat16)
+        sq = sq + jnp.sum(dq.reshape(B // 8, 8, 128), axis=0)
+    sk = jnp.zeros((8, 128), jnp.float32)
+    for b in range(nb):
+        r0 = b * B
+        outs = []
         for h in range(2):
-            dst = ds_ref[h, :, pl.ds(r0,B)].T
+            rows = slice(h * 64, h * 64 + 64)
+            dst = ds_ref[h, :, r0 : r0 + B].T
             for a in range(0, B, SR):
-                x = dst[a:a+SR].astype(jnp.float32)
-                dd[h][a:a+SR, :] = jnp.concatenate([unskew(x[s:s+8], a+s) for s in range(0,SR,8)],axis=0).astype(jnp.bfloat16)
-            outs.append(dotnn(dst, q_ref[...]) + dotnn(dd[h][...], qf_ref[pl.ds(base, W), :]))
-            aqf[h*64:h*64+64, pl.ds(base, W)] += dotnn(kt_ref[h*64:h*64+64, pl.ds(r0,B)], dd[h][...])
+                x = dst[a : a + SR].astype(jnp.float32)
+                place_back([x[s : s + 8] for s in range(0, SR, 8)], dd[h], a, b, nb)
+            outs.append(
+                dotnn(dst, q_ref[...])
+                + window_products(dd[h], qf_ref, ends, 2, kt_ref[rows, r0 : r0 + B], aqf, far, rows, b, nb)
+            )
         dk = jnp.where(mine[0], outs[0], outs[1]) * scale
-        dk_ref[pl.ds(r0,B),:] = dk.astype(jnp.bfloat16)
-        return sk + jnp.sum(dk.reshape(B//8,8,128), axis=0)
-    sk = lax.fori_loop(0, nb, jblock, jnp.zeros((8,128),jnp.float32), unroll=UN)
+        dk_ref[r0 : r0 + B, :] = dk.astype(jnp.bfloat16)
+        sk = sk + jnp.sum(dk.reshape(B // 8, 8, 128), axis=0)
+    for e, acc in ((0, akf), (2, aqf)):
+        for k, at in ((0, 0), (1, last)):
+            tile = at // 128 * 128
+            total = jnp.sum(far[e + k], axis=1, keepdims=True)
+            acc[:, tile : tile + 128] += jnp.where(lane == at - tile, total, 0.0)
     dvt = jnp.concatenate([dotnn(dot_ref[h*64:h*64+64,:], p_ref[h]) for h in range(2)], axis=0)
     dv = dvt.T
     dv_ref[...] = dv.astype(jnp.bfloat16)
@@ -223,8 +272,9 @@
         scratch_shapes=[pltpu.VMEM((2, L, 128), bf)]
         + [pltpu.VMEM((128, L), bf)] * 3
         + [pltpu.VMEM((2, L, 128), bf), pltpu.VMEM((2, L, L), bf)]
-        + [pltpu.VMEM((B, L + B), bf)] * 2
-        + [pltpu.VMEM((128, 2 * L), jnp.float32)] * 2,
+        + [pltpu.VMEM((B, L + 3 * B), bf)] * 2
+        + [pltpu.VMEM((128, 2 * L), jnp.float32)] * 2
+        + [pltpu.VMEM((4, 128, 128), bf), pltpu.VMEM((4, 128, 128), jnp.float32)],
         out_shape=[jax.ShapeDtypeStruct((L, C), bf)] * 3
         + [jax.ShapeDtypeStruct((C, 2 * L), bf)] * 2
         + [jax.ShapeDtypeStruct((24, C), jnp.float32)],
@@ -885,7 +935,7 @@
     dma = lambda *k: pltpu.SemaphoreType.DMA(k)
     return pl.pallas_call(
         functools.partial(reduce_kernel, tn=tn, gn=gn, keep=keep),
-        in_specs=[pl.BlockSpec(memory_space=pl.ANY)],
+        in_specs=[pl.BlockSpec(memory_space=pltpu.VMEM)],
         out_specs=[pl.BlockSpec(memory_space=pltpu.VMEM)] * 5,
         out_shape=[jax.ShapeDtypeStruct((keep // 3, dt), f32)] * 3
         + [
@@ -970,8 +1020,7 @@
     payload, dctx = merge_back(dattn, ctx, second, payload)
     wide_grads = lax.psum_scatter(payload, "dp", scatter_dimension=0, tiled=False)
     dq, dk, dv, dkf, dqf, sums = attn_bwd(probs, qkv, dctx, ctx, inv, far, scale=scale)
-    dq, out, wide_grads = lax.optimization_barrier((dq, out, wide_grads))
-    wide_grads = lax.psum_scatter(wide_grads, "tensor", scatter_dimension=0, tiled=False)
+    dq, out = lax.optimization_barrier((dq, out))
     ff = hidden.shape[2]
     small = jnp.concatenate(
         [
@@ -986,7 +1035,8 @@
     small = small.reshape(sr, tn, dt).transpose(1, 0, 2)[:, None]
     small = jnp.pad(small, ((0, 0), (0, gn - 1), (0, 0), (0, 0)))
     dx = input_back(dattn, dq, dk, dv, first, later)
-    dx, dq = lax.optimization_barrier((dx, dq))
+    dx, dq, wide_grads = lax.optimization_barrier((dx, dq, wide_grads))
+    wide_grads = lax.psum_scatter(wide_grads, "tensor", scatter_dimension=0, tiled=False)
     pay = tail(x, rel, hot, dq, dk, dv, dqf, dkf, sums, first, small, first_shift)
     grad_in = swap(dx.reshape(count, lg, dt))
     wide_grads = wide_grads.astype(f32)

time: 632 us -> 629 us (level); the launches traced: 623 us -> 627 us
  Pallas kernels: 541 us -> 548 us
    pallas_call x1, Pallas kernels: 75.6 us -> 85.7 us  [reduce_all(): pl.pallas_call(functools.partial(reduce_kernel, tn=tn, gn=gn, keep=keep),...]
    pallas_call x1, Pallas kernels: 120 us -> 110 us  [attn_bwd(): pl.pallas_call(functools.partial(bwd_kernel, L=L, scale=scale), grid=(C /...]
where the time goes in v5:
time: 629 us; the launch traced here: 627 us
  Pallas kernels  548 us (87%)
  starting transfers between devices  22.6 us (4%)
  local copies, waits for them, and re-layouts  22.2 us (4%)
  waiting for transfers between devices  14.3 us (2%)
  between operations  14.3 us (2%)
    pallas_call x1, Pallas kernels, attn_bwd(): pl.pallas_call(functools.partial(bwd_kernel, L=L, scale=scale), grid=(C /...  110 us
    pallas_call x2, Pallas kernels, gather_all(): pl.pallas_call(functools.partial(gather_kernel, tn=tn, gn=gn, cuts=cuts),...  108 us
    pallas_call x1, Pallas kernels, middle(): pl.pallas_call(middle_kernel, grid=(2 * tn,), in_specs=[pl.BlockSpec(memo...  93 us
    pallas_call x1, Pallas kernels, reduce_all(): pl.pallas_call(functools.partial(reduce_kernel, tn=tn, gn=gn, keep=keep),...  85.7 us
    pallas_call x1, Pallas kernels, attn_fwd(): pl.pallas_call(functools.partial(fwd_kernel, L=L, scale=scale), grid_spec...  76.1 us
    pallas_call x1, Pallas kernels, project(): pl.pallas_call(project_kernel, grid=(tn, 3), in_specs=[spec((gn, tn, lg,...  29.1 us
    pallas_call x1, Pallas kernels, tail(): pl.pallas_call(functools.partial(tail_kernel, first_shift=first_shift), g...  24.6 us
    all_to_all x4, starting transfers between devices, swap(): return lax.all_to_all(a, seq_axes, split_axis=0, concat_axis=0, tiled=True)  22.5 us
  transfers between devices with their start and end apart: 7, of which 2 were waited for; matrix products, arithmetic and copies ran while one was open for 2% of the time, Pallas kernels for 71%

profile of v5, /device:TPU:0, one launch (start us, length us, event | category | flops | bytes accessed | tf_op | source)
XLA Modules:
  0.0 626.8 jit_solution(13710414573202484413)
XLA Ops:
  7.2 0.0 copy-start
  7.2 7.3 %all-to-all-start = ((bf16[32,128,256]{2,1,0:T(8,128)(2,1)}), bf16[32,128,256]{2,1,0:T(8,128)(2,1)S(1)}, u32[]{:S(2)}, u32[]{:S(2)}) async-start(bf16[32,128,256]{2,1,0:T(8,128)(2,1)} %param.15), calls=%async_computation | async-start | bytes 4194304 | tf_op jit(solution)/shard_map/all_to_all | solution.py:992
  14.5 0.0 all-gather.3.cloned.1.call-start
  14.6 0.7 maximum_bitcast_fusion.src_ref
  15.3 0.0 copy-start.14
  15.3 0.0 copy-start.18
  15.3 76.3 %shard_map.238.wa_ref.w_ref = bf16[8,4,256,256]{3,2,1,0:T(8,128)(2,1)} custom-call(bf16[1,256,256]{2,1,0:T(8,128)(2,1)} %maximum_bitcast_fusion.src_ref), custom_call_target="tpu_custom_call" | custom-call | bytes 33554432 | tf_op jit(solution)/shard_map/pallas_call | solution.py:807
  91.7 0.0 copy-start.17
  91.7 0.0 copy-start.21
  91.7 0.0 copy-start.22
  91.8 1.9 concatenate.16
  93.6 0.9 pad_maximum_fusion
  94.5 0.0 all-to-all-done
  94.5 0.0 all-gather.3.cloned.1.call-update
  94.6 0.1 reverse
  94.6 0.1 slice.43
  94.7 0.9 convert_element_type.21.vec_ref
  95.6 0.1 pad_add_fusion
  95.7 0.4 copy.28.pl_ref
  96.1 0.6 fusion
  96.7 31.5 %shard_map.239.rel4_ref.wb_ref = bf16[8,4,200,256]{3,2,1,0:T(8,128)(2,1)} custom-call(bf16[1,200,256]{2,1,0:T(8,128)(2,1)} %bitcast.41), custom_call_target="tpu_custom_call" | custom-call | bytes 26214400 | tf_op jit(solution)/shard_map/pallas_call | solution.py:807
  128.2 0.7 bitcast_convert_fusion.1
  128.9 6.8 %all-to-all-start.1 = ((bf16[32,128,256]{2,1,0:T(8,128)(2,1)}), bf16[32,128,256]{2,1,0:T(8,128)(2,1)}, u32[]{:S(2)}, u32[]{:S(2)}) async-start(bf16[32,128,256]{2,1,0:T(8,128)(2,1)} %param.16), calls=%async_computation.1 | async-start | bytes 4194304 | tf_op jit(solution)/shard_map/all_to_all | solution.py:992
  135.7 0.0 reduce-scatter.3.cloned.1.call-start
  135.8 0.6 reshape.65.hb_ref
  136.4 29.1 %shard_map.240 = (bf16[3,1024,1024]{2,1,0:T(8,128)(2,1)}, bf16[2,2048,1024]{2,1,0:T(8,128)(2,1)}, bf16[1024,1024]{1,0:T(8,128)(2,1)}, bf16[512,1024]{1,0:T(8,128)(2,1)S(1)}, bf16[2048,512]{1,0:T(8,128)(2,1)}) custom-call(bf16[8,4,128,256]{3,2,1,0:T(8,128)(2,1)} %bitcast.39, bf16[8,4,200,256]{3,2,1,0:T(8,128)(2,1)} %shard_map.239.rel4_ref.wb_ref, ...), custom_call_target="tpu_custom_call" | custom-call | flops 14000000000 | bytes 30000000 | tf_op jit(solution)/shard_map/pallas_call | solution.py:338
  165.5 1.0 copy-done.5
  166.4 76.1 %shard_map.241 = (bf16[1024,1024]{1,0:T(8,128)(2,1)S(1)}, bf16[16,1024,1024]{2,1,0:T(8,128)(2,1)}, f32[1024,1024]{1,0:T(8,128)}) custom-call(s32[1]{0:T(128)} %bitcast.len_ref, bf16[3,1024,1024]{2,1,0:T(8,128)(2,1)} %get-tuple-element.51.q_ref.k_ref.v_ref, bf16[3,1024,1024]{2,1,0:T(8,128)(2,1)} %get-tuple-element.51.q_ref.k_ref.v_ref, ...), custom_call_target="tpu_custom_call" | custom-call | flops 80000000000 | bytes 60000000 | tf_op jit(solution)/shard_map/pallas_call | solution.py:108
  242.6 1.3 copy-done.3
  243.9 0.0 all-to-all-done.1
  243.9 12.4 %all-gather.3.cloned.1.call-done = bf16[4096,2304]{1,0:T(8,128)(2,1)} async-done(((bf16[128,2304]{1,0:T(8,128)(2,1)}), bf16[4096,2304]{1,0:T(8,128)(2,1)}) %all-gather.3.cloned.1.call-update) | async-done | bytes 18874384 | tf_op jit(solution)/shard_map/all_gather | solution.py:995
  256.3 93.0 %shard_map.242 = (bf16[8,4,128,256]{3,2,1,0:T(8,128)(2,1)}, bf16[8,4,128,2304]{3,2,1,0:T(8,128)(2,1)}, f32[4,8,1024]{2,1,0:T(8,128)}, bf16[1024,1024]{1,0:T(8,128)(2,1)}, f32[48,1024]{1,0:T(8,128)}) custom-call(bf16[1024,1024]{1,0:T(8,128)(2,1)} %copy-done.3, bf16[1024,1024]{1,0:T(8,128)(2,1)} %get-tuple-element.55.x_ref, ...), custom_call_target="tpu_custom_call" | custom-call | flops 74999996416 | bytes 100000000 | tf_op jit(solution)/shard_map/pallas_call | solution.py:492
  349.4 8.9 %shard_map.243 = (bf16[8,4,128,2304]{3,2,1,0:T(8,128)(2,1)}, bf16[1024,1024]{1,0:T(8,128)(2,1)S(1)}) custom-call(bf16[1024,1024]{1,0:T(8,128)(2,1)} %get-tuple-element.58.da_ref, bf16[1024,1024]{1,0:T(8,128)(2,1)} %copy-done.3, bf16[4,8,128,2304]{3,2,1,0:T(8,128)(2,1)} %bitcast.37, ...), custom_call_target="tpu_custom_call", output_to_operand_aliasing={{0}: (3, {})} | custom-call | flops 4000000000 | bytes 10000000 | tf_op jit(solution)/shard_map/pallas_call | solution.py:550
  358.3 1.3 copy-done.4
  359.6 0.0 reduce-scatter.3.cloned.1.call-update
  359.6 3.6 all-to-all-start.2
  363.2 0.0 reduce-scatter.5.cloned.1.call-start
  363.3 109.9 %shard_map.244 = (bf16[1024,1024]{1,0:T(8,128)(2,1)}, bf16[1024,1024]{1,0:T(8,128)(2,1)}, bf16[1024,1024]{1,0:T(8,128)(2,1)}, bf16[1024,2048]{1,0:T(8,128)(2,1)}...) custom-call(bf16[16,1024,1024]{2,1,0:T(8,128)(2,1)} %get-tuple-element.53.p_ref, ...), custom_call_target="tpu_custom_call" | custom-call | flops 120000004096 | bytes 80000000 | tf_op jit(solution)/shard_map/pallas_call | solution.py:265
  473.1 0.0 all-to-all-done.2
  473.2 0.0 copy-start.6
  473.2 13.0 %shard_map.245 = bf16[8,4,128,256]{3,2,1,0:T(8,128)(2,1)} custom-call(bf16[1024,1024]{1,0:T(8,128)(2,1)} %get-tuple-element.58.da_ref, bf16[1024,1024]{1,0:T(8,128)(2,1)} %get-tuple-element.72.dq_ref, bf16[1024,1024]{1,0:T(8,128)(2,1)} %get-tuple-element.66.dk_ref, bf16[1024,1024]{1,0:T(8,128)(2,1)} %get-tuple-element.67.dv_ref, ...), custom_call_target="tpu_custom_call" | custom-call | flops 7000000000 | bytes 20000000 | tf_op jit(solution)/shard_map/pallas_call | solution.py:602
  486.2 1.8 reduce-scatter.3.cloned.1.call-done
  488.0 0.0 reduce-scatter.5.cloned.1.call-update
  488.0 0.0 copy-start.12
  488.0 0.0 copy-start.11
  488.0 4.7 all-to-all-start.3
  492.9 0.1 bitcast_reduce_fusion
  492.9 0.9 pad.9.small_ref
  493.8 24.6 %shard_map.246.pay_ref = bf16[8,4,464,256]{3,2,1,0:T(8,128)(2,1)} custom-call(bf16[1024,1024]{1,0:T(8,128)(2,1)} %get-tuple-element.55.x_ref, bf16[512,1024]{1,0:T(8,128)(2,1)} %copy-done.5, bf16[2048,512]{1,0:T(8,128)(2,1)} %get-tuple-element.71.hot_ref, bf16[1024,1024]{1,0:T(8,128)(2,1)} %get-tuple-element.72.dq_ref, ...), custom_call_target="tpu_custom_call" | custom-call | flops 12999999488 | bytes 40000000 | tf_op jit(solution)/shard_map/pallas_call | solution.py:673
  518.4 3.2 copy-done.2
  521.6 85.7 %shard_map.247 = (f32[128,256]{1,0:T(8,128)S(1)}, f32[128,256]{1,0:T(8,128)S(1)}, f32[128,256]{1,0:T(8,128)S(1)}, f32[512,1024]{1,0:T(8,128)S(1)}, f32[16,1024]{1,0:T(8,128)S(1)}) custom-call(bf16[8,4,464,256]{3,2,1,0:T(8,128)(2,1)S(1)} %copy-done.2), custom_call_target="tpu_custom_call" | custom-call | bytes 200000000 | tf_op jit(solution)/shard_map/pallas_call | solution.py:936
  607.4 0.6 slice.30
  608.0 0.6 slice.35
  608.6 0.6 copy.35
  609.2 0.0 all-to-all-done.3
  609.2 1.3 bitcast_convert_fusion
  610.5 0.7 slice.38
  611.2 1.1 fusion.1
  612.3 1.3 copy.43
  613.6 3.2 copy.44
  616.8 1.3 copy.45
  618.1 0.7 copy.46
  618.7 0.7 copy.47
  619.4 0.7 copy.48
  (43 shorter events, 0.2 us)
Async XLA Ops:
  7.2 84.5 %copy-start = (bf16[64,1024]{1,0:T(8,128)(2,1)S(1)}, bf16[64,1024]{1,0:T(8,128)(2,1)}, u32[]{:S(2)}) copy-start(bf16[64,1024]{1,0:T(8,128)(2,1)} %param.20) | copy-start | bytes 393220
  7.2 7.4 %copy-start.20 = (bf16[1024]{0:T(1024)(128)(2,1)S(1)}, bf16[1024]{0:T(1024)(128)(2,1)}, u32[]{:S(2)}) copy-start(bf16[1024]{0:T(1024)(128)(2,1)} %param.27) | copy-start | bytes 6148
  7.2 7.4 %copy-start.15 = (bf16[128,256]{1,0:T(8,128)(2,1)S(1)}, bf16[128,256]{1,0:T(8,128)(2,1)}, u32[]{:S(2)}) copy-start(bf16[128,256]{1,0:T(8,128)(2,1)} %param.22) | copy-start | bytes 196612
  7.2 7.4 %copy-start.16 = (bf16[128,256]{1,0:T(8,128)(2,1)S(1)}, bf16[128,256]{1,0:T(8,128)(2,1)}, u32[]{:S(2)}) copy-start(bf16[128,256]{1,0:T(8,128)(2,1)} %param.21) | copy-start | bytes 196612
  7.2 87.3 %all-to-all-start = ((bf16[32,128,256]{2,1,0:T(8,128)(2,1)}), bf16[32,128,256]{2,1,0:T(8,128)(2,1)S(1)}, u32[]{:S(2)}, u32[]{:S(2)}) async-start(bf16[32,128,256]{2,1,0:T(8,128)(2,1)} %param.15), calls=%async_computation | async-start | bytes 4194304 | tf_op jit(solution)/shard_map/all_to_all | solution.py:992
  14.5 241.8 %all-gather.3.cloned.1.call-start = ((), (), s32[]{:S(2)}) async-start(), calls=%async_computation.8 | async-start | bytes 19464192 | tf_op jit(solution)/shard_map/all_gather | solution.py:995
  15.3 76.5 %copy-start.13 = (bf16[128,256]{1,0:T(8,128)(2,1)S(1)}, bf16[128,256]{1,0:T(8,128)(2,1)}, u32[]{:S(2)}) copy-start(bf16[128,256]{1,0:T(8,128)(2,1)} %param.23) | copy-start | bytes 196612
  15.3 76.5 %copy-start.19 = (bf16[3,256]{1,0:T(4,128)(2,1)S(1)}, bf16[3,256]{1,0:T(4,128)(2,1)}, u32[]{:S(2)}) copy-start(bf16[3,256]{1,0:T(4,128)(2,1)} %param.24) | copy-start | bytes 4612
  15.3 78.3 %copy-start.9 = (bf16[128,1024]{1,0:T(8,128)(2,1)S(1)}, bf16[128,1024]{1,0:T(8,128)(2,1)}, u32[]{:S(2)}) copy-start(bf16[128,1024]{1,0:T(8,128)(2,1)} %param.28) | copy-start | bytes 786436
  15.3 78.3 %copy-start.10 = (bf16[128,1024]{1,0:T(8,128)(2,1)S(1)}, bf16[128,1024]{1,0:T(8,128)(2,1)}, u32[]{:S(2)}) copy-start(bf16[128,1024]{1,0:T(8,128)(2,1)} %param.26) | copy-start | bytes 786436
  15.3 78.3 %copy-start.14 = (bf16[128,256]{1,0:T(8,128)(2,1)S(1)}, bf16[128,256]{1,0:T(8,128)(2,1)}, u32[]{:S(2)}) copy-start(bf16[128,256]{1,0:T(8,128)(2,1)} %param.25) | copy-start | bytes 196612
  15.3 79.2 %copy-start.18 = (s32[2047]{0:T(1024)S(1)}, s32[2047]{0:T(1024)}, u32[]{:S(2)}) copy-start(s32[2047]{0:T(1024)} %param.19) | copy-start | bytes 24568
  91.7 3.0 copy-start.17
  91.7 4.3 copy-start.21
  91.7 4.3 copy-start.22
  94.5 33.6 %copy-start.8 = (bf16[32,128,256]{2,1,0:T(8,128)(2,1)}, bf16[32,128,256]{2,1,0:T(8,128)(2,1)S(1)}, u32[]{:S(2)}) copy-start(bf16[32,128,256]{2,1,0:T(8,128)(2,1)S(1)} %all-to-all-done) | copy-start | bytes 6291460
  128.9 115.0 %all-to-all-start.1 = ((bf16[32,128,256]{2,1,0:T(8,128)(2,1)}), bf16[32,128,256]{2,1,0:T(8,128)(2,1)}, u32[]{:S(2)}, u32[]{:S(2)}) async-start(bf16[32,128,256]{2,1,0:T(8,128)(2,1)} %param.16), calls=%async_computation.1 | async-start | bytes 4194304 | tf_op jit(solution)/shard_map/all_to_all | solution.py:992
  135.7 352.3 %reduce-scatter.3.cloned.1.call-start = ((), (), s32[]{:S(2)}) async-start(), calls=%async_computation.6 | async-start | bytes 21233664 | tf_op jit(solution)/shard_map/reduce_scatter | solution.py:1021
  165.5 1.0 copy-start.5
  242.6 1.3 copy-start.3
  358.3 1.3 copy-start.4
  359.6 113.6 %all-to-all-start.2 = ((bf16[32,128,256]{2,1,0:T(8,128)(2,1)}), bf16[32,128,256]{2,1,0:T(8,128)(2,1)S(1)}, u32[]{:S(2)}, u32[]{:S(2)}) async-start(bf16[32,128,256]{2,1,0:T(8,128)(2,1)} %bitcast.40), calls=%async_computation.2 | async-start | bytes 4194304 | tf_op jit(solution)/shard_map/all_to_all | solution.py:992
  363.2 246.0 %reduce-scatter.5.cloned.1.call-start = ((), (), s32[]{:S(2)}) async-start(), calls=%async_computation.7 | async-start | bytes 2949120 | tf_op jit(solution)/shard_map/reduce_scatter | solution.py:1039
  473.2 13.0 %copy-start.6 = (bf16[32,128,256]{2,1,0:T(8,128)(2,1)}, bf16[32,128,256]{2,1,0:T(8,128)(2,1)S(1)}, u32[]{:S(2)}) copy-start(bf16[32,128,256]{2,1,0:T(8,128)(2,1)S(1)} %all-to-all-done.2) | copy-start | bytes 6291460
  488.0 4.8 copy-start.12
  488.0 4.8 copy-start.11
  488.0 121.2 %all-to-all-start.3 = ((bf16[32,128,256]{2,1,0:T(8,128)(2,1)}), bf16[32,128,256]{2,1,0:T(8,128)(2,1)}, u32[]{:S(2)}, u32[]{:S(2)}) async-start(bf16[32,128,256]{2,1,0:T(8,128)(2,1)} %bitcast.11), calls=%async_computation.4 | async-start | bytes 4194304 | tf_op jit(solution)/shard_map/all_to_all | solution.py:992
  518.4 3.2 copy-start.2
  609.2 3.1 copy-start.7
  613.6 6.5 %copy-start.1 = (bf16[64,1024]{1,0:T(8,128)(2,1)S(1)}, bf16[64,1024]{1,0:T(8,128)(2,1)}, u32[]{:S(2)}) copy-start(bf16[64,1024]{1,0:T(8,128)(2,1)} %param.20) | copy-start | bytes 393220
Sparse Core Ops, SparseCore 0:
  94.7 161.6 all-gather.2
  359.7 128.2 reduce-scatter.2
  490.3 81.0 reduce-scatter.4

commit v6 on v5

--- a/solution.py
+++ b/solution.py
@@ -481,7 +481,7 @@
 
 def middle(ctx, x, second, hidden_bias, vectors, cot):
     gn, tn, lg, dt = cot.shape
-    per, wide = second.shape[2:]
+    per = second.shape[2]
     L, D = x.shape
     assert L == D
     ff = hidden_bias.shape[2]
@@ -511,7 +511,7 @@
         ],
         out_shape=[
             jax.ShapeDtypeStruct((gn, tn, lg, dt), bf),
-            jax.ShapeDtypeStruct((gn, tn, per, wide), bf),
+            jax.ShapeDtypeStruct((gn, tn, per, 2 * ff), bf),
             jax.ShapeDtypeStruct((tn, 8, ff), f32),
             jax.ShapeDtypeStruct((L, D), bf),
             jax.ShapeDtypeStruct((48, D), f32),
@@ -527,7 +527,7 @@
     )(ctx, x, second, second, second, hidden_bias, vectors, cot)
 
 
-def merge_back_kernel(da_ref, ctx_ref, wm_ref, pay_in, pay_ref, dctx_ref, dat_ref):
+def merge_back_kernel(da_ref, ctx_ref, wm_ref, pay_ref, dctx_ref, dat_ref):
     t = pl.program_id(0)
     L, D = da_ref.shape
     gn, _, per, dt = pay_ref.shape
@@ -541,7 +541,7 @@
     pay_ref[:, 0] = dotnn(dat_ref[...], ctx_ref[...]).astype(jnp.bfloat16).reshape(gn, per, dt)
 
 
-def merge_back(dattn, ctx, second, payload):
+def merge_back(dattn, ctx, second):
     tn, gn, per, wide = second.shape
     L, D = dattn.shape
     dt = D // tn
@@ -554,21 +554,19 @@
             spec((L, D), lambda t: (0, 0), True),
             spec((L, dt), lambda t: (0, t)),
             spec((1, gn, per, dt), lambda t: (t, 0, 0, last)),
-            pl.BlockSpec(memory_space=pl.ANY),
         ],
         out_specs=[
-            spec((gn, 1, per, dt), lambda t: (0, t, 0, last)),
+            spec((gn, 1, per, dt), lambda t: (0, t, 0, 0)),
             spec((L, dt), lambda t: (0, t)),
         ],
         out_shape=[
-            jax.ShapeDtypeStruct((gn, tn, per, wide), bf),
+            jax.ShapeDtypeStruct((gn, tn, per, dt), bf),
             jax.ShapeDtypeStruct((L, D), bf),
         ],
         scratch_shapes=[pltpu.VMEM((D, L), bf)],
-        input_output_aliases={3: 0},
         compiler_params=pltpu.CompilerParams(vmem_limit_bytes=50 << 20),
         cost_estimate=pl.CostEstimate(flops=4 * 10**9, bytes_accessed=10 * 10**6, transcendentals=0),
-    )(dattn, ctx, second, payload)
+    )(dattn, ctx, second)
 
 
 def input_back_kernel(da_ref, dq_ref, dk_ref, dv_ref, wa_ref, wb_ref, dx_ref, acc_ref):
@@ -616,7 +614,7 @@
     )(dattn, dq, dk, dv, first, later)
 
 
-def tail_kernel(x_ref, rel_ref, hot_ref, dq_ref, dk_ref, dv_ref, dqf_ref, dkf_ref, sm_ref, w_ref, small_ref,
+def tail_kernel(x_ref, rel_ref, hot_ref, dq_ref, dk_ref, dv_ref, dqf_ref, dkf_ref, sm_ref, w_ref, small_ref, mg_ref,
                 pay_ref, xt_ref, ra_ref, *, first_shift):
     t = pl.program_id(0)
     L, D = x_ref.shape
@@ -640,7 +638,8 @@
     kp = dotnn(dkf_ref[...], hot_ref[...]).T
     pos = [qp.astype(bf), kp.astype(bf)]
     tops = [dq_ref, dk_ref, dv_ref]
-    rows = 3 * per + rg
+    rows = 4 * per + rg
+    pay_ref[:, t, 3 * per : 4 * per, :] = mg_ref[:, 0]
     pay_ref[:, t, rows : rows + sr, :] = small_ref[0].astype(bf)
     for j in range(3):
         total = jnp.sum(sm_ref[8 * j : 8 * j + 8], axis=0, keepdims=True)
@@ -659,14 +658,14 @@
         for g in range(gn):
             for s in range(tn):
                 cols = slice(s * dt, (s + 1) * dt)
-                pay_ref[g, s, 3 * per : rows, :] = ra_ref[g * rg : (g + 1) * rg, cols].astype(bf)
-
-
-def tail(x, rel, hot, dq, dk, dv, dqf, dkf, sums, first, small, first_shift):
+                pay_ref[g, s, 4 * per : rows, :] = ra_ref[g * rg : (g + 1) * rg, cols].astype(bf)
+
+
+def tail(x, rel, hot, dq, dk, dv, dqf, dkf, sums, first, small, merged, first_shift):
     gn, tn, wide, dt = first.shape
     L, D = x.shape
     spans = rel.shape[0]
-    rows = 3 * D // gn + spans // gn + small.shape[2]
+    rows = 4 * D // gn + spans // gn + small.shape[2]
     bf, f32 = jnp.bfloat16, jnp.float32
     full = lambda shape: spec(shape, lambda t: (0,) * len(shape), True)
     col = lambda: spec((L, dt), lambda t: (0, t))
@@ -680,13 +679,14 @@
             spec((24, dt), lambda t: (0, t)),
             spec((gn, 1, wide, dt), lambda t: (0, t, 0, 0)),
             spec((1,) + small.shape[1:], lambda t: (t, 0, 0, 0)),
+            spec((gn, 1, D // gn, dt), lambda t: (0, t, 0, 0)),
         ],
         out_specs=full((gn, tn, rows, dt)),
         out_shape=jax.ShapeDtypeStruct((gn, tn, rows, dt), bf),
         scratch_shapes=[pltpu.VMEM((D, L + spans), bf), pltpu.VMEM((spans, D), f32)],
         compiler_params=pltpu.CompilerParams(vmem_limit_bytes=56 << 20),
         cost_estimate=pl.CostEstimate(flops=13 * 10**9, bytes_accessed=40 * 10**6, transcendentals=0),
-    )(x, rel, hot, dq, dk, dv, dqf, dkf, sums, first, small)
+    )(x, rel, hot, dq, dk, dv, dqf, dkf, sums, first, small, merged)
 
 
 MESH = pl.DeviceIdType.MESH
@@ -815,13 +815,13 @@
     )(w[None])
 
 
-def reduce_kernel(pay_ref, q_ref, k_ref, v_ref, rel_ref, small_ref, all_ref, acc_ref, rx_ref, ry_ref, rz_ref, rest_ref,
+def reduce_kernel(pay_ref, q_ref, k_ref, v_ref, m_ref, rel_ref, small_ref, all_ref, acc_ref, rx_ref, ry_ref, rz_ref, rest_ref,
                   local, send, recv, *, tn, gn, keep):
     t, g = lax.axis_index("tensor"), lax.axis_index("dp")
     bits = list(range(gn.bit_length() - 1))
     f32, bf = jnp.float32, jnp.bfloat16
     rows = acc_ref.shape[2]
-    per = keep // 3
+    per = keep // 4
     greet(tn, gn)
     wire = Wire(send, recv)
     outer = bits[1:]
@@ -829,7 +829,7 @@
     index = {s: n for n, s in enumerate(masks)}
     half = tn // 2
     plans = [(0, outer), (half, outer[::-1])]
-    grads = (q_ref, k_ref, v_ref)
+    grads = (q_ref, k_ref, v_ref, m_ref)
 
     def reduce_stages(n, lo, hi):
         span = pl.ds(lo, hi - lo)
@@ -895,7 +895,7 @@
             if lo >= keep:
                 rest_ref[0] = total.astype(bf)
             else:
-                for j in range(3):
+                for j in range(4):
                     a, b = max(lo, j * per), min(hi, (j + 1) * per)
                     if a < b:
                         grads[j][a - j * per : b - j * per] = total[a - lo : b - lo]
@@ -935,9 +935,9 @@
     dma = lambda *k: pltpu.SemaphoreType.DMA(k)
     return pl.pallas_call(
         functools.partial(reduce_kernel, tn=tn, gn=gn, keep=keep),
-        in_specs=[pl.BlockSpec(memory_space=pltpu.VMEM)],
-        out_specs=[pl.BlockSpec(memory_space=pltpu.VMEM)] * 5,
-        out_shape=[jax.ShapeDtypeStruct((keep // 3, dt), f32)] * 3
+        in_specs=[pl.BlockSpec(memory_space=pl.ANY)],
+        out_specs=[pl.BlockSpec(memory_space=pltpu.VMEM)] * 6,
+        out_shape=[jax.ShapeDtypeStruct((keep // 4, dt), f32)] * 4
         + [
             jax.ShapeDtypeStruct((spans, tn * dt), f32),
             jax.ShapeDtypeStruct((rows - keep - spans // gn, tn * dt), f32),
@@ -951,7 +951,7 @@
             pltpu.VMEM((1, rows - keep, dt), bf),
             dma(4, m), dma(count), dma(count),
         ],
-        compiler_params=pltpu.CompilerParams(collective_id=number, has_side_effects=True, vmem_limit_bytes=40 << 20),
+        compiler_params=pltpu.CompilerParams(collective_id=number, has_side_effects=True, vmem_limit_bytes=58 << 20),
         cost_estimate=pl.CostEstimate(flops=0, bytes_accessed=200 * 10**6, transcendentals=0),
     )(pay)
 
@@ -1017,10 +1017,11 @@
     ctx, probs, inv = attn_fwd(length, qkv, far, scale=scale)
     y, payload, hidden, dattn, sums12 = middle(ctx, x, second, hidden_bias, vectors, cot)
     out = swap(y.reshape(count, lg, dt))
-    payload, dctx = merge_back(dattn, ctx, second, payload)
     wide_grads = lax.psum_scatter(payload, "dp", scatter_dimension=0, tiled=False)
+    merged, dctx = merge_back(dattn, ctx, second)
     dq, dk, dv, dkf, dqf, sums = attn_bwd(probs, qkv, dctx, ctx, inv, far, scale=scale)
-    dq, out = lax.optimization_barrier((dq, out))
+    dq, out, wide_grads = lax.optimization_barrier((dq, out, wide_grads))
+    wide_grads = lax.psum_scatter(wide_grads, "tensor", scatter_dimension=0, tiled=False)
     ff = hidden.shape[2]
     small = jnp.concatenate(
         [
@@ -1035,12 +1036,11 @@
     small = small.reshape(sr, tn, dt).transpose(1, 0, 2)[:, None]
     small = jnp.pad(small, ((0, 0), (0, gn - 1), (0, 0), (0, 0)))
     dx = input_back(dattn, dq, dk, dv, first, later)
-    dx, dq, wide_grads = lax.optimization_barrier((dx, dq, wide_grads))
-    wide_grads = lax.psum_scatter(wide_grads, "tensor", scatter_dimension=0, tiled=False)
-    pay = tail(x, rel, hot, dq, dk, dv, dqf, dkf, sums, first, small, first_shift)
+    dx, dq = lax.optimization_barrier((dx, dq))
+    pay = tail(x, rel, hot, dq, dk, dv, dqf, dkf, sums, first, small, merged, first_shift)
     grad_in = swap(dx.reshape(count, lg, dt))
     wide_grads = wide_grads.astype(f32)
-    query_grad, key_grad, value_grad, rel_grad, rest = reduce_all(pay, 3 * per, spans, 1)
+    query_grad, key_grad, value_grad, merge_grad, rel_grad, rest = reduce_all(pay, 4 * per, spans, 1)
     return (
         out,
         grad_in,
@@ -1049,10 +1049,10 @@
         key_grad,
         value_grad,
         rest[first_shift : first_shift + 3],
-        wide_grads[:, 2 * ff :],
+        merge_grad,
         wide_grads[:, :ff],
         rest[6:first_shift].reshape(-1),
-        wide_grads[:, ff : 2 * ff],
+        wide_grads[:, ff:],
         rest[:6],
     )
 

time: 629 us -> 620 us (0.986)
  Pallas kernels: 548 us -> 541 us
    pallas_call x1, Pallas kernels: 85.7 us -> 77.4 us  [reduce_all(): pl.pallas_call(functools.partial(reduce_kernel, tn=tn, gn=gn, keep=keep),...]
    unnamed x56 -> x61, local copies, waits for them, and re-layouts: 15.4 us -> 13.9 us
  transfers between devices with their start and end apart: 7 -> 7, of which waited for: 2 -> 1; matrix products, arithmetic and copies ran while one was open for 2% -> 2% of each run, Pallas kernels for 71% -> 72%
where the time goes in v6:
time: 620 us; the launch traced here: 618 us
  Pallas kernels  541 us (87%)
  starting transfers between devices  23.5 us (4%)
  local copies, waits for them, and re-layouts  21.5 us (3%)
  between operations  14.3 us (2%)
  waiting for transfers between devices  13 us (2%)
    pallas_call x1, Pallas kernels, attn_bwd(): pl.pallas_call(functools.partial(bwd_kernel, L=L, scale=scale), grid=(C /...  110 us
    pallas_call x2, Pallas kernels, gather_all(): pl.pallas_call(functools.partial(gather_kernel, tn=tn, gn=gn, cuts=cuts),...  108 us
    pallas_call x1, Pallas kernels, middle(): pl.pallas_call(middle_kernel, grid=(2 * tn,), in_specs=[pl.BlockSpec(memo...  93 us
    pallas_call x1, Pallas kernels, reduce_all(): pl.pallas_call(functools.partial(reduce_kernel, tn=tn, gn=gn, keep=keep),...  77.4 us
    pallas_call x1, Pallas kernels, attn_fwd(): pl.pallas_call(functools.partial(fwd_kernel, L=L, scale=scale), grid_spec...  76.1 us
    pallas_call x1, Pallas kernels, project(): pl.pallas_call(project_kernel, grid=(tn, 3), in_specs=[spec((gn, tn, lg,...  29.1 us
    pallas_call x1, Pallas kernels, tail(): pl.pallas_call(functools.partial(tail_kernel, first_shift=first_shift), g...  25.4 us
    all_to_all x4, starting transfers between devices, swap(): return lax.all_to_all(a, seq_axes, split_axis=0, concat_axis=0, tiled=True)  23.4 us
  transfers between devices with their start and end apart: 7, of which 1 were waited for; matrix products, arithmetic and copies ran while one was open for 2% of the time, Pallas kernels for 72%

profile of v6, /device:TPU:0, one launch (start us, length us, event | category | flops | bytes accessed | tf_op | source)
XLA Modules:
  0.0 618.1 jit_solution(8826639159631018764)
XLA Ops:
  7.2 0.0 copy-start
  7.2 7.3 %all-to-all-start = ((bf16[32,128,256]{2,1,0:T(8,128)(2,1)}), bf16[32,128,256]{2,1,0:T(8,128)(2,1)S(1)}, u32[]{:S(2)}, u32[]{:S(2)}) async-start(bf16[32,128,256]{2,1,0:T(8,128)(2,1)} %param.15), calls=%async_computation | async-start | bytes 4194304 | tf_op jit(solution)/shard_map/all_to_all | solution.py:992
  14.5 0.0 all-gather.3.cloned.1.call-start
  14.6 0.7 maximum_bitcast_fusion.src_ref
  15.3 0.0 copy-start.16
  15.3 0.0 copy-start.20
  15.3 76.3 %shard_map.238.wa_ref.w_ref = bf16[8,4,256,256]{3,2,1,0:T(8,128)(2,1)} custom-call(bf16[1,256,256]{2,1,0:T(8,128)(2,1)} %maximum_bitcast_fusion.src_ref), custom_call_target="tpu_custom_call" | custom-call | bytes 33554432 | tf_op jit(solution)/shard_map/pallas_call | solution.py:807
  91.7 0.0 copy-start.19
  91.7 0.0 copy-start.23
  91.7 0.0 copy-start.24
  91.7 0.0 copy-done
  91.8 1.9 concatenate.16
  93.6 0.0 copy-done.7
  93.6 0.0 copy-done.16
  93.6 0.9 pad_maximum_fusion
  94.5 0.0 all-to-all-done
  94.5 0.0 all-gather.3.cloned.1.call-update
  94.6 0.1 reverse
  94.6 0.1 slice.38
  94.7 0.8 convert_element_type.21.vec_ref
  95.5 0.1 pad_add_fusion
  95.6 0.4 copy.27.pl_ref
  96.0 0.6 fusion
  96.6 31.4 %shard_map.239.rel4_ref.wb_ref = bf16[8,4,200,256]{3,2,1,0:T(8,128)(2,1)} custom-call(bf16[1,200,256]{2,1,0:T(8,128)(2,1)} %bitcast.41), custom_call_target="tpu_custom_call" | custom-call | bytes 26214400 | tf_op jit(solution)/shard_map/pallas_call | solution.py:807
  128.1 0.7 bitcast_convert_fusion.1
  128.8 6.5 %all-to-all-start.1 = ((bf16[32,128,256]{2,1,0:T(8,128)(2,1)}), bf16[32,128,256]{2,1,0:T(8,128)(2,1)}, u32[]{:S(2)}, u32[]{:S(2)}) async-start(bf16[32,128,256]{2,1,0:T(8,128)(2,1)} %param.16), calls=%async_computation.1 | async-start | bytes 4194304 | tf_op jit(solution)/shard_map/all_to_all | solution.py:992
  135.4 0.0 reduce-scatter.3.cloned.1.call-start
  135.4 0.6 reshape.65.hb_ref
  136.1 29.1 %shard_map.240 = (bf16[3,1024,1024]{2,1,0:T(8,128)(2,1)}, bf16[2,2048,1024]{2,1,0:T(8,128)(2,1)}, bf16[1024,1024]{1,0:T(8,128)(2,1)}, bf16[512,1024]{1,0:T(8,128)(2,1)S(1)}, bf16[2048,512]{1,0:T(8,128)(2,1)}) custom-call(bf16[8,4,128,256]{3,2,1,0:T(8,128)(2,1)} %bitcast.39, bf16[8,4,200,256]{3,2,1,0:T(8,128)(2,1)} %shard_map.239.rel4_ref.wb_ref, ...), custom_call_target="tpu_custom_call" | custom-call | flops 14000000000 | bytes 30000000 | tf_op jit(solution)/shard_map/pallas_call | solution.py:338
  165.1 1.0 copy-done.4
  166.1 76.1 %shard_map.241 = (bf16[1024,1024]{1,0:T(8,128)(2,1)S(1)}, bf16[16,1024,1024]{2,1,0:T(8,128)(2,1)}, f32[1024,1024]{1,0:T(8,128)}) custom-call(s32[1]{0:T(128)} %bitcast.len_ref, bf16[3,1024,1024]{2,1,0:T(8,128)(2,1)} %get-tuple-element.52.q_ref.k_ref.v_ref, bf16[3,1024,1024]{2,1,0:T(8,128)(2,1)} %get-tuple-element.52.q_ref.k_ref.v_ref, ...), custom_call_target="tpu_custom_call" | custom-call | flops 80000000000 | bytes 60000000 | tf_op jit(solution)/shard_map/pallas_call | solution.py:108
  242.2 1.3 copy-done.2
  243.5 0.0 all-to-all-done.1
  243.5 12.9 %all-gather.3.cloned.1.call-done = bf16[4096,2304]{1,0:T(8,128)(2,1)} async-done(((bf16[128,2304]{1,0:T(8,128)(2,1)}), bf16[4096,2304]{1,0:T(8,128)(2,1)}) %all-gather.3.cloned.1.call-update) | async-done | bytes 18874384 | tf_op jit(solution)/shard_map/all_gather | solution.py:995
  256.4 93.0 %shard_map.242 = (bf16[8,4,128,256]{3,2,1,0:T(8,128)(2,1)}, bf16[8,4,128,2048]{3,2,1,0:T(8,128)(2,1)}, f32[4,8,1024]{2,1,0:T(8,128)}, bf16[1024,1024]{1,0:T(8,128)(2,1)}, f32[48,1024]{1,0:T(8,128)}) custom-call(bf16[1024,1024]{1,0:T(8,128)(2,1)} %copy-done.2, bf16[1024,1024]{1,0:T(8,128)(2,1)} %get-tuple-element.56.x_ref, ...), custom_call_target="tpu_custom_call" | custom-call | flops 74999996416 | bytes 100000000 | tf_op jit(solution)/shard_map/pallas_call | solution.py:492
  349.5 0.0 reduce-scatter.3.cloned.1.call-update
  349.5 3.5 all-to-all-start.2
  353.0 0.0 reduce-scatter.5.cloned.1.call-start
  353.1 9.7 %shard_map.243 = (bf16[8,4,128,256]{3,2,1,0:T(8,128)(2,1)S(1)}, bf16[1024,1024]{1,0:T(8,128)(2,1)}) custom-call(bf16[1024,1024]{1,0:T(8,128)(2,1)} %get-tuple-element.59.da_ref, bf16[1024,1024]{1,0:T(8,128)(2,1)} %copy-done.2, bf16[4,8,128,2304]{3,2,1,0:T(8,128)(2,1)} %bitcast.37), custom_call_target="tpu_custom_call" | custom-call | flops 4000000000 | bytes 10000000 | tf_op jit(solution)/shard_map/pallas_call | solution.py:550
  362.8 1.3 copy-done.3
  364.1 110.1 %shard_map.244 = (bf16[1024,1024]{1,0:T(8,128)(2,1)}, bf16[1024,1024]{1,0:T(8,128)(2,1)}, bf16[1024,1024]{1,0:T(8,128)(2,1)}, bf16[1024,2048]{1,0:T(8,128)(2,1)}...) custom-call(bf16[16,1024,1024]{2,1,0:T(8,128)(2,1)} %get-tuple-element.54.p_ref, ...), custom_call_target="tpu_custom_call" | custom-call | flops 120000004096 | bytes 80000000 | tf_op jit(solution)/shard_map/pallas_call | solution.py:265
  474.3 0.0 all-to-all-done.2
  474.3 0.0 reduce-scatter.3.cloned.1.call-done
  474.3 0.0 reduce-scatter.5.cloned.1.call-update
  474.3 12.2 %shard_map.245 = bf16[8,4,128,256]{3,2,1,0:T(8,128)(2,1)} custom-call(bf16[1024,1024]{1,0:T(8,128)(2,1)} %get-tuple-element.59.da_ref, bf16[1024,1024]{1,0:T(8,128)(2,1)} %get-tuple-element.72.dq_ref, bf16[1024,1024]{1,0:T(8,128)(2,1)} %get-tuple-element.67.dk_ref, bf16[1024,1024]{1,0:T(8,128)(2,1)} %get-tuple-element.68.dv_ref, ...), custom_call_target="tpu_custom_call" | custom-call | flops 7000000000 | bytes 20000000 | tf_op jit(solution)/shard_map/pallas_call | solution.py:600
  486.6 6.0 all-to-all-start.3
  492.7 0.1 bitcast_reduce_fusion
  492.8 0.9 pad.9.small_ref
  493.6 25.4 %shard_map.246.pay_ref = bf16[8,4,592,256]{3,2,1,0:T(8,128)(2,1)} custom-call(bf16[1024,1024]{1,0:T(8,128)(2,1)} %get-tuple-element.56.x_ref, bf16[512,1024]{1,0:T(8,128)(2,1)} %copy-done.4, bf16[2048,512]{1,0:T(8,128)(2,1)} %get-tuple-element.71.hot_ref, bf16[1024,1024]{1,0:T(8,128)(2,1)} %get-tuple-element.72.dq_ref, ...), custom_call_target="tpu_custom_call" | custom-call | flops 12999999488 | bytes 40000000 | tf_op jit(solution)/shard_map/pallas_call | solution.py:672
  519.0 77.4 %shard_map.247 = (f32[128,256]{1,0:T(8,128)}, f32[128,256]{1,0:T(8,128)}, f32[128,256]{1,0:T(8,128)}, f32[128,256]{1,0:T(8,128)}, f32[512,1024]{1,0:T(8,128)}, /*index=5*/f32[16,1024]{1,0:T(8,128)}) custom-call(bf16[8,4,592,256]{3,2,1,0:T(8,128)(2,1)} %shard_map.246.pay_ref), custom_call_target="tpu_custom_call" | custom-call | bytes 200000000 | tf_op jit(solution)/shard_map/pallas_call | solution.py:936
  596.4 1.4 slice.27
  597.8 1.4 slice.31
  599.1 0.8 slice_bitcast_fusion
  600.0 0.6 copy.34
  600.6 0.0 all-to-all-done.3
  600.6 1.1 bitcast_convert_fusion
  601.7 1.1 fusion.1
  602.8 1.3 copy.42
  604.2 3.3 copy.43
  607.5 1.3 copy.44
  608.8 0.7 copy.45
  609.4 0.7 copy.46
  610.1 0.7 copy.47
  610.8 0.7 copy.48
  (47 shorter events, 0.2 us)
Async XLA Ops:
  7.2 84.5 %copy-start = (bf16[64,1024]{1,0:T(8,128)(2,1)S(1)}, bf16[64,1024]{1,0:T(8,128)(2,1)}, u32[]{:S(2)}) copy-start(bf16[64,1024]{1,0:T(8,128)(2,1)} %param.20) | copy-start | bytes 393220
  7.2 7.4 %copy-start.22 = (bf16[1024]{0:T(1024)(128)(2,1)S(1)}, bf16[1024]{0:T(1024)(128)(2,1)}, u32[]{:S(2)}) copy-start(bf16[1024]{0:T(1024)(128)(2,1)} %param.27) | copy-start | bytes 6148
  7.2 7.4 %copy-start.17 = (bf16[128,256]{1,0:T(8,128)(2,1)S(1)}, bf16[128,256]{1,0:T(8,128)(2,1)}, u32[]{:S(2)}) copy-start(bf16[128,256]{1,0:T(8,128)(2,1)} %param.22) | copy-start | bytes 196612
  7.2 7.4 %copy-start.18 = (bf16[128,256]{1,0:T(8,128)(2,1)S(1)}, bf16[128,256]{1,0:T(8,128)(2,1)}, u32[]{:S(2)}) copy-start(bf16[128,256]{1,0:T(8,128)(2,1)} %param.21) | copy-start | bytes 196612
  7.2 87.3 %all-to-all-start = ((bf16[32,128,256]{2,1,0:T(8,128)(2,1)}), bf16[32,128,256]{2,1,0:T(8,128)(2,1)S(1)}, u32[]{:S(2)}, u32[]{:S(2)}) async-start(bf16[32,128,256]{2,1,0:T(8,128)(2,1)} %param.15), calls=%async_computation | async-start | bytes 4194304 | tf_op jit(solution)/shard_map/all_to_all | solution.py:992
  14.5 241.9 %all-gather.3.cloned.1.call-start = ((), (), s32[]{:S(2)}) async-start(), calls=%async_computation.8 | async-start | bytes 19464192 | tf_op jit(solution)/shard_map/all_gather | solution.py:995
  15.3 76.5 %copy-start.15 = (bf16[128,256]{1,0:T(8,128)(2,1)S(1)}, bf16[128,256]{1,0:T(8,128)(2,1)}, u32[]{:S(2)}) copy-start(bf16[128,256]{1,0:T(8,128)(2,1)} %param.23) | copy-start | bytes 196612
  15.3 76.5 %copy-start.21 = (bf16[3,256]{1,0:T(4,128)(2,1)S(1)}, bf16[3,256]{1,0:T(4,128)(2,1)}, u32[]{:S(2)}) copy-start(bf16[3,256]{1,0:T(4,128)(2,1)} %param.24) | copy-start | bytes 4612
  15.3 78.3 %copy-start.7 = (bf16[128,1024]{1,0:T(8,128)(2,1)S(1)}, bf16[128,1024]{1,0:T(8,128)(2,1)}, u32[]{:S(2)}) copy-start(bf16[128,1024]{1,0:T(8,128)(2,1)} %param.28) | copy-start | bytes 786436
  15.3 78.3 %copy-start.8 = (bf16[128,1024]{1,0:T(8,128)(2,1)S(1)}, bf16[128,1024]{1,0:T(8,128)(2,1)}, u32[]{:S(2)}) copy-start(bf16[128,1024]{1,0:T(8,128)(2,1)} %param.26) | copy-start | bytes 786436
  15.3 78.3 %copy-start.16 = (bf16[128,256]{1,0:T(8,128)(2,1)S(1)}, bf16[128,256]{1,0:T(8,128)(2,1)}, u32[]{:S(2)}) copy-start(bf16[128,256]{1,0:T(8,128)(2,1)} %param.25) | copy-start | bytes 196612
  15.3 79.2 %copy-start.20 = (s32[2047]{0:T(1024)S(1)}, s32[2047]{0:T(1024)}, u32[]{:S(2)}) copy-start(s32[2047]{0:T(1024)} %param.19) | copy-start | bytes 24568
  91.7 3.0 copy-start.19
  91.7 4.3 copy-start.23
  91.7 4.3 copy-start.24
  94.5 33.6 %copy-start.5 = (bf16[32,128,256]{2,1,0:T(8,128)(2,1)}, bf16[32,128,256]{2,1,0:T(8,128)(2,1)S(1)}, u32[]{:S(2)}) copy-start(bf16[32,128,256]{2,1,0:T(8,128)(2,1)S(1)} %all-to-all-done) | copy-start | bytes 6291460
  128.8 114.7 %all-to-all-start.1 = ((bf16[32,128,256]{2,1,0:T(8,128)(2,1)}), bf16[32,128,256]{2,1,0:T(8,128)(2,1)}, u32[]{:S(2)}, u32[]{:S(2)}) async-start(bf16[32,128,256]{2,1,0:T(8,128)(2,1)} %param.16), calls=%async_computation.1 | async-start | bytes 4194304 | tf_op jit(solution)/shard_map/all_to_all | solution.py:992
  135.4 338.9 %reduce-scatter.3.cloned.1.call-start = ((), (), s32[]{:S(2)}) async-start(), calls=%async_computation.6 | async-start | bytes 18874368 | tf_op jit(solution)/shard_map/reduce_scatter | solution.py:1020
  165.1 1.0 copy-start.4
  242.2 1.3 copy-start.2
  349.5 124.8 %all-to-all-start.2 = ((bf16[32,128,256]{2,1,0:T(8,128)(2,1)}), bf16[32,128,256]{2,1,0:T(8,128)(2,1)S(1)}, u32[]{:S(2)}, u32[]{:S(2)}) async-start(bf16[32,128,256]{2,1,0:T(8,128)(2,1)} %bitcast.40), calls=%async_computation.2 | async-start | bytes 4194304 | tf_op jit(solution)/shard_map/all_to_all | solution.py:992
  353.0 247.6 %reduce-scatter.5.cloned.1.call-start = ((), (), s32[]{:S(2)}) async-start(), calls=%async_computation.7 | async-start | bytes 2621440 | tf_op jit(solution)/shard_map/reduce_scatter | solution.py:1024
  362.8 1.3 copy-start.3
  486.6 6.0 copy-start.10
  486.6 6.1 copy-start.9
  486.6 114.0 %all-to-all-start.3 = ((bf16[32,128,256]{2,1,0:T(8,128)(2,1)}), bf16[32,128,256]{2,1,0:T(8,128)(2,1)}, u32[]{:S(2)}, u32[]{:S(2)}) async-start(bf16[32,128,256]{2,1,0:T(8,128)(2,1)} %bitcast.11), calls=%async_computation.4 | async-start | bytes 4194304 | tf_op jit(solution)/shard_map/all_to_all | solution.py:992
  604.1 3.3 copy-start.6
  604.2 7.3 %copy-start.1 = (bf16[64,1024]{1,0:T(8,128)(2,1)S(1)}, bf16[64,1024]{1,0:T(8,128)(2,1)}, u32[]{:S(2)}) copy-start(bf16[64,1024]{1,0:T(8,128)(2,1)} %param.20) | copy-start | bytes 393220
  607.4 1.3 copy-start.14
  607.4 2.0 copy-start.13
  607.4 2.7 copy-start.12
  607.4 3.3 copy-start.11
Sparse Core Ops, SparseCore 0:
  94.7 161.7 all-gather.2
  349.6 118.4 reduce-scatter.2
  474.4 66.2 reduce-scatter.4

commit v7 on v6

--- a/solution.py
+++ b/solution.py
@@ -907,15 +907,13 @@
             base += 2 * (gn // 4 >> step)
         return stages + [(last, last_done)]
 
-    cut = keep // 32 * 16
+    cuts = [0, keep // 48 * 16, keep // 24 * 16, keep]
     chunks = [
         reduce_stages(0, keep, rows)
         + spread_stages(
-            lambda: rest_ref, lambda i, s: all_ref.at[i, s], local.at[3, 0], wire, tn, gn
+            lambda: rest_ref, lambda i, s: all_ref.at[i, s], local.at[4, 0], wire, tn, gn
         ),
-        reduce_stages(1, 0, cut),
-        reduce_stages(2, cut, keep),
-    ]
+    ] + [reduce_stages(n + 1, cuts[n], cuts[n + 1]) for n in range(3)]
     run_waves(chunks)
     dt = q_ref.shape[1]
     rg = rel_ref.shape[0] // gn
@@ -931,7 +929,7 @@
     bf, f32 = jnp.bfloat16, jnp.float32
     m = gn // 2
     pieces = 2 * (m - 1)
-    count = 3 * (m + pieces + tn - 1) + spread_count(tn, gn)
+    count = 4 * (m + pieces + tn - 1) + spread_count(tn, gn)
     dma = lambda *k: pltpu.SemaphoreType.DMA(k)
     return pl.pallas_call(
         functools.partial(reduce_kernel, tn=tn, gn=gn, keep=keep),
@@ -949,7 +947,7 @@
             pltpu.VMEM((pieces, tn // 2, rows, dt), bf),
             pltpu.VMEM((tn - 1, rows, dt), bf),
             pltpu.VMEM((1, rows - keep, dt), bf),
-            dma(4, m), dma(count), dma(count),
+            dma(5, m), dma(count), dma(count),
         ],
         compiler_params=pltpu.CompilerParams(collective_id=number, has_side_effects=True, vmem_limit_bytes=58 << 20),
         cost_estimate=pl.CostEstimate(flops=0, bytes_accessed=200 * 10**6, transcendentals=0),

time: 620 us -> 620 us (level)
  no operation moved by 1% of the time
where the time goes in v7:
time: 620 us; the launch traced here: 618 us
  Pallas kernels  541 us (87%)
  starting transfers between devices  23.5 us (4%)
  local copies, waits for them, and re-layouts  21.5 us (3%)
  between operations  14.3 us (2%)
  waiting for transfers between devices  13 us (2%)
    pallas_call x1, Pallas kernels, attn_bwd(): pl.pallas_call(functools.partial(bwd_kernel, L=L, scale=scale), grid=(C /...  110 us
    pallas_call x2, Pallas kernels, gather_all(): pl.pallas_call(functools.partial(gather_kernel, tn=tn, gn=gn, cuts=cuts),...  108 us
    pallas_call x1, Pallas kernels, middle(): pl.pallas_call(middle_kernel, grid=(2 * tn,), in_specs=[pl.BlockSpec(memo...  93 us
    pallas_call x1, Pallas kernels, reduce_all(): pl.pallas_call(functools.partial(reduce_kernel, tn=tn, gn=gn, keep=keep),...  77.7 us
    pallas_call x1, Pallas kernels, attn_fwd(): pl.pallas_call(functools.partial(fwd_kernel, L=L, scale=scale), grid_spec...  76.1 us
    pallas_call x1, Pallas kernels, project(): pl.pallas_call(project_kernel, grid=(tn, 3), in_specs=[spec((gn, tn, lg,...  29.1 us
    pallas_call x1, Pallas kernels, tail(): pl.pallas_call(functools.partial(tail_kernel, first_shift=first_shift), g...  25.4 us
    all_to_all x4, starting transfers between devices, swap(): return lax.all_to_all(a, seq_axes, split_axis=0, concat_axis=0, tiled=True)  23.4 us
  transfers between devices with their start and end apart: 7, of which 1 were waited for; matrix products, arithmetic and copies ran while one was open for 2% of the time, Pallas kernels for 72%

profile of v7, /device:TPU:0, one launch (start us, length us, event | category | flops | bytes accessed | tf_op | source)
XLA Modules:
  0.0 618.5 jit_solution(13680838564708516824)
XLA Ops:
  7.2 0.0 copy-start
  7.2 7.3 %all-to-all-start = ((bf16[32,128,256]{2,1,0:T(8,128)(2,1)}), bf16[32,128,256]{2,1,0:T(8,128)(2,1)S(1)}, u32[]{:S(2)}, u32[]{:S(2)}) async-start(bf16[32,128,256]{2,1,0:T(8,128)(2,1)} %param.15), calls=%async_computation | async-start | bytes 4194304 | tf_op jit(solution)/shard_map/all_to_all | solution.py:990
  14.5 0.0 all-gather.3.cloned.1.call-start
  14.6 0.0 copy-done.22
  14.6 0.0 copy-done.17
  14.6 0.0 copy-done.18
  14.6 0.7 maximum_bitcast_fusion.src_ref
  15.3 0.0 copy-start.16
  15.3 0.0 copy-start.20
  15.3 76.3 %shard_map.238.wa_ref.w_ref = bf16[8,4,256,256]{3,2,1,0:T(8,128)(2,1)} custom-call(bf16[1,256,256]{2,1,0:T(8,128)(2,1)} %maximum_bitcast_fusion.src_ref), custom_call_target="tpu_custom_call" | custom-call | bytes 33554432 | tf_op jit(solution)/shard_map/pallas_call | solution.py:807
  91.7 0.0 copy-start.19
  91.7 0.0 copy-start.23
  91.7 0.0 copy-start.24
  91.8 1.9 concatenate.16
  93.6 0.9 pad_maximum_fusion
  94.5 0.0 all-to-all-done
  94.5 0.0 all-gather.3.cloned.1.call-update
  94.6 0.1 reverse
  94.6 0.1 slice.38
  94.7 0.8 convert_element_type.21.vec_ref
  95.5 0.1 pad_add_fusion
  95.6 0.4 copy.27.pl_ref
  96.0 0.6 fusion
  96.6 31.4 %shard_map.239.rel4_ref.wb_ref = bf16[8,4,200,256]{3,2,1,0:T(8,128)(2,1)} custom-call(bf16[1,200,256]{2,1,0:T(8,128)(2,1)} %bitcast.41), custom_call_target="tpu_custom_call" | custom-call | bytes 26214400 | tf_op jit(solution)/shard_map/pallas_call | solution.py:807
  128.1 0.7 bitcast_convert_fusion.1
  128.8 6.5 %all-to-all-start.1 = ((bf16[32,128,256]{2,1,0:T(8,128)(2,1)}), bf16[32,128,256]{2,1,0:T(8,128)(2,1)}, u32[]{:S(2)}, u32[]{:S(2)}) async-start(bf16[32,128,256]{2,1,0:T(8,128)(2,1)} %param.16), calls=%async_computation.1 | async-start | bytes 4194304 | tf_op jit(solution)/shard_map/all_to_all | solution.py:990
  135.4 0.0 reduce-scatter.3.cloned.1.call-start
  135.4 0.6 reshape.65.hb_ref
  136.1 29.1 %shard_map.240 = (bf16[3,1024,1024]{2,1,0:T(8,128)(2,1)}, bf16[2,2048,1024]{2,1,0:T(8,128)(2,1)}, bf16[1024,1024]{1,0:T(8,128)(2,1)}, bf16[512,1024]{1,0:T(8,128)(2,1)S(1)}, bf16[2048,512]{1,0:T(8,128)(2,1)}) custom-call(bf16[8,4,128,256]{3,2,1,0:T(8,128)(2,1)} %bitcast.39, bf16[8,4,200,256]{3,2,1,0:T(8,128)(2,1)} %shard_map.239.rel4_ref.wb_ref, ...), custom_call_target="tpu_custom_call" | custom-call | flops 14000000000 | bytes 30000000 | tf_op jit(solution)/shard_map/pallas_call | solution.py:338
  165.1 1.0 copy-done.4
  166.1 76.1 %shard_map.241 = (bf16[1024,1024]{1,0:T(8,128)(2,1)S(1)}, bf16[16,1024,1024]{2,1,0:T(8,128)(2,1)}, f32[1024,1024]{1,0:T(8,128)}) custom-call(s32[1]{0:T(128)} %bitcast.len_ref, bf16[3,1024,1024]{2,1,0:T(8,128)(2,1)} %get-tuple-element.52.q_ref.k_ref.v_ref, bf16[3,1024,1024]{2,1,0:T(8,128)(2,1)} %get-tuple-element.52.q_ref.k_ref.v_ref, ...), custom_call_target="tpu_custom_call" | custom-call | flops 80000000000 | bytes 60000000 | tf_op jit(solution)/shard_map/pallas_call | solution.py:108
  242.2 1.3 copy-done.2
  243.5 0.0 all-to-all-done.1
  243.5 12.9 %all-gather.3.cloned.1.call-done = bf16[4096,2304]{1,0:T(8,128)(2,1)} async-done(((bf16[128,2304]{1,0:T(8,128)(2,1)}), bf16[4096,2304]{1,0:T(8,128)(2,1)}) %all-gather.3.cloned.1.call-update) | async-done | bytes 18874384 | tf_op jit(solution)/shard_map/all_gather | solution.py:993
  256.4 93.0 %shard_map.242 = (bf16[8,4,128,256]{3,2,1,0:T(8,128)(2,1)}, bf16[8,4,128,2048]{3,2,1,0:T(8,128)(2,1)}, f32[4,8,1024]{2,1,0:T(8,128)}, bf16[1024,1024]{1,0:T(8,128)(2,1)}, f32[48,1024]{1,0:T(8,128)}) custom-call(bf16[1024,1024]{1,0:T(8,128)(2,1)} %copy-done.2, bf16[1024,1024]{1,0:T(8,128)(2,1)} %get-tuple-element.56.x_ref, ...), custom_call_target="tpu_custom_call" | custom-call | flops 74999996416 | bytes 100000000 | tf_op jit(solution)/shard_map/pallas_call | solution.py:492
  349.5 0.0 reduce-scatter.3.cloned.1.call-update
  349.5 3.5 all-to-all-start.2
  353.0 0.0 reduce-scatter.5.cloned.1.call-start
  353.1 9.7 %shard_map.243 = (bf16[8,4,128,256]{3,2,1,0:T(8,128)(2,1)S(1)}, bf16[1024,1024]{1,0:T(8,128)(2,1)}) custom-call(bf16[1024,1024]{1,0:T(8,128)(2,1)} %get-tuple-element.59.da_ref, bf16[1024,1024]{1,0:T(8,128)(2,1)} %copy-done.2, bf16[4,8,128,2304]{3,2,1,0:T(8,128)(2,1)} %bitcast.37), custom_call_target="tpu_custom_call" | custom-call | flops 4000000000 | bytes 10000000 | tf_op jit(solution)/shard_map/pallas_call | solution.py:550
  362.8 1.3 copy-done.3
  364.1 110.1 %shard_map.244 = (bf16[1024,1024]{1,0:T(8,128)(2,1)}, bf16[1024,1024]{1,0:T(8,128)(2,1)}, bf16[1024,1024]{1,0:T(8,128)(2,1)}, bf16[1024,2048]{1,0:T(8,128)(2,1)}...) custom-call(bf16[16,1024,1024]{2,1,0:T(8,128)(2,1)} %get-tuple-element.54.p_ref, ...), custom_call_target="tpu_custom_call" | custom-call | flops 120000004096 | bytes 80000000 | tf_op jit(solution)/shard_map/pallas_call | solution.py:265
  474.3 0.0 all-to-all-done.2
  474.3 0.0 reduce-scatter.3.cloned.1.call-done
  474.3 0.0 reduce-scatter.5.cloned.1.call-update
  474.3 12.2 %shard_map.245 = bf16[8,4,128,256]{3,2,1,0:T(8,128)(2,1)} custom-call(bf16[1024,1024]{1,0:T(8,128)(2,1)} %get-tuple-element.59.da_ref, bf16[1024,1024]{1,0:T(8,128)(2,1)} %get-tuple-element.72.dq_ref, bf16[1024,1024]{1,0:T(8,128)(2,1)} %get-tuple-element.67.dk_ref, bf16[1024,1024]{1,0:T(8,128)(2,1)} %get-tuple-element.68.dv_ref, ...), custom_call_target="tpu_custom_call" | custom-call | flops 7000000000 | bytes 20000000 | tf_op jit(solution)/shard_map/pallas_call | solution.py:600
  486.6 6.0 all-to-all-start.3
  492.7 0.1 bitcast_reduce_fusion
  492.8 0.9 pad.9.small_ref
  493.6 25.4 %shard_map.246.pay_ref = bf16[8,4,592,256]{3,2,1,0:T(8,128)(2,1)} custom-call(bf16[1024,1024]{1,0:T(8,128)(2,1)} %get-tuple-element.56.x_ref, bf16[512,1024]{1,0:T(8,128)(2,1)} %copy-done.4, bf16[2048,512]{1,0:T(8,128)(2,1)} %get-tuple-element.71.hot_ref, bf16[1024,1024]{1,0:T(8,128)(2,1)} %get-tuple-element.72.dq_ref, ...), custom_call_target="tpu_custom_call" | custom-call | flops 12999999488 | bytes 40000000 | tf_op jit(solution)/shard_map/pallas_call | solution.py:672
  519.0 77.7 %shard_map.247 = (f32[128,256]{1,0:T(8,128)}, f32[128,256]{1,0:T(8,128)}, f32[128,256]{1,0:T(8,128)}, f32[128,256]{1,0:T(8,128)}, f32[512,1024]{1,0:T(8,128)}, /*index=5*/f32[16,1024]{1,0:T(8,128)}) custom-call(bf16[8,4,592,256]{3,2,1,0:T(8,128)(2,1)} %shard_map.246.pay_ref), custom_call_target="tpu_custom_call" | custom-call | bytes 200000000 | tf_op jit(solution)/shard_map/pallas_call | solution.py:934
  596.7 1.4 slice.27
  598.1 1.4 slice.31
  599.5 0.8 slice_bitcast_fusion
  600.3 0.6 copy.34
  600.9 0.0 all-to-all-done.3
  600.9 1.1 bitcast_convert_fusion
  602.1 1.1 fusion.1
  603.2 1.3 copy.42
  604.5 3.3 copy.43
  607.8 1.3 copy.44
  609.1 0.7 copy.45
  609.8 0.7 copy.46
  610.4 0.7 copy.47
  611.1 0.7 copy.48
  (47 shorter events, 0.2 us)
Async XLA Ops:
  7.2 84.5 %copy-start = (bf16[64,1024]{1,0:T(8,128)(2,1)S(1)}, bf16[64,1024]{1,0:T(8,128)(2,1)}, u32[]{:S(2)}) copy-start(bf16[64,1024]{1,0:T(8,128)(2,1)} %param.20) | copy-start | bytes 393220
  7.2 7.4 %copy-start.22 = (bf16[1024]{0:T(1024)(128)(2,1)S(1)}, bf16[1024]{0:T(1024)(128)(2,1)}, u32[]{:S(2)}) copy-start(bf16[1024]{0:T(1024)(128)(2,1)} %param.27) | copy-start | bytes 6148
  7.2 7.4 %copy-start.17 = (bf16[128,256]{1,0:T(8,128)(2,1)S(1)}, bf16[128,256]{1,0:T(8,128)(2,1)}, u32[]{:S(2)}) copy-start(bf16[128,256]{1,0:T(8,128)(2,1)} %param.22) | copy-start | bytes 196612
  7.2 7.4 %copy-start.18 = (bf16[128,256]{1,0:T(8,128)(2,1)S(1)}, bf16[128,256]{1,0:T(8,128)(2,1)}, u32[]{:S(2)}) copy-start(bf16[128,256]{1,0:T(8,128)(2,1)} %param.21) | copy-start | bytes 196612
  7.2 87.3 %all-to-all-start = ((bf16[32,128,256]{2,1,0:T(8,128)(2,1)}), bf16[32,128,256]{2,1,0:T(8,128)(2,1)S(1)}, u32[]{:S(2)}, u32[]{:S(2)}) async-start(bf16[32,128,256]{2,1,0:T(8,128)(2,1)} %param.15), calls=%async_computation | async-start | bytes 4194304 | tf_op jit(solution)/shard_map/all_to_all | solution.py:990
  14.5 241.9 %all-gather.3.cloned.1.call-start = ((), (), s32[]{:S(2)}) async-start(), calls=%async_computation.8 | async-start | bytes 19464192 | tf_op jit(solution)/shard_map/all_gather | solution.py:993
  15.3 76.5 %copy-start.15 = (bf16[128,256]{1,0:T(8,128)(2,1)S(1)}, bf16[128,256]{1,0:T(8,128)(2,1)}, u32[]{:S(2)}) copy-start(bf16[128,256]{1,0:T(8,128)(2,1)} %param.23) | copy-start | bytes 196612
  15.3 76.5 %copy-start.21 = (bf16[3,256]{1,0:T(4,128)(2,1)S(1)}, bf16[3,256]{1,0:T(4,128)(2,1)}, u32[]{:S(2)}) copy-start(bf16[3,256]{1,0:T(4,128)(2,1)} %param.24) | copy-start | bytes 4612
  15.3 78.3 %copy-start.7 = (bf16[128,1024]{1,0:T(8,128)(2,1)S(1)}, bf16[128,1024]{1,0:T(8,128)(2,1)}, u32[]{:S(2)}) copy-start(bf16[128,1024]{1,0:T(8,128)(2,1)} %param.28) | copy-start | bytes 786436
  15.3 78.3 %copy-start.8 = (bf16[128,1024]{1,0:T(8,128)(2,1)S(1)}, bf16[128,1024]{1,0:T(8,128)(2,1)}, u32[]{:S(2)}) copy-start(bf16[128,1024]{1,0:T(8,128)(2,1)} %param.26) | copy-start | bytes 786436
  15.3 78.3 %copy-start.16 = (bf16[128,256]{1,0:T(8,128)(2,1)S(1)}, bf16[128,256]{1,0:T(8,128)(2,1)}, u32[]{:S(2)}) copy-start(bf16[128,256]{1,0:T(8,128)(2,1)} %param.25) | copy-start | bytes 196612
  15.3 79.2 %copy-start.20 = (s32[2047]{0:T(1024)S(1)}, s32[2047]{0:T(1024)}, u32[]{:S(2)}) copy-start(s32[2047]{0:T(1024)} %param.19) | copy-start | bytes 24568
  91.7 3.0 copy-start.19
  91.7 4.3 copy-start.23
  91.7 4.3 copy-start.24
  94.5 33.6 %copy-start.5 = (bf16[32,128,256]{2,1,0:T(8,128)(2,1)}, bf16[32,128,256]{2,1,0:T(8,128)(2,1)S(1)}, u32[]{:S(2)}) copy-start(bf16[32,128,256]{2,1,0:T(8,128)(2,1)S(1)} %all-to-all-done) | copy-start | bytes 6291460
  128.8 114.7 %all-to-all-start.1 = ((bf16[32,128,256]{2,1,0:T(8,128)(2,1)}), bf16[32,128,256]{2,1,0:T(8,128)(2,1)}, u32[]{:S(2)}, u32[]{:S(2)}) async-start(bf16[32,128,256]{2,1,0:T(8,128)(2,1)} %param.16), calls=%async_computation.1 | async-start | bytes 4194304 | tf_op jit(solution)/shard_map/all_to_all | solution.py:990
  135.4 338.9 %reduce-scatter.3.cloned.1.call-start = ((), (), s32[]{:S(2)}) async-start(), calls=%async_computation.6 | async-start | bytes 18874368 | tf_op jit(solution)/shard_map/reduce_scatter | solution.py:1018
  165.1 1.0 copy-start.4
  242.2 1.3 copy-start.2
  349.5 124.8 %all-to-all-start.2 = ((bf16[32,128,256]{2,1,0:T(8,128)(2,1)}), bf16[32,128,256]{2,1,0:T(8,128)(2,1)S(1)}, u32[]{:S(2)}, u32[]{:S(2)}) async-start(bf16[32,128,256]{2,1,0:T(8,128)(2,1)} %bitcast.40), calls=%async_computation.2 | async-start | bytes 4194304 | tf_op jit(solution)/shard_map/all_to_all | solution.py:990
  353.0 247.9 %reduce-scatter.5.cloned.1.call-start = ((), (), s32[]{:S(2)}) async-start(), calls=%async_computation.7 | async-start | bytes 2621440 | tf_op jit(solution)/shard_map/reduce_scatter | solution.py:1022
  362.8 1.3 copy-start.3
  486.6 6.0 copy-start.10
  486.6 6.1 copy-start.9
  486.6 114.4 %all-to-all-start.3 = ((bf16[32,128,256]{2,1,0:T(8,128)(2,1)}), bf16[32,128,256]{2,1,0:T(8,128)(2,1)}, u32[]{:S(2)}, u32[]{:S(2)}) async-start(bf16[32,128,256]{2,1,0:T(8,128)(2,1)} %bitcast.11), calls=%async_computation.4 | async-start | bytes 4194304 | tf_op jit(solution)/shard_map/all_to_all | solution.py:990
  604.5 3.3 copy-start.6
  604.5 7.3 %copy-start.1 = (bf16[64,1024]{1,0:T(8,128)(2,1)S(1)}, bf16[64,1024]{1,0:T(8,128)(2,1)}, u32[]{:S(2)}) copy-start(bf16[64,1024]{1,0:T(8,128)(2,1)} %param.20) | copy-start | bytes 393220
  607.8 1.3 copy-start.14
  607.8 2.0 copy-start.13
  607.8 2.7 copy-start.12
  607.8 3.3 copy-start.11
Sparse Core Ops, SparseCore 0:
  94.7 161.7 all-gather.2
  349.6 118.4 reduce-scatter.2
  474.4 66.2 reduce-scatter.4
